TPU v7x, 32 devices: a whole 2x2x4 slice. The times are simulated.
32 devices in a mesh: dp: 16 (over z, y, x), mp: 2 (over core).
Axes of the slice: x: 2, y: 2, z: 4, core: 2. Of those that a mesh axis runs over, the one named last changes fastest.
Arguments:
- inputs: bfloat16 [16, 1024, 768], P('dp', 'mp'), may hold values from -6 to 6
- grad_out: bfloat16 [16, 1024, 768], P('dp', 'mp'), may hold values from -6 to 6
- lengths: int32 [16], P('dp'), may hold values from 512 to 1024, as said below
- rand_blocks: int32 [16, 16, 3], P('dp', 'mp'), may hold values from 0 to 15, as said below
- w_query: bfloat16 [768, 768], replicated, may hold values from -0.3125 to 0.3125
- b_query: bfloat16 [768], replicated, may hold values from -1.5 to 1.5
- w_key: bfloat16 [768, 768], replicated, may hold values from -0.3125 to 0.3125
- w_value: bfloat16 [768, 768], replicated, may hold values from -0.21875 to 0.21875
- b_value: bfloat16 [768], replicated, may hold values from -0.5 to 0.5
- w_output: bfloat16 [768, 768], replicated, may hold values from -1.75 to 1.75
- b_output: bfloat16 [768], replicated, may hold values from -1.5 to 1.5
- gain_one: bfloat16 [768], replicated, may hold values from 0.099609375 to 1.8984375
- shift_one: bfloat16 [768], replicated, may hold values from -1.5 to 1.5
- w_in: bfloat16 [768, 3072], P(None, 'mp'), may hold values from -0.21875 to 0.21875
- b_in: bfloat16 [3072], P('mp'), may hold values from -1.5 to 1.5
- w_out: bfloat16 [768, 3072], P(None, 'mp'), may hold values from -0.109375 to 0.109375
- b_out: bfloat16 [768], replicated, may hold values from -1.5 to 1.5
- gain_two: bfloat16 [768], replicated, may hold values from 0.099609375 to 1.8984375
- shift_two: bfloat16 [768], replicated, may hold values from -1.5 to 1.5
Outputs:
- output: bfloat16 [16, 1024, 768], P('dp', 'mp')
- input_grad: float32 [16, 1024, 768], P('dp', 'mp')
- w_query_grad: float32 [768, 768], P('dp', 'mp')
- b_query_grad: float32 [768], P('dp')
- w_key_grad: float32 [768, 768], P('dp', 'mp')
- w_value_grad: float32 [768, 768], P('dp', 'mp')
- b_value_grad: float32 [768], P('dp')
- w_output_grad: float32 [768, 768], P('dp', 'mp')
- b_output_grad: float32 [768], P('dp')
- gain_one_grad: float32 [768], P('dp')
- shift_one_grad: float32 [768], P('dp')
- w_in_grad: float32 [768, 3072], P('dp', 'mp')
- b_in_grad: float32 [3072], P('dp')
- w_out_grad: float32 [768, 3072], P('dp', 'mp')
- b_out_grad: float32 [768], P('dp')
- gain_two_grad: float32 [768], P('dp')
- shift_two_grad: float32 [768], P('dp')
Inputs may be any that keep to these rules, and one draw needn't show every extreme that they name: Positions below lengths[s] of sequence s are real tokens, the rest padding; some sequence has 1024 real tokens and some has 512. rand_blocks[s, i, j] lies below ceil(lengths[s] / 64).
All inputs are finite; a program needn't handle non-finite values.
Results may differ from a plain program's by a relative error of at most 0.02.
Values may be sent and summed in bfloat16 or wider, within the bound.
A program may use at most 256 MiB of HBM per device.

v0:
```python
import jax
import jax.numpy as jnp
from jax import lax
from jax.sharding import PartitionSpec as P

HEADS = 12
HD = 64
FF = 3072
BLK = 64
NB = 16


negative_fill = -1000000000.0
norm_epsilon = 1e-12


def layer_norm(features, norm_gain, norm_shift):
    row_mean = jnp.mean(features, axis=-1, keepdims=True)
    centered = features - row_mean
    variance = jnp.mean(centered * centered, axis=-1, keepdims=True)
    return centered * lax.rsqrt(variance + norm_epsilon) * norm_gain + norm_shift


def gelu_tanh(features):
    return jax.nn.gelu(features, approximate=True)


def slot_table_ids(block_ids, rand_rows, length):
    valid_blocks = (length + BLK - 1) // BLK
    column = block_ids[:, None]
    columns = jnp.concatenate(
        [
            column - 1,
            column,
            column + 1,
            rand_rows,
            jnp.zeros_like(column),
            jnp.zeros_like(column) + valid_blocks - 1,
        ],
        axis=1,
    )
    in_range = (columns >= 0) & (columns < valid_blocks)
    slot_ids = jnp.arange(columns.shape[1], dtype=jnp.int32)
    earlier = slot_ids[None, :] < slot_ids[:, None]
    repeated = jnp.any(
        (columns[:, :, None] == columns[:, None, :]) & earlier[None, :, :] & in_range[:, None, :],
        axis=2,
    )
    return (jnp.clip(columns, 0, NB - 1), in_range & jnp.logical_not(repeated))


def slot_table(first_block, rand_rows, length):
    block_ids = first_block + jnp.arange(rand_rows.shape[0], dtype=jnp.int32)
    return slot_table_ids(block_ids, rand_rows, length)


def slot_mask(slot_blocks, slot_valid, length):
    positions = slot_blocks[:, :, None] * BLK + jnp.arange(BLK, dtype=jnp.int32)
    allowed = slot_valid[:, :, None] & (positions < length)
    return allowed.reshape(slot_blocks.shape[0], 1, 1, -1)


def gather_slots(whole_rows, slot_blocks):
    picked = whole_rows.reshape(NB, BLK, whole_rows.shape[1])[slot_blocks]
    return picked.reshape(slot_blocks.shape[0], slot_blocks.shape[1] * BLK, HEADS, HD)


def log_total(scores, allowed):
    masked = jnp.where(allowed, scores, negative_fill)
    top_score = jnp.max(masked, axis=-1, keepdims=True)
    return top_score + jnp.log(jnp.sum(jnp.exp(masked - top_score), axis=-1, keepdims=True))


def exp_probs(scores, allowed, totals):
    return jnp.exp(jnp.where(allowed, scores, negative_fill) - totals)


def global_targets(length, device, local_blocks):
    last_block = (length + BLK - 1) // BLK - 1
    targets = []
    for target_block in (jnp.zeros_like(last_block), last_block):
        is_owner = target_block // local_blocks == device
        local_block = jnp.clip(target_block - device * local_blocks, 0, local_blocks - 1)
        targets.append((is_owner, local_block))
    return targets


def global_scores(query_rows, key_one, length):
    scores = jnp.einsum(
        "qhd,khd->hqk",
        query_rows.reshape(BLK, HEADS, HD),
        key_one.reshape(-1, HEADS, HD),
        preferred_element_type=jnp.float32,
    ) * HD ** (-0.5)
    allowed = (jnp.arange(key_one.shape[0], dtype=jnp.int32) < length)[None, None, :]
    return (scores, allowed)


def global_forward(query_rows, key_one, value_one, length):
    scores, allowed = global_scores(query_rows, key_one, length)
    totals = log_total(scores, allowed)
    weighting = exp_probs(scores, allowed, totals).astype(jnp.bfloat16)
    out_rows = jnp.einsum(
        "hqk,khd->qhd",
        weighting,
        value_one.reshape(-1, HEADS, HD),
        preferred_element_type=jnp.float32,
    )
    return (out_rows.reshape(BLK, -1), totals)


def global_skip(query_rows, key_one, value_one, length):
    return (jnp.zeros((BLK, HEADS * HD), jnp.float32), jnp.zeros((HEADS, BLK, 1), jnp.float32))


def global_backward(query_rows, grad_rows, key_one, value_one, length, row_totals):
    score_scale = HD ** (-0.5)
    scores, allowed = global_scores(query_rows, key_one, length)
    exact_probs = exp_probs(scores, allowed, row_totals)
    grad_heads = grad_rows.reshape(BLK, HEADS, HD)
    grad_weights = jnp.einsum(
        "qhd,khd->hqk",
        grad_heads,
        value_one.reshape(-1, HEADS, HD),
        preferred_element_type=jnp.float32,
    )
    delta_sum = jnp.sum(exact_probs * grad_weights, axis=-1, keepdims=True)
    grad_scores = (exact_probs * (grad_weights - delta_sum)).astype(jnp.bfloat16)
    grad_query = (
        jnp.einsum(
            "hqk,khd->qhd",
            grad_scores,
            key_one.reshape(-1, HEADS, HD),
            preferred_element_type=jnp.float32,
        )
        * score_scale
    )
    grad_keys = (
        jnp.einsum(
            "hqk,qhd->khd",
            grad_scores,
            query_rows.reshape(BLK, HEADS, HD),
            preferred_element_type=jnp.float32,
        )
        * score_scale
    )
    grad_values = jnp.einsum(
        "hqk,qhd->khd",
        exact_probs.astype(jnp.bfloat16),
        grad_heads,
        preferred_element_type=jnp.float32,
    )
    return (
        grad_query.reshape(BLK, -1),
        grad_keys.reshape(key_one.shape[0], -1),
        grad_values.reshape(key_one.shape[0], -1),
    )


def global_back_skip(query_rows, grad_rows, key_one, value_one, length, row_totals):
    key_zeros = jnp.zeros(key_one.shape, jnp.float32)
    return (jnp.zeros((BLK, key_one.shape[1]), jnp.float32), key_zeros, key_zeros)


def attend_forward(query_one, key_one, value_one, length, rand_rows, device):
    local_blocks = rand_rows.shape[0]
    slot_blocks, slot_valid = slot_table(device * local_blocks, rand_rows, length)
    allowed = slot_mask(slot_blocks, slot_valid, length)
    query_blocks = query_one.reshape(local_blocks, BLK, HEADS, HD)
    scores = jnp.einsum(
        "nqhd,nkhd->nhqk",
        query_blocks,
        gather_slots(key_one, slot_blocks),
        preferred_element_type=jnp.float32,
    ) * HD ** (-0.5)
    totals = log_total(scores, allowed)
    weighting = exp_probs(scores, allowed, totals).astype(jnp.bfloat16)
    attended = jnp.einsum(
        "nhqk,nkhd->nqhd",
        weighting,
        gather_slots(value_one, slot_blocks),
        preferred_element_type=jnp.float32,
    ).reshape(query_one.shape[0], -1)
    global_totals = []
    for is_owner, local_block in global_targets(length, device, local_blocks):
        query_rows = lax.dynamic_slice_in_dim(query_one, local_block * BLK, BLK, 0)
        out_rows, row_totals = lax.cond(
            is_owner, global_forward, global_skip, query_rows, key_one, value_one, length
        )
        updated = lax.dynamic_update_slice_in_dim(attended, out_rows, local_block * BLK, 0)
        attended = jnp.where(is_owner, updated, attended)
        global_totals.append(row_totals)
    return (attended, totals, global_totals[0], global_totals[1])


def attend_backward(
    query_one,
    key_one,
    value_one,
    length,
    rand_rows,
    totals,
    first_totals,
    last_totals,
    grad_one,
    device,
):
    score_scale = HD ** (-0.5)
    local_blocks = rand_rows.shape[0]
    first_block = device * local_blocks
    slot_blocks, slot_valid = slot_table(first_block, rand_rows, length)
    allowed = slot_mask(slot_blocks, slot_valid, length)
    query_blocks = query_one.reshape(local_blocks, BLK, HEADS, HD)
    key_slots = gather_slots(key_one, slot_blocks)
    value_slots = gather_slots(value_one, slot_blocks)
    scores = (
        jnp.einsum("nqhd,nkhd->nhqk", query_blocks, key_slots, preferred_element_type=jnp.float32)
        * score_scale
    )
    exact_probs = exp_probs(scores, allowed, totals)
    last_block = (length + BLK - 1) // BLK - 1
    row_blocks = first_block + jnp.arange(query_one.shape[0], dtype=jnp.int32) // BLK
    is_global = (row_blocks == 0) | (row_blocks == last_block)
    grad_sparse = jnp.where(is_global[:, None], jnp.zeros_like(grad_one), grad_one)
    grad_heads = grad_sparse.reshape(local_blocks, BLK, HEADS, HD)
    grad_weights = jnp.einsum(
        "nqhd,nkhd->nhqk", grad_heads, value_slots, preferred_element_type=jnp.float32
    )
    delta_sum = jnp.sum(exact_probs * grad_weights, axis=-1, keepdims=True)
    grad_scores = (exact_probs * (grad_weights - delta_sum)).astype(jnp.bfloat16)
    grad_query = (
        jnp.einsum(
            "nhqk,nkhd->nqhd", grad_scores, key_slots, preferred_element_type=jnp.float32
        ).reshape(query_one.shape[0], -1)
        * score_scale
    )
    grad_key_slots = (
        jnp.einsum("nhqk,nqhd->nkhd", grad_scores, query_blocks, preferred_element_type=jnp.float32)
        * score_scale
    )
    grad_value_slots = jnp.einsum(
        "nhqk,nqhd->nkhd",
        exact_probs.astype(jnp.bfloat16),
        grad_heads,
        preferred_element_type=jnp.float32,
    )
    flat_ids = slot_blocks.reshape(-1)
    slot_width = BLK * query_one.shape[1]
    grad_keys = jax.ops.segment_sum(
        grad_key_slots.reshape(-1, slot_width), flat_ids, num_segments=NB
    ).reshape(-1, query_one.shape[1])
    grad_values = jax.ops.segment_sum(
        grad_value_slots.reshape(-1, slot_width), flat_ids, num_segments=NB
    ).reshape(-1, query_one.shape[1])
    for (is_owner, local_block), row_totals in zip(
        global_targets(length, device, local_blocks), (first_totals, last_totals)
    ):
        query_rows = lax.dynamic_slice_in_dim(query_one, local_block * BLK, BLK, 0)
        grad_rows = lax.dynamic_slice_in_dim(grad_one, local_block * BLK, BLK, 0)
        query_add, key_add, value_add = lax.cond(
            is_owner,
            global_backward,
            global_back_skip,
            query_rows,
            grad_rows,
            key_one,
            value_one,
            length,
            row_totals,
        )
        current = lax.dynamic_slice_in_dim(grad_query, local_block * BLK, BLK, 0)
        grad_query = lax.dynamic_update_slice_in_dim(
            grad_query, current + query_add, local_block * BLK, 0
        )
        grad_keys = grad_keys + key_add
        grad_values = grad_values + value_add
    return (grad_query, grad_keys, grad_values)


def local(
    inputs,
    grad_out,
    lengths,
    rand_blocks,
    w_query,
    b_query,
    w_key,
    w_value,
    b_value,
    w_output,
    b_output,
    gain_one,
    shift_one,
    w_in,
    b_in,
    w_out,
    b_out,
    gain_two,
    shift_two,
):
    device = lax.axis_index("mp")
    seq_count, local_rows, width = inputs.shape
    flat_in = inputs.reshape(-1, width)
    query = (jnp.dot(flat_in, w_query, preferred_element_type=jnp.float32) + b_query).astype(
        jnp.bfloat16
    )
    keys = jnp.dot(flat_in, w_key, preferred_element_type=jnp.float32).astype(jnp.bfloat16)
    values = (jnp.dot(flat_in, w_value, preferred_element_type=jnp.float32) + b_value).astype(
        jnp.bfloat16
    )
    key_all, value_all = (
        lax.all_gather(keys.reshape(seq_count, local_rows, width), "mp", axis=1, tiled=True),
        lax.all_gather(values.reshape(seq_count, local_rows, width), "mp", axis=1, tiled=True),
    )
    query_seq = query.reshape(seq_count, local_rows, width)

    def forward_item(seq_items):
        query_one, key_one, value_one, length, rand_rows = seq_items
        return attend_forward(query_one, key_one, value_one, length, rand_rows, device)

    attended, totals, first_totals, last_totals = lax.map(
        forward_item, (query_seq, key_all, value_all, lengths, rand_blocks)
    )
    attended_low = attended.reshape(-1, width).astype(jnp.bfloat16)
    summed_one = (
        flat_in.astype(jnp.float32)
        + jnp.dot(attended_low, w_output, preferred_element_type=jnp.float32)
        + b_output
    )
    first, norm_one_back = jax.vjp(
        layer_norm, summed_one, gain_one.astype(jnp.float32), shift_one.astype(jnp.float32)
    )
    first_low = first.astype(jnp.bfloat16)
    rows_all = lax.all_gather(first_low, "mp", axis=0, tiled=True)
    hidden = jnp.dot(rows_all, w_in, preferred_element_type=jnp.float32) + b_in
    active_full, gelu_back = jax.vjp(gelu_tanh, hidden)
    active = active_full.astype(jnp.bfloat16)
    feed = lax.psum_scatter(
        jnp.einsum(
            "rf,df->rd",
            lax.slice_in_dim(active, 0, first_low.shape[0] * lax.axis_size("mp"), axis=0),
            w_out,
            preferred_element_type=jnp.float32,
        ),
        "mp",
        scatter_dimension=0,
        tiled=True,
    )
    summed_two = first + feed + b_out
    output, norm_two_back = jax.vjp(
        layer_norm, summed_two, gain_two.astype(jnp.float32), shift_two.astype(jnp.float32)
    )
    grad_two, gain_two_grad, shift_two_grad = norm_two_back(
        grad_out.reshape(-1, width).astype(jnp.float32)
    )
    grad_feed = grad_two.astype(jnp.bfloat16)
    b_out_grad = jnp.sum(grad_feed, axis=0, dtype=jnp.float32)
    grads_all = lax.all_gather(grad_feed, "mp", axis=0, tiled=True)
    w_out_grad = jnp.einsum("rd,rf->df", grads_all, active, preferred_element_type=jnp.float32)
    grad_hidden = gelu_back(jnp.dot(grads_all, w_out, preferred_element_type=jnp.float32))[
        0
    ].astype(jnp.bfloat16)
    w_in_grad = jnp.einsum("rd,rf->df", rows_all, grad_hidden, preferred_element_type=jnp.float32)
    grad_first = grad_two + lax.psum_scatter(
        jnp.einsum(
            "rf,df->rd",
            lax.slice_in_dim(grad_hidden, 0, grad_feed.shape[0] * lax.axis_size("mp"), axis=0),
            w_in,
            preferred_element_type=jnp.float32,
        ),
        "mp",
        scatter_dimension=0,
        tiled=True,
    )
    b_in_grad = lax.dynamic_update_slice_in_dim(
        jnp.zeros((FF,), jnp.float32),
        jnp.sum(grad_hidden, axis=0, dtype=jnp.float32),
        device * w_in.shape[1],
        0,
    )
    grad_sum_one, gain_one_grad, shift_one_grad = norm_one_back(grad_first)
    grad_branch = grad_sum_one.astype(jnp.bfloat16)
    b_output_grad = jnp.sum(grad_branch, axis=0, dtype=jnp.float32)
    w_output_grad = jnp.einsum(
        "rd,re->de", attended_low, grad_branch, preferred_element_type=jnp.float32
    )
    grad_attended = (
        jnp.einsum("re,de->rd", grad_branch, w_output, preferred_element_type=jnp.float32)
        .astype(jnp.bfloat16)
        .reshape(seq_count, local_rows, width)
    )

    def backward_item(seq_items):
        (
            query_one,
            key_one,
            value_one,
            length,
            rand_rows,
            sparse_totals,
            first_one,
            last_one,
            grad_one,
        ) = seq_items
        return attend_backward(
            query_one,
            key_one,
            value_one,
            length,
            rand_rows,
            sparse_totals,
            first_one,
            last_one,
            grad_one,
            device,
        )

    grad_query, grad_keys, grad_values = lax.map(
        backward_item,
        (
            query_seq,
            key_all,
            value_all,
            lengths,
            rand_blocks,
            totals,
            first_totals,
            last_totals,
            grad_attended,
        ),
    )
    key_sums, value_sums = (
        lax.psum_scatter(
            grad_keys.astype(jnp.bfloat16), "mp", scatter_dimension=1, tiled=True
        ).astype(jnp.float32),
        lax.psum_scatter(
            grad_values.astype(jnp.bfloat16), "mp", scatter_dimension=1, tiled=True
        ).astype(jnp.float32),
    )
    grad_q_low = grad_query.reshape(-1, width).astype(jnp.bfloat16)
    grad_k_low = key_sums.reshape(-1, width).astype(jnp.bfloat16)
    grad_v_low = value_sums.reshape(-1, width).astype(jnp.bfloat16)
    input_grad = grad_sum_one + jnp.einsum(
        "re,de->rd", grad_q_low, w_query, preferred_element_type=jnp.float32
    )
    input_grad = input_grad + jnp.einsum(
        "re,de->rd", grad_k_low, w_key, preferred_element_type=jnp.float32
    )
    input_grad = input_grad + jnp.einsum(
        "re,de->rd", grad_v_low, w_value, preferred_element_type=jnp.float32
    )
    w_query_grad = jnp.einsum("rd,re->de", flat_in, grad_q_low, preferred_element_type=jnp.float32)
    w_key_grad = jnp.einsum("rd,re->de", flat_in, grad_k_low, preferred_element_type=jnp.float32)
    w_value_grad = jnp.einsum("rd,re->de", flat_in, grad_v_low, preferred_element_type=jnp.float32)
    b_query_grad = jnp.sum(grad_q_low, axis=0, dtype=jnp.float32)
    b_value_grad = jnp.sum(grad_v_low, axis=0, dtype=jnp.float32)
    reduced = (
        lax.psum_scatter(
            w_query_grad.astype(jnp.bfloat16), "dp", scatter_dimension=0, tiled=True
        ).astype(jnp.float32),
        lax.psum_scatter(
            w_key_grad.astype(jnp.bfloat16), "dp", scatter_dimension=0, tiled=True
        ).astype(jnp.float32),
        lax.psum_scatter(
            w_value_grad.astype(jnp.bfloat16), "dp", scatter_dimension=0, tiled=True
        ).astype(jnp.float32),
        lax.psum_scatter(
            w_output_grad.astype(jnp.bfloat16), "dp", scatter_dimension=0, tiled=True
        ).astype(jnp.float32),
        lax.psum_scatter(
            w_in_grad.astype(jnp.bfloat16), "dp", scatter_dimension=0, tiled=True
        ).astype(jnp.float32),
        lax.psum_scatter(
            w_out_grad.astype(jnp.bfloat16), "dp", scatter_dimension=0, tiled=True
        ).astype(jnp.float32),
        lax.psum_scatter(
            b_query_grad.astype(jnp.bfloat16), "dp", scatter_dimension=0, tiled=True
        ).astype(jnp.float32),
        lax.psum_scatter(
            b_value_grad.astype(jnp.bfloat16), "dp", scatter_dimension=0, tiled=True
        ).astype(jnp.float32),
        lax.psum_scatter(
            b_output_grad.astype(jnp.bfloat16), "dp", scatter_dimension=0, tiled=True
        ).astype(jnp.float32),
        lax.psum_scatter(
            gain_one_grad.astype(jnp.bfloat16), "dp", scatter_dimension=0, tiled=True
        ).astype(jnp.float32),
        lax.psum_scatter(
            shift_one_grad.astype(jnp.bfloat16), "dp", scatter_dimension=0, tiled=True
        ).astype(jnp.float32),
        lax.psum_scatter(
            b_in_grad.astype(jnp.bfloat16), "dp", scatter_dimension=0, tiled=True
        ).astype(jnp.float32),
        lax.psum_scatter(
            b_out_grad.astype(jnp.bfloat16), "dp", scatter_dimension=0, tiled=True
        ).astype(jnp.float32),
        lax.psum_scatter(
            gain_two_grad.astype(jnp.bfloat16), "dp", scatter_dimension=0, tiled=True
        ).astype(jnp.float32),
        lax.psum_scatter(
            shift_two_grad.astype(jnp.bfloat16), "dp", scatter_dimension=0, tiled=True
        ).astype(jnp.float32),
    )
    query_part, key_part_out, value_part, output_part = (
        lax.psum_scatter(
            reduced[0].astype(jnp.bfloat16), "mp", scatter_dimension=1, tiled=True
        ).astype(jnp.float32),
        lax.psum_scatter(
            reduced[1].astype(jnp.bfloat16), "mp", scatter_dimension=1, tiled=True
        ).astype(jnp.float32),
        lax.psum_scatter(
            reduced[2].astype(jnp.bfloat16), "mp", scatter_dimension=1, tiled=True
        ).astype(jnp.float32),
        lax.psum_scatter(
            reduced[3].astype(jnp.bfloat16), "mp", scatter_dimension=1, tiled=True
        ).astype(jnp.float32),
    )
    in_part = reduced[4]
    out_part = reduced[5]
    vectors = lax.psum(
        (
            reduced[6],
            reduced[7],
            reduced[8],
            reduced[9],
            reduced[10],
            reduced[11],
            reduced[12],
            reduced[13],
            reduced[14],
        ),
        "mp",
    )
    return (
        output.astype(jnp.bfloat16).reshape(seq_count, local_rows, width),
        input_grad.reshape(seq_count, local_rows, width),
        query_part,
        vectors[0],
        key_part_out,
        value_part,
        vectors[1],
        output_part,
        vectors[2],
        vectors[3],
        vectors[4],
        in_part,
        vectors[5],
        out_part,
        vectors[6],
        vectors[7],
        vectors[8],
    )


def solution(mesh):
    in_specs = (
        P("dp", "mp", None),
        P("dp", "mp", None),
        P("dp"),
        P("dp", "mp", None),
        P(),
        P(),
        P(),
        P(),
        P(),
        P(),
        P(),
        P(),
        P(),
        P(None, "mp"),
        P("mp"),
        P(None, "mp"),
        P(),
        P(),
        P(),
    )
    out_specs = (
        P("dp", "mp", None),
        P("dp", "mp", None),
        P("dp", "mp"),
        P("dp"),
        P("dp", "mp"),
        P("dp", "mp"),
        P("dp"),
        P("dp", "mp"),
        P("dp"),
        P("dp"),
        P("dp"),
        P("dp", "mp"),
        P("dp"),
        P("dp", "mp"),
        P("dp"),
        P("dp"),
        P("dp"),
    )
    return jax.shard_map(local, mesh=mesh, in_specs=in_specs, out_specs=out_specs, check_vma=False)
```

profile of v0, /device:TPU:0, one launch (start us, length us, event | category | flops | bytes accessed | tf_op | source)
XLA Modules:
  0.0 1131.7 jit_solution(14632041343678927208)
XLA Ops:
  41.5 19.7 %reshape.750 = bf16[8,512,12,64]{3,2,1,0:T(8,128)(2,1)} reshape(bf16[64,64,768]{2,1,0:T(8,128)(2,1)} %gather_fusion) | data formatting | bytes 12582912 | tf_op jit(solution)/shard_map/while/body/eval_jaxpr/reshape | solution.py:65
  61.2 17.7 %copy.302 = bf16[8,512,12,64]{1,3,2,0:T(8,128)(2,1)} copy(bf16[8,512,12,64]{3,2,1,0:T(8,128)(2,1)} %reshape.750) | data formatting | bytes 12582912 | tf_op jit(solution)/shard_map/while/body/eval_jaxpr/reshape | solution.py:65
  78.8 19.7 %reshape.751 = bf16[8,512,12,64]{3,2,1,0:T(8,128)(2,1)} reshape(bf16[64,64,768]{2,1,0:T(8,128)(2,1)} %gather_fusion.1) | data formatting | bytes 12582912 | tf_op jit(solution)/shard_map/while/body/eval_jaxpr/reshape | solution.py:65
  98.5 17.7 %copy.301 = bf16[8,512,12,64]{1,3,2,0:T(8,128)(2,1)} copy(bf16[8,512,12,64]{3,2,1,0:T(8,128)(2,1)} %reshape.751) | data formatting | bytes 12582912 | tf_op jit(solution)/shard_map/while/body/eval_jaxpr/reshape | solution.py:65
  126.6 9.4 convolution_bitcast_fusion.1
  141.6 14.5 %conditional.4 = (f32[12,64,1]{1,0,2:T(8,128)}, bf16[64,768]{0,1:T(8,128)(2,1)}) conditional(s32[]{:T(128)} %convert_element_type.251, () %tuple.48, (s32[]{:T(128)}, bf16[64,768]{1,0:T(8,128)(2,1)S(1)}, bf16[1024,768]{1,0:T(8,128)(2,1)}, bf16[1024,768]{1,0:T(8,128)(2,1)}) %tuple.49), branch_computations={%region_3.4_spmd, %region_4.7_spmd} | conditional | flops 209977600 | bytes 25781296 | solution.py:187
  171.3 23.4 %all-gather.7.cloned.1.call-done = bf16[1024,768]{1,0:T(8,128)(2,1)} async-done(((bf16[512,768]{1,0:T(8,128)(2,1)}), bf16[1024,768]{1,0:T(8,128)(2,1)}) %all-gather.7.cloned.1.call-update) | async-done | bytes 1572880 | tf_op jit(solution)/shard_map/all_gather | solution.py:334
  194.7 7.1 multiply_convert_fusion.3
  208.4 11.5 %reduce-scatter.23.cloned.1.call-done = f32[512,768]{1,0:T(8,128)} async-done(((f32[1024,768]{1,0:T(8,128)}), f32[512,768]{1,0:T(8,128)}) %reduce-scatter.23.cloned.1.call-update) | async-done | bytes 1572880 | tf_op jit(solution)/shard_map/reduce_scatter | solution.py:338
  228.6 11.1 all-gather.9.cloned.1.call-done
  239.7 9.3 convert_reduce_fusion
  255.1 12.2 %reduce-scatter.25.cloned.1.call-done = f32[512,768]{1,0:T(8,128)} async-done(((f32[1024,768]{1,0:T(8,128)}), f32[512,768]{1,0:T(8,128)}) %reduce-scatter.25.cloned.1.call-update) | async-done | bytes 1572880 | tf_op jit(solution)/shard_map/reduce_scatter | solution.py:364
  283.4 9.8 multiply_reduce_fusion.2
  293.2 9.8 multiply_convert_fusion.2
  317.2 28.0 %conditional.6 = (f32[64,768]{0,1:T(8,128)S(1)}, f32[1024,768]{1,0:T(8,128)}, f32[1024,768]{1,0:T(8,128)}) conditional(s32[]{:T(128)} %convert_element_type.251, () %tuple.52, (s32[]{:T(128)}, bf16[64,768]{1,0:T(8,128)(2,1)S(1)}, bf16[1024,768]{1,0:T(8,128)(2,1)S(1)}, f32[12,64,1]{1,0,2:T(8,128)}, bf16[512,768]{1,0:T(8,128)(2,1)S(1)}, ...), branch_computations={%region_22.23_spmd, %region_23.25_spmd} | conditional | flops 511230208 | bytes 80227448 | solution.py:260
  362.1 9.0 multiply_bitcast_fusion
  371.1 25.2 %copy.324 = f32[8,512,12,64]{3,2,1,0:T(8,128)} copy(f32[8,512,12,64]{1,3,2,0:T(8,128)} %multiply_bitcast_fusion) | data formatting | bytes 25165824 | tf_op jit(solution)/shard_map/while/body/eval_jaxpr/mul | solution.py:238
  396.3 18.9 %reshape.709 = f32[64,49152]{1,0:T(8,128)} reshape(f32[8,512,12,64]{3,2,1,0:T(8,128)} %copy.324) | data formatting | bytes 25165824 | tf_op jit(solution)/shard_map/while/body/eval_jaxpr/reshape | solution.py:250
  415.2 20.2 %scatter_custom_fusion = f32[16,49152]{1,0:T(8,128)} fusion(s32[64]{0:T(128)S(1)} %reshape.707, f32[64,49152]{1,0:T(8,128)} %reshape.709, f32[]{:T(128)} %constant.258.clone.1), kind=kCustom, calls=%fused_computation.96 | custom fusion | flops 3145728 | bytes 3146240 | tf_op jit(solution)/shard_map/while/body/eval_jaxpr/scatter-add | solution.py:249
  444.4 9.1 convolution_bitcast_fusion
  453.5 25.2 %copy.328 = f32[8,512,12,64]{3,2,1,0:T(8,128)} copy(f32[8,512,12,64]{1,3,2,0:T(8,128)} %convolution_bitcast_fusion) | data formatting | bytes 25165824 | tf_op jit(solution)/shard_map/while/body/eval_jaxpr/nhqk,nqhd->nkhd/transpose | solution.py:241
  478.7 18.9 %reshape.717 = f32[64,49152]{1,0:T(8,128)} reshape(f32[8,512,12,64]{3,2,1,0:T(8,128)} %copy.328) | data formatting | bytes 25165824 | tf_op jit(solution)/shard_map/while/body/eval_jaxpr/reshape | solution.py:253
  497.6 19.8 %scatter_custom_fusion.1 = f32[16,49152]{1,0:T(8,128)} fusion(s32[64]{0:T(128)S(1)} %reshape.707, f32[64,49152]{1,0:T(8,128)} %reshape.717, f32[]{:T(128)} %constant.258.clone.1), kind=kCustom, calls=%fused_computation.94 | custom fusion | flops 3145728 | bytes 3146240 | tf_op jit(solution)/shard_map/while/body/eval_jaxpr/scatter-add | solution.py:252
  526.2 6.5 convolution_convert_fusion
  545.9 12.4 %reduce-scatter.29.cloned.1.call-done = bf16[1,512,768]{2,1,0:T(8,128)(2,1)} async-done(((bf16[1,1024,768]{2,1,0:T(8,128)(2,1)}), bf16[1,512,768]{2,1,0:T(8,128)(2,1)}) %reduce-scatter.29.cloned.1.call-update) | async-done | bytes 786448 | tf_op jit(solution)/shard_map/reduce_scatter | solution.py:436
  564.5 127.8 %reduce-scatter.41.cloned.1.call-done = bf16[48,1536]{1,0:T(8,128)(2,1)} async-done(((bf16[768,1536]{1,0:T(8,128)(2,1)}), bf16[48,1536]{1,0:T(8,128)(2,1)}) %reduce-scatter.41.cloned.1.call-update) | async-done | bytes 147472 | tf_op jit(solution)/shard_map/reduce_scatter | solution.py:473
  693.9 131.5 %reduce-scatter.39.cloned.1.call-done = bf16[48,1536]{1,0:T(8,128)(2,1)} async-done(((bf16[768,1536]{1,0:T(8,128)(2,1)}), bf16[48,1536]{1,0:T(8,128)(2,1)}) %reduce-scatter.39.cloned.1.call-update) | async-done | bytes 147472 | tf_op jit(solution)/shard_map/reduce_scatter | solution.py:470
  836.0 9.2 reduce-scatter.31.cloned.1.call-done
  847.0 77.1 %all-reduce.10 = (bf16[768]{0:T(1024)(128)(2,1)S(1)}, bf16[768]{0:T(1024)(128)(2,1)S(1)}, bf16[768]{0:T(1024)(128)(2,1)S(1)}, bf16[768]{0:T(1024)(128)(2,1)S(1)}...) all-reduce(bf16[768]{0:T(1024)(128)(2,1)S(1)} %convert_reduce_fusio, ...), channel_id=10, replica_groups=mesh['dp'=16,'mp'=2] {'dp'}, use_global_device_ids=true, to_apply=%region_35.36.clone | all-reduce | flops 9216 | bytes 36864
  930.8 44.6 %reduce-scatter.45.cloned.1.call-done = bf16[48,768]{1,0:T(8,128)(2,1)} async-done(((bf16[768,768]{1,0:T(8,128)(2,1)}), bf16[48,768]{1,0:T(8,128)(2,1)}) %reduce-scatter.45.cloned.1.call-update) | async-done | bytes 73744
  977.3 126.1 %reduce-scatter.47.cloned.1.call-done = bf16[48,768]{1,0:T(8,128)(2,1)} async-done(((bf16[768,768]{1,0:T(8,128)(2,1)}), bf16[48,768]{1,0:T(8,128)(2,1)}) %reduce-scatter.47.cloned.1.call-update) | async-done | bytes 73744
  1113.7 9.3 reduce-scatter.35.cloned.1.call-done
  (302 shorter events, 250.1 us)
Async XLA Ops:
  7.2 187.5 %copy-start = (bf16[768,1536]{1,0:T(8,128)(2,1)S(1)}, bf16[768,1536]{1,0:T(8,128)(2,1)}, u32[]{:S(2)}) copy-start(bf16[768,1536]{1,0:T(8,128)(2,1)} %param.40) | copy-start | bytes 7077892
  7.2 19.6 %all-gather.13.cloned.1.call-start = ((), (), s32[]{:S(2)}) async-start(), calls=%async_computation.27 | async-start | bytes 2359296 | tf_op jit(solution)/shard_map/all_gather | solution.py:312
  10.7 25.8 %all-gather.11.cloned.1.call-start = ((), (), s32[]{:S(2)}) async-start(), calls=%async_computation.26 | async-start | bytes 2359296 | tf_op jit(solution)/shard_map/all_gather | solution.py:313
  13.6 181.1 %all-gather.7.cloned.1.call-start = ((), (), s32[]{:S(2)}) async-start(), calls=%async_computation.14 | async-start | bytes 2359296 | tf_op jit(solution)/shard_map/all_gather | solution.py:334
  126.6 166.6 %copy-start.25 = (f32[8,12,64]{2,1,0:T(8,128)}, f32[8,12,64]{2,1,0:T(8,128)S(1)}, u32[]{:S(2)}) copy-start(f32[8,12,64]{2,1,0:T(8,128)S(1)} %log_add_fusion.2) | copy-start | bytes 73732
  171.3 48.7 %reduce-scatter.23.cloned.1.call-start = ((), (), s32[]{:S(2)}) async-start(), calls=%async_computation.15 | async-start | bytes 4718592 | tf_op jit(solution)/shard_map/reduce_scatter | solution.py:338
  207.7 31.9 %all-gather.9.cloned.1.call-start = ((), (), s32[]{:S(2)}) async-start(), calls=%async_computation.16 | async-start | bytes 2359296 | tf_op jit(solution)/shard_map/all_gather | solution.py:358
  228.5 38.7 %reduce-scatter.25.cloned.1.call-start = ((), (), s32[]{:S(2)}) async-start(), calls=%async_computation.17 | async-start | bytes 4718592 | tf_op jit(solution)/shard_map/reduce_scatter | solution.py:364
  255.0 283.6 %reduce-scatter.37.cloned.1.call-start = ((), (), s32[]{:S(2)}) async-start(), calls=%async_computation.23 | async-start | bytes 1253376 | tf_op jit(solution)/shard_map/reduce_scatter | solution.py:467
  275.0 265.6 %reduce-scatter.43.cloned.1.call-start = ((), (), s32[]{:S(2)}) async-start(), calls=%async_computation.28 | async-start | bytes 1253376
  277.6 39.6 %copy-start.29 = (bf16[512,768]{1,0:T(8,128)(2,1)}, bf16[512,768]{1,0:T(8,128)(2,1)S(1)}, u32[]{:S(2)}) copy-start(bf16[512,768]{1,0:T(8,128)(2,1)S(1)} %get-tuple-element.508) | copy-start | bytes 2359300
  361.9 180.5 %reduce-scatter.27.cloned.1.call-start = ((), (), s32[]{:S(2)}) async-start(), calls=%async_computation.18 | async-start | bytes 2359296 | tf_op jit(solution)/shard_map/reduce_scatter | solution.py:433
  444.3 114.0 %reduce-scatter.29.cloned.1.call-start = ((), (), s32[]{:S(2)}) async-start(), calls=%async_computation.19 | async-start | bytes 2359296 | tf_op jit(solution)/shard_map/reduce_scatter | solution.py:436
  526.1 166.1 %reduce-scatter.41.cloned.1.call-start = ((), (), s32[]{:S(2)}) async-start(), calls=%async_computation.25 | async-start | bytes 2506752 | tf_op jit(solution)/shard_map/reduce_scatter | solution.py:473
  532.8 292.7 %reduce-scatter.39.cloned.1.call-start = ((), (), s32[]{:S(2)}) async-start(), calls=%async_computation.24 | async-start | bytes 2506752 | tf_op jit(solution)/shard_map/reduce_scatter | solution.py:470
  538.6 295.8 %reduce-scatter.49.cloned.1.call-start = ((), (), s32[]{:S(2)}) async-start(), calls=%async_computation.31 | async-start | bytes 294912
  540.5 304.7 %reduce-scatter.31.cloned.1.call-start = ((), (), s32[]{:S(2)}) async-start(), calls=%async_computation.20 | async-start | bytes 294912 | tf_op jit(solution)/shard_map/reduce_scatter | solution.py:505
  542.3 433.0 %reduce-scatter.45.cloned.1.call-start = ((), (), s32[]{:S(2)}) async-start(), calls=%async_computation.29 | async-start | bytes 1253376
  545.8 18.2 %copy-start.18 = (bf16[1,512,768]{2,1,0:T(8,128)(2,1)S(1)}, bf16[1,512,768]{2,1,0:T(8,128)(2,1)}, u32[]{:S(2)}) copy-start(bf16[1,512,768]{2,1,0:T(8,128)(2,1)} %param.28) | copy-start | bytes 2359300
  545.8 18.4 %copy-start.40 = (bf16[1536]{0:T(1024)(128)(2,1)S(1)}, bf16[1536]{0:T(1024)(128)(2,1)}, u32[]{:S(2)}) copy-start(bf16[1536]{0:T(1024)(128)(2,1)} %get-tuple-element.477) | copy-start | bytes 9220
  545.9 557.5 %reduce-scatter.47.cloned.1.call-start = ((), (), s32[]{:S(2)}) async-start(), calls=%async_computation.30 | async-start | bytes 1253376
  560.5 266.5 %copy-start.6 = (f32[512,768]{0,1:T(8,128)S(1)}, f32[512,768]{0,1:T(8,128)}, u32[]{:S(2)}) copy-start(f32[512,768]{0,1:T(8,128)} %dynamic_update_slice.37) | copy-start | bytes 4718596
  562.1 550.1 %reduce-scatter.33.cloned.1.call-start = ((), (), s32[]{:S(2)}) async-start(), calls=%async_computation.21 | async-start | bytes 294912 | tf_op jit(solution)/shard_map/reduce_scatter | solution.py:508
  827.1 19.8 %copy-start.20 = (bf16[1,512,768]{2,1,0:T(8,128)(2,1)S(1)}, bf16[1,512,768]{2,1,0:T(8,128)(2,1)}, u32[]{:S(2)}) copy-start(bf16[1,512,768]{2,1,0:T(8,128)(2,1)} %reduce-scatter.29.cloned.1.call-done) | copy-start | bytes 2359300
  827.2 19.7 %copy-start.33 = (bf16[768]{0:T(1024)(128)(2,1)S(1)}, bf16[768]{0:T(1024)(128)(2,1)}, u32[]{:S(2)}) copy-start(bf16[768]{0:T(1024)(128)(2,1)} %get-tuple-element.454) | copy-start | bytes 4612
  827.3 19.7 %copy-start.34 = (bf16[768]{0:T(1024)(128)(2,1)S(1)}, bf16[768]{0:T(1024)(128)(2,1)}, u32[]{:S(2)}) copy-start(bf16[768]{0:T(1024)(128)(2,1)} %get-tuple-element.475) | copy-start | bytes 4612
  827.3 19.7 %copy-start.35 = (bf16[768]{0:T(1024)(128)(2,1)S(1)}, bf16[768]{0:T(1024)(128)(2,1)}, u32[]{:S(2)}) copy-start(bf16[768]{0:T(1024)(128)(2,1)} %get-tuple-element.452) | copy-start | bytes 4612
  827.3 19.7 %copy-start.36 = (bf16[768]{0:T(1024)(128)(2,1)S(1)}, bf16[768]{0:T(1024)(128)(2,1)}, u32[]{:S(2)}) copy-start(bf16[768]{0:T(1024)(128)(2,1)} %get-tuple-element.456) | copy-start | bytes 4612
  827.3 19.7 %copy-start.37 = (bf16[768]{0:T(1024)(128)(2,1)S(1)}, bf16[768]{0:T(1024)(128)(2,1)}, u32[]{:S(2)}) copy-start(bf16[768]{0:T(1024)(128)(2,1)} %get-tuple-element.479) | copy-start | bytes 4612
  830.6 96.4 %copy-start.31 = (f32[512]{0:T(512)S(1)}, f32[512]{0:T(512)}, u32[]{:S(2)}) copy-start(f32[512]{0:T(512)} %copy-done.30) | copy-start | bytes 6148
  924.5 200.2 %copy-start.1 = (bf16[768,1536]{1,0:T(8,128)(2,1)S(1)}, bf16[768,1536]{1,0:T(8,128)(2,1)}, u32[]{:S(2)}) copy-start(bf16[768,1536]{1,0:T(8,128)(2,1)} %param.40) | copy-start | bytes 7077892
  977.1 145.9 %reduce-scatter.35.cloned.1.call-start = ((), (), s32[]{:S(2)}) async-start(), calls=%async_computation.22 | async-start | bytes 294912 | tf_op jit(solution)/shard_map/reduce_scatter | solution.py:511
  (35 other events, 154.4 us)
Sparse Core Ops, SparseCore 0:
  10.8 12.4 all-gather.12
  25.4 10.9 all-gather.10
  171.4 23.2 all-gather.6
  207.9 12.0 reduce-scatter.22
  228.7 10.9 all-gather.8
  255.2 12.0 reduce-scatter.24
  275.1 125.4 reduce-scatter.36
  405.4 123.4 reduce-scatter.42
  531.7 8.0 reduce-scatter.26
  542.0 16.2 reduce-scatter.28
  563.3 128.9 reduce-scatter.40
  697.8 127.5 reduce-scatter.38
  827.6 6.6 reduce-scatter.48
  836.5 8.7 reduce-scatter.30
  849.8 125.4 reduce-scatter.44
  980.0 123.3 reduce-scatter.46
  1105.5 6.6 reduce-scatter.32
  1114.2 8.7 reduce-scatter.34
where the time goes:
time: 1140 us; the launch traced here: 1130 us
  waiting for transfers between devices  532 us (47%)
  local copies, waits for them, and re-layouts  271 us (24%)
  matrix products  137 us (12%)
  other arithmetic  93.3 us (8%)
  blocking collectives  80.1 us (7%)
  between operations  17.3 us (2%)
    unnamed x22, waiting for transfers between devices  175 us
    reduce_scatter x1, waiting for transfers between devices, local(): lax.psum_scatter(w_in_grad.astype(jnp.bfloat16), 'dp', scatter_dimension=...  132 us
    reduce_scatter x1, waiting for transfers between devices, local(): lax.psum_scatter(w_out_grad.astype(jnp.bfloat16), 'dp', scatter_dimension...  128 us
    unnamed x1, blocking collectives  77.1 us
    reshape x4, local copies, waits for them, and re-layouts, gather_slots(): picked.reshape(slot_blocks.shape[0], slot_blocks.shape[1] * BLK, HEADS, HD)  74.7 us
    unnamed x107, local copies, waits for them, and re-layouts  26.1 us
    transpose x1, local copies, waits for them, and re-layouts, attend_backward(): jnp.einsum('nhqk,nqhd->nkhd', exact_probs.astype(jnp.bfloat16), grad_head...  25.2 us
    mul x1, local copies, waits for them, and re-layouts, attend_backward(): jnp.einsum('nhqk,nqhd->nkhd', grad_scores, query_blocks, preferred_elemen...  25.2 us
  transfers between devices with their start and end apart: 18, of which 14 were waited for; matrix products, arithmetic and copies ran while one was open for 28% of the time, Pallas kernels for 0%

commit v1 on v0

--- a/solution.py
+++ b/solution.py
@@ -1,6 +1,10 @@
+import functools
+
 import jax
 import jax.numpy as jnp
 from jax import lax
+from jax.experimental import pallas as pl
+from jax.experimental.pallas import tpu as pltpu
 from jax.sharding import PartitionSpec as P
 
 HEADS = 12
@@ -12,6 +16,604 @@
 
 negative_fill = -1000000000.0
 norm_epsilon = 1e-12
+
+
+F32 = jnp.float32
+BF16 = jnp.bfloat16
+NN = (((1,), (0,)), ((), ()))
+NT = (((1,), (1,)), ((), ()))
+TN = (((0,), (0,)), ((), ()))
+
+
+def mm(a, b, dims=NN):
+    return lax.dot_general(a, b, dims, preferred_element_type=F32)
+
+
+def params(mib=56):
+    return pltpu.CompilerParams(vmem_limit_bytes=mib << 20)
+
+
+def cost(flops, nbytes, trans=0):
+    return pl.CostEstimate(flops=int(flops), bytes_accessed=int(nbytes), transcendentals=int(trans))
+
+
+def shape(dims, dtype):
+    return jax.ShapeDtypeStruct(dims, dtype)
+
+
+def row_stats(u):
+    mean = jnp.mean(u, axis=-1, keepdims=True)
+    cen = u - mean
+    var = jnp.mean(cen * cen, axis=-1, keepdims=True)
+    rs = lax.rsqrt(var + norm_epsilon)
+    return cen * rs, rs
+
+
+def attn_fwd_body(sc, xo, xt, wq, wk, wv, bq, bv, rand, q_o, k_o, v_o, p_o, ao, at, bias):
+    half = xo.shape[0]
+    rows = 2 * half
+    nb = rows // BLK
+    tile = 256
+
+    @pl.when(pl.program_id(0) == 0)
+    def _():
+        c = sc[0]
+        ln = sc[1]
+        last = (ln + BLK - 1) // BLK - 1
+        lb = lax.broadcasted_iota(jnp.int32, (nb, rows), 0)
+        kp = lax.broadcasted_iota(jnp.int32, (nb, rows), 1)
+        qb = jnp.where(lb < nb // 2, lb + (nb // 2) * c, lb - (nb // 2) * c)
+        kpos = jnp.where(kp < half, kp + half * c, kp - half * c)
+        kb = kpos // BLK
+        ok = (jnp.abs(kb - qb) <= 1) | (kb == 0) | (kb == last)
+        for j in range(rand.shape[1]):
+            ok = ok | (kb == rand[:, j : j + 1])
+        ok = ok | (qb == 0) | (qb == last)
+        ok = ok & (kpos < ln)
+        table = jnp.where(ok, 0.0, -1e30).astype(F32)
+        for b in range(nb):
+            bias[b] = jnp.broadcast_to(table[b : b + 1, :], (8, rows))
+
+    for i, xr in enumerate((xo, xt)):
+        rs = slice(i * half, (i + 1) * half)
+        q_o[rs, :] = (mm(xr[...], wq[...]) + bq[...].astype(F32)).astype(BF16)
+        k_o[rs, :] = mm(xr[...], wk[...]).astype(BF16)
+        v_o[rs, :] = (mm(xr[...], wv[...]) + bv[...].astype(F32)).astype(BF16)
+
+    lane = lax.broadcasted_iota(jnp.int32, (tile, 2 * HD), 1)
+    low = lane < HD
+    for i, a_ref in enumerate((ao, at)):
+
+        def step(t, carry, i=i, a_ref=a_ref):
+            r0 = pl.multiple_of(i * half + t * tile, tile)
+            q = q_o[pl.ds(r0, tile), :] * BF16(HD**-0.5)
+            outs = []
+            for h in range(2):
+                qh = jnp.where(low if h == 0 else ~low, q, BF16(0))
+                s = mm(qh, k_o[...], NT)
+                s = s.reshape(tile // BLK, BLK // 8, 8, rows)
+                s = s + bias[pl.ds(r0 // BLK, tile // BLK)][:, None]
+                s = s.reshape(tile, rows)
+                e = jnp.exp(s - jnp.max(s, axis=-1, keepdims=True))
+                p = (e * (1.0 / jnp.sum(e, axis=-1, keepdims=True))).astype(BF16)
+                p_o[h, pl.ds(r0, tile), :] = p
+                outs.append(mm(p, v_o[...]))
+            a = jnp.where(low, outs[0], outs[1]).astype(BF16)
+            a_ref[pl.ds(pl.multiple_of(t * tile, tile), tile), :] = a
+            return carry
+
+        lax.fori_loop(0, half // tile, step, 0)
+
+
+def attn_fwd(sc, xo, xt, wq, wk, wv, bq, bv, rand):
+    half, width = xo.shape
+    rows = 2 * half
+    pairs = HEADS // 4
+    pw = 2 * HD
+    whole = lambda a: pl.BlockSpec(a.shape, lambda p, s: (0,) * a.ndim)
+    wspec = pl.BlockSpec((width, pw), lambda p, s: (0, s[0] * pairs + p))
+    bspec = pl.BlockSpec((1, pw), lambda p, s: (0, s[0] * pairs + p))
+    ospec = lambda r: pl.BlockSpec((r, pw), lambda p, s: (0, p))
+    return pl.pallas_call(
+        attn_fwd_body,
+        grid_spec=pltpu.PrefetchScalarGridSpec(
+            num_scalar_prefetch=1,
+            grid=(pairs,),
+            in_specs=[whole(xo), whole(xt), wspec, wspec, wspec, bspec, bspec, whole(rand)],
+            out_specs=[ospec(rows)] * 3
+            + [pl.BlockSpec((2, rows, rows), lambda p, s: (p, 0, 0))]
+            + [ospec(half)] * 2,
+            scratch_shapes=[pltpu.VMEM((rows // BLK, 8, rows), F32)],
+        ),
+        out_shape=[shape((rows, pairs * pw), BF16)] * 3
+        + [shape((2 * pairs, rows, rows), BF16)]
+        + [shape((half, pairs * pw), BF16)] * 2,
+        compiler_params=params(),
+        cost_estimate=cost(20e9, 20e6, 6 * rows * rows),
+        name="attn_fwd",
+    )(sc, xo, xt, wq, wk, wv, bq, bv, rand)
+
+
+def attn_bwd_body(
+    sc, xo, xt, wq, wk, wv, q_i, k_i, v_i, p_i, ao, at, go, gt,
+    wg, bqg, bvg, igo, igt, g_s, gT, qT, dkT, dvT, dqkv, wcat, xT, acc,
+):
+    half = xo.shape[0]
+    rows = 2 * half
+    pw = 2 * HD
+    tile = 256
+    step_id = pl.program_id(0)
+
+    @pl.when(step_id == 0)
+    def _():
+        xT[:, :half] = xo[...].T
+        xT[:, half:] = xt[...].T
+
+    for i, w in enumerate((wq, wk, wv)):
+        wcat[:, i * pw : (i + 1) * pw] = w[...]
+    g_s[:half, :] = go[...]
+    g_s[half:, :] = gt[...]
+    gT[...] = g_s[...].T
+    qT[...] = q_i[...].T
+    dkT[...] = jnp.zeros_like(dkT)
+    dvT[...] = jnp.zeros_like(dvT)
+    lane = lax.broadcasted_iota(jnp.int32, (tile, pw), 1)
+    low = lane < HD
+
+    for i, a_ref in enumerate((ao, at)):
+
+        def step(t, carry, i=i, a_ref=a_ref):
+            r0 = pl.multiple_of(i * half + t * tile, tile)
+            a0 = pl.multiple_of(t * tile, tile)
+            g = g_s[pl.ds(r0, tile), :]
+            ga = g.astype(F32) * a_ref[pl.ds(a0, tile), :].astype(F32)
+            outs = []
+            for h in range(2):
+                mine = low if h == 0 else ~low
+                hs = slice(h * HD, (h + 1) * HD)
+                dp = mm(jnp.where(mine, g, BF16(0)), v_i[...], NT)
+                delta = jnp.sum(jnp.where(mine, ga, 0.0), axis=-1, keepdims=True)
+                p = p_i[h, pl.ds(r0, tile), :]
+                ds = (p.astype(F32) * (dp - delta)).astype(BF16)
+                outs.append(mm(ds, k_i[...]))
+                dvT[hs, :] += mm(gT[hs, pl.ds(r0, tile)], p)
+                dkT[hs, :] += mm(qT[hs, pl.ds(r0, tile)], ds)
+            dq = jnp.where(low, outs[0], outs[1]) * HD**-0.5
+            dqkv[pl.ds(r0, tile), 0:pw] = dq.astype(BF16)
+            return carry
+
+        lax.fori_loop(0, half // tile, step, 0)
+
+    dqkv[:, pw : 2 * pw] = (dkT[...].T * HD**-0.5).astype(BF16)
+    dqkv[:, 2 * pw : 3 * pw] = dvT[...].T.astype(BF16)
+    d = dqkv[...]
+    wg[...] = mm(xT[...], d).astype(BF16)
+    bqg[...] = jnp.sum(d[:, 0:pw].astype(F32), axis=0, keepdims=True)
+    bvg[...] = jnp.sum(d[:, 2 * pw :].astype(F32), axis=0, keepdims=True)
+    part = mm(d, wcat[...], NT)
+
+    @pl.when(step_id == 0)
+    def _():
+        acc[...] = part
+
+    @pl.when((step_id > 0) & (step_id < pl.num_programs(0) - 1))
+    def _():
+        acc[...] += part
+
+    @pl.when(step_id == pl.num_programs(0) - 1)
+    def _():
+        total = acc[...] + part
+        igo[...] = total[:half]
+        igt[...] = total[half:].astype(BF16)
+
+
+def attn_bwd(sc, xo, xt, wq, wk, wv, q, k, v, probs, ao, at, go, gt):
+    half, width = xo.shape
+    rows = 2 * half
+    pairs = HEADS // 4
+    pw = 2 * HD
+    whole = lambda a: pl.BlockSpec(a.shape, lambda p, s: (0,) * a.ndim)
+    wspec = pl.BlockSpec((width, pw), lambda p, s: (0, s[0] * pairs + p))
+    col = lambda r, w: pl.BlockSpec((r, w), lambda p, s: (0, p))
+    return pl.pallas_call(
+        attn_bwd_body,
+        grid_spec=pltpu.PrefetchScalarGridSpec(
+            num_scalar_prefetch=1,
+            grid=(pairs,),
+            in_specs=[whole(xo), whole(xt), wspec, wspec, wspec]
+            + [col(rows, pw)] * 3
+            + [pl.BlockSpec((2, rows, rows), lambda p, s: (p, 0, 0))]
+            + [col(half, pw)] * 4,
+            out_specs=[col(width, 3 * pw), col(1, pw), col(1, pw)]
+            + [pl.BlockSpec((half, width), lambda p, s: (0, 0))] * 2,
+            scratch_shapes=[
+                pltpu.VMEM((rows, pw), BF16),
+                pltpu.VMEM((pw, rows), BF16),
+                pltpu.VMEM((pw, rows), BF16),
+                pltpu.VMEM((pw, rows), F32),
+                pltpu.VMEM((pw, rows), F32),
+                pltpu.VMEM((rows, 3 * pw), BF16),
+                pltpu.VMEM((width, 3 * pw), BF16),
+                pltpu.VMEM((width, rows), BF16),
+                pltpu.VMEM((rows, width), F32),
+            ],
+        ),
+        out_shape=[
+            shape((width, 3 * pw * pairs), BF16),
+            shape((1, pw * pairs), F32),
+            shape((1, pw * pairs), F32),
+            shape((half, width), F32),
+            shape((half, width), BF16),
+        ],
+        compiler_params=params(),
+        cost_estimate=cost(40e9, 20e6),
+        name="attn_bwd",
+    )(sc, xo, xt, wq, wk, wv, q, k, v, probs, ao, at, go, gt)
+
+
+def proj_body(sc, a0, a1, x, w0, w1, b, g, s, u_o, f_o, fl_o):
+    u = x[...].astype(F32) + (mm(a0[...], w0[...]) + mm(a1[...], w1[...])) + b[...].astype(F32)
+    n, _ = row_stats(u)
+    first = n * g[...].astype(F32) + s[...].astype(F32)
+    u_o[...] = u
+    f_o[...] = first
+    fl_o[...] = first.astype(BF16)
+
+
+def proj_norm(sc, a_own, a_got, x, w_output, b, g, s):
+    rows, width = x.shape
+    t = 256
+    row = lambda w: pl.BlockSpec((t, w), lambda i, c: (i, 0))
+    vec = pl.BlockSpec((1, width), lambda i, c: (0, 0))
+    return pl.pallas_call(
+        proj_body,
+        grid_spec=pltpu.PrefetchScalarGridSpec(
+            num_scalar_prefetch=1,
+            grid=(rows // t,),
+            in_specs=[
+                row(width // 2),
+                row(width // 2),
+                row(width),
+                pl.BlockSpec((width // 2, width), lambda i, c: (c[0], 0)),
+                pl.BlockSpec((width // 2, width), lambda i, c: (1 - c[0], 0)),
+                vec,
+                vec,
+                vec,
+            ],
+            out_specs=[row(width)] * 3,
+        ),
+        out_shape=[shape((rows, width), F32), shape((rows, width), F32), shape((rows, width), BF16)],
+        compiler_params=params(),
+        cost_estimate=cost(2 * rows * width * width, 8e6),
+        name="proj_norm",
+    )(sc, a_own, a_got, x, w_output, w_output, b, g, s)
+
+
+def norm_one_back_body(sc, gtwo, p0, p1, u, g, w0, w1, gs_o, gb_o, ga0, ga1, gg, sg, bg):
+    e = gtwo[...] + p0[...] + p1[...].astype(F32)
+    n, rs = row_stats(u[...])
+    eg = e * g[...].astype(F32)
+    d = (eg - jnp.mean(eg, -1, keepdims=True) - n * jnp.mean(eg * n, -1, keepdims=True)) * rs
+    low = d.astype(BF16)
+    gs_o[...] = d
+    gb_o[...] = low
+    ga0[...] = mm(low, w0[...], NT).astype(BF16)
+    ga1[...] = mm(low, w1[...], NT).astype(BF16)
+
+    @pl.when(pl.program_id(0) == 0)
+    def _():
+        gg[...] = jnp.zeros_like(gg)
+        sg[...] = jnp.zeros_like(sg)
+        bg[...] = jnp.zeros_like(bg)
+
+    gg[...] += jnp.sum(e * n, 0, keepdims=True)
+    sg[...] += jnp.sum(e, 0, keepdims=True)
+    bg[...] += jnp.sum(low.astype(F32), 0, keepdims=True)
+
+
+def norm_one_back(sc, gtwo, p0, p1, u, g, w_output):
+    rows, width = u.shape
+    t = 256
+    row = lambda w: pl.BlockSpec((t, w), lambda i, c: (i, 0))
+    vec = pl.BlockSpec((1, width), lambda i, c: (0, 0))
+    return pl.pallas_call(
+        norm_one_back_body,
+        grid_spec=pltpu.PrefetchScalarGridSpec(
+            num_scalar_prefetch=1,
+            grid=(rows // t,),
+            in_specs=[row(width)] * 4
+            + [
+                vec,
+                pl.BlockSpec((width // 2, width), lambda i, c: (c[0], 0)),
+                pl.BlockSpec((width // 2, width), lambda i, c: (1 - c[0], 0)),
+            ],
+            out_specs=[row(width)] * 2 + [row(width // 2)] * 2 + [vec] * 3,
+        ),
+        out_shape=[shape((rows, width), F32), shape((rows, width), BF16)]
+        + [shape((rows, width // 2), BF16)] * 2
+        + [shape((1, width), F32)] * 3,
+        compiler_params=params(),
+        cost_estimate=cost(2 * rows * width * width, 10e6),
+        name="norm_one_back",
+    )(sc, gtwo, p0, p1, u, g, w_output, w_output)
+
+
+def w_output_body(sc, a0, a1, keep_cols, send_cols, keep, send):
+    for i, a in enumerate((a0, a1)):
+
+        @pl.when(pl.program_id(0) == i)
+        def _(a=a):
+            keep[...] = mm(a[...], keep_cols[...], TN)
+            send[...] = mm(a[...], send_cols[...], TN).astype(BF16)
+
+
+def w_output_grad(sc, a_own, a_got, gb):
+    rows, width = gb.shape
+    hw = width // 2
+    whole = pl.BlockSpec((rows, hw), lambda i, c: (0, 0))
+    out = pl.BlockSpec((hw, hw), lambda i, c: (i + c[0] - 2 * i * c[0], 0))
+    return pl.pallas_call(
+        w_output_body,
+        grid_spec=pltpu.PrefetchScalarGridSpec(
+            num_scalar_prefetch=1,
+            grid=(2,),
+            in_specs=[
+                whole,
+                whole,
+                pl.BlockSpec((rows, hw), lambda i, c: (0, c[0])),
+                pl.BlockSpec((rows, hw), lambda i, c: (0, 1 - c[0])),
+            ],
+            out_specs=[out, out],
+        ),
+        out_shape=[shape((width, hw), F32), shape((width, hw), BF16)],
+        compiler_params=params(),
+        cost_estimate=cost(2 * rows * width * width, 5e6),
+        name="w_output_grad",
+    )(sc, a_own, a_got, gb, gb)
+
+
+def ffn_fwd_body(x, w_in, b_in, w_out, act_o, slope_o, feed_o):
+    v = mm(x[...], w_in[...]) + b_in[...].astype(F32)
+    k0 = 0.7978845608028654
+    k1 = 0.044715
+    v2 = v * v
+    t = jnp.tanh(v * (k0 + (k0 * k1) * v2))
+    hp = 0.5 * t + 0.5
+    act = (v * hp).astype(BF16)
+    slope = hp + (0.5 * v) * (1.0 - t * t) * (k0 + (3 * k0 * k1) * v2)
+    act_o[...] = act
+    slope_o[...] = slope.astype(BF16)
+    feed_o[...] = mm(act, w_out[...], NT).astype(feed_o.dtype)
+
+
+def ffn_fwd(x, w_in, b_in, w_out, dtype):
+    rows, width = x.shape
+    ff = w_in.shape[1]
+    t = 256
+    whole = lambda a: pl.BlockSpec(a.shape, lambda i: (0, 0))
+    row = lambda w: pl.BlockSpec((t, w), lambda i: (i, 0))
+    return pl.pallas_call(
+        ffn_fwd_body,
+        grid=(rows // t,),
+        in_specs=[row(width), whole(w_in), whole(b_in), whole(w_out)],
+        out_specs=[row(ff), row(ff), row(width)],
+        out_shape=[shape((rows, ff), BF16)] * 2 + [shape((rows, width), dtype)],
+        compiler_params=params(),
+        cost_estimate=cost(4 * rows * width * ff, 8e6, rows * ff),
+        name="ffn_fwd",
+    )(x, w_in, b_in, w_out)
+
+
+def norm_two_body(first, f0, f1, b, g, s, go, out_o, gtwo_o, gf_o, gg, sg, bg):
+    u = first[...] + (f0[...] + f1[...].astype(F32)) + b[...].astype(F32)
+    n, rs = row_stats(u)
+    gain = g[...].astype(F32)
+    out_o[...] = (n * gain + s[...].astype(F32)).astype(BF16)
+    e = go[...].astype(F32)
+    eg = e * gain
+    d = (eg - jnp.mean(eg, -1, keepdims=True) - n * jnp.mean(eg * n, -1, keepdims=True)) * rs
+    low = d.astype(BF16)
+    gtwo_o[...] = d
+    gf_o[...] = low
+
+    @pl.when(pl.program_id(0) == 0)
+    def _():
+        gg[...] = jnp.zeros_like(gg)
+        sg[...] = jnp.zeros_like(sg)
+        bg[...] = jnp.zeros_like(bg)
+
+    gg[...] += jnp.sum(e * n, 0, keepdims=True)
+    sg[...] += jnp.sum(e, 0, keepdims=True)
+    bg[...] += jnp.sum(low.astype(F32), 0, keepdims=True)
+
+
+def norm_two(first, f0, f1, b, g, s, go):
+    rows, width = first.shape
+    t = 256
+    row = pl.BlockSpec((t, width), lambda i: (i, 0))
+    vec = pl.BlockSpec((1, width), lambda i: (0, 0))
+    return pl.pallas_call(
+        norm_two_body,
+        grid=(rows // t,),
+        in_specs=[row] * 3 + [vec] * 3 + [row],
+        out_specs=[row] * 3 + [vec] * 3,
+        out_shape=[
+            shape((rows, width), BF16),
+            shape((rows, width), F32),
+            shape((rows, width), BF16),
+        ]
+        + [shape((1, width), F32)] * 3,
+        compiler_params=params(),
+        cost_estimate=cost(30 * rows * width, 8e6),
+        name="norm_two",
+    )(first, f0, f1, b, g, s, go)
+
+
+def ffn_bwd_body(gf, slope, w_in, w_out, gh_o, part_o, bg):
+    gh = (mm(gf[...], w_out[...]) * slope[...].astype(F32)).astype(BF16)
+    gh_o[...] = gh
+    part_o[...] = mm(gh, w_in[...], NT).astype(part_o.dtype)
+
+    @pl.when(pl.program_id(0) == 0)
+    def _():
+        bg[...] = jnp.zeros_like(bg)
+
+    bg[...] += jnp.sum(gh.astype(F32), 0, keepdims=True)
+
+
+def ffn_bwd(gf, slope, w_in, w_out, dtype):
+    rows, width = gf.shape
+    ff = w_in.shape[1]
+    t = 256
+    whole = lambda a: pl.BlockSpec(a.shape, lambda i: (0, 0))
+    row = lambda w: pl.BlockSpec((t, w), lambda i: (i, 0))
+    return pl.pallas_call(
+        ffn_bwd_body,
+        grid=(rows // t,),
+        in_specs=[row(width), row(ff), whole(w_in), whole(w_out)],
+        out_specs=[row(ff), row(width), pl.BlockSpec((1, ff), lambda i: (0, 0))],
+        out_shape=[shape((rows, ff), BF16), shape((rows, width), dtype), shape((1, ff), F32)],
+        compiler_params=params(),
+        cost_estimate=cost(4 * rows * width * ff, 8e6),
+        name="ffn_bwd",
+    )(gf, slope, w_in, w_out)
+
+
+def ffn_weights_body(a0, a1, b0, b1, out):
+    out[...] = (mm(a0[...], b0[...], TN) + mm(a1[...], b1[...], TN)).astype(BF16)
+
+
+def ffn_weights(a0, a1, b0, b1):
+    rows, width = a0.shape
+    ff = b0.shape[1]
+    t = 256
+    whole = pl.BlockSpec((rows, ff), lambda i: (0, 0))
+    lhs = pl.BlockSpec((rows, t), lambda i: (0, i))
+    return pl.pallas_call(
+        ffn_weights_body,
+        grid=(width // t,),
+        in_specs=[lhs, lhs, whole, whole],
+        out_specs=pl.BlockSpec((t, ff), lambda i: (i, 0)),
+        out_shape=shape((width, ff), BF16),
+        compiler_params=params(),
+        cost_estimate=cost(4 * rows * width * ff, 8e6),
+        name="ffn_weights",
+    )(a0, a1, b0, b1)
+
+
+def pick(a, index, axis):
+    return lax.dynamic_index_in_dim(a, index, axis, keepdims=False)
+
+
+def halve(parts, size, bit_axis, stride):
+    me = lax.axis_index("dp")
+    mine = (me // stride) % 2
+    pairs = [(i, i ^ stride) for i in range(size)]
+    got = lax.ppermute(pick(parts, 1 - mine, bit_axis), "dp", pairs)
+    return (pick(parts, mine, bit_axis).astype(F32) + got.astype(F32)).astype(parts.dtype)
+
+
+def sum_rest(parts, size):
+    groups = size // 4
+    me = lax.axis_index("dp")
+    high = me // 4
+    total = pick(parts, high, 0).astype(F32)
+    for s in range(1, groups):
+        perm = [(i, (i + 4 * s) % size) for i in range(size)]
+        got = lax.ppermute(pick(parts, (high + s) % groups, 0), "dp", perm)
+        total = total + got.astype(F32)
+    return total
+
+
+def sum_sequences(grad, size, x_first):
+    rows = grad.shape[0]
+    parts = grad.reshape(size // 4, 2, 2, rows // size, grad.shape[1])
+    if x_first:
+        parts = halve(parts, size, 2, 1)
+        parts = halve(parts, size, 1, 2)
+    else:
+        parts = halve(parts, size, 1, 2)
+        parts = halve(parts, size, 1, 1)
+    return sum_rest(parts, size)
+
+
+def local_pair(
+    dp_size, inputs, grad_out, lengths, rand_blocks, w_query, b_query, w_key, w_value, b_value,
+    w_output, b_output, gain_one, shift_one, w_in, b_in, w_out, b_out, gain_two, shift_two,
+):
+    core = lax.axis_index("mp").astype(jnp.int32)
+    swap = lambda a: lax.ppermute(a, "mp", [(0, 1), (1, 0)])
+    vec = lambda a: a.reshape(1, -1)
+    x = inputs[0]
+    half, width = x.shape
+    x_got = swap(x)
+    rand = jnp.concatenate([rand_blocks[0], swap(rand_blocks[0])], axis=0)
+    sc = jnp.stack([core, lengths[0]])
+    q, k, v, probs, a_own, a_send = attn_fwd(
+        sc, x, x_got, w_query, w_key, w_value, vec(b_query), vec(b_value), rand
+    )
+    a_got = swap(a_send)
+    u_one, first, first_low = proj_norm(
+        sc, a_own, a_got, x, w_output, vec(b_output), vec(gain_one), vec(shift_one)
+    )
+    first_got = swap(first_low)
+    act0, slope0, feed0 = ffn_fwd(first_low, w_in, vec(b_in), w_out, F32)
+    act1, slope1, feed1 = ffn_fwd(first_got, w_in, vec(b_in), w_out, BF16)
+    out, grad_two, grad_feed, gain_two_g, shift_two_g, b_out_g = norm_two(
+        first, feed0, swap(feed1), vec(b_out), vec(gain_two), vec(shift_two), grad_out[0]
+    )
+    gf_got = swap(grad_feed)
+    gh0, part0, bi0 = ffn_bwd(grad_feed, slope0, w_in, w_out, F32)
+    gh1, part1, bi1 = ffn_bwd(gf_got, slope1, w_in, w_out, BF16)
+    part_got = swap(part1)
+    w_out_g = ffn_weights(grad_feed, gf_got, act0, act1)
+    w_in_g = ffn_weights(first_low, first_got, gh0, gh1)
+    gsum, gb, ga0, ga1, gain_one_g, shift_one_g, b_output_g = norm_one_back(
+        sc, grad_two, part0, part_got, u_one, vec(gain_one), w_output
+    )
+    ga_got = swap(ga1)
+    wo_keep, wo_send = w_output_grad(sc, a_own, a_got, gb)
+    w_output_g = (wo_keep + swap(wo_send).astype(F32)).astype(BF16)
+    wqkv_g, bq_g, bv_g, ig_own, ig_send = attn_bwd(
+        sc, x, x_got, w_query, w_key, w_value, q, k, v, probs, a_own, a_send, ga0, ga_got
+    )
+    input_grad = gsum + (ig_own + swap(ig_send).astype(F32))
+
+    def spread(part, total):
+        return lax.dynamic_update_slice(
+            jnp.zeros((1, total), F32), part, (jnp.int32(0), core * part.shape[1])
+        )
+
+    ff_all = 2 * w_in.shape[1]
+    vectors = [
+        spread(bq_g, width), spread(bv_g, width), b_output_g, gain_one_g, shift_one_g, b_out_g,
+        gain_two_g, shift_two_g, spread(bi0 + bi1, ff_all),
+    ]
+    table = jnp.concatenate([a.reshape(dp_size, -1) for a in vectors], axis=1)
+    table = table + swap(table)
+    rows = width // dp_size
+    lanes = 2 * HD
+    table = jnp.pad(table, ((0, 0), (0, rows * lanes - table.shape[1])))
+    table = table.astype(BF16).reshape(width, lanes)
+
+    cut = 2 * width // 2
+    late = jnp.concatenate([wqkv_g[:, cut:], w_output_g, table], axis=1)
+    out_part = sum_sequences(w_out_g, dp_size, True)
+    in_part = sum_sequences(w_in_g, dp_size, False)
+    early_part = sum_sequences(wqkv_g[:, :cut], dp_size, True)
+    late_part = sum_sequences(late, dp_size, False)
+
+    qkv = jnp.concatenate([early_part, late_part[:, : wqkv_g.shape[1] - cut]], axis=1)
+    qkv = qkv.reshape(rows, HEADS // 4, 3, 2 * HD)
+    wq_p, wk_p, wv_p = (qkv[:, :, i].reshape(rows, width // 2) for i in range(3))
+    wo_p = late_part[:, wqkv_g.shape[1] - cut :][:, : width // 2]
+    flat = late_part[:, wqkv_g.shape[1] - cut + width // 2 :].reshape(-1)
+    vs = [flat[i * rows : (i + 1) * rows] for i in range(8)]
+    bi_p = flat[8 * rows : 8 * rows + ff_all // dp_size]
+    return (
+        out[None], input_grad[None], wq_p, vs[0], wk_p, wv_p, vs[1], wo_p, vs[2], vs[3], vs[4],
+        in_part, bi_p, out_part, vs[5], vs[6], vs[7],
+    )
 
 
 def layer_norm(features, norm_gain, norm_shift):
@@ -593,4 +1195,9 @@
         P("dp"),
         P("dp"),
     )
-    return jax.shard_map(local, mesh=mesh, in_specs=in_specs, out_specs=out_specs, check_vma=False)
+    sizes = dict(mesh.shape)
+    if sizes["mp"] == 2 and sizes["dp"] % 4 == 0:
+        local_fn = functools.partial(local_pair, sizes["dp"])
+    else:
+        local_fn = local
+    return jax.shard_map(local_fn, mesh=mesh, in_specs=in_specs, out_specs=out_specs, check_vma=False)

time: 1140 us -> 242 us (0.21)
  waiting for transfers between devices: 532 us -> 18.9 us
  local copies, waits for them, and re-layouts: 271 us -> 45.2 us
  matrix products: 137 us -> 0 us
  Pallas kernels: 0 us -> 114 us
  blocking collectives: 80.1 us -> 0 us
  other arithmetic: 93.3 us -> 20.9 us
  starting transfers between devices: 1.15 us -> 39.3 us
  between operations: 17.3 us -> 1.74 us
    reduce_scatter x10 -> x0, waiting for transfers between devices: 318 us -> none  [the longest x1 132 us: local(): lax.psum_scatter(w_in_grad.astype(jnp.bfloat16), 'dp', scatter_dimension=...]
    unnamed x22 -> x0, waiting for transfers between devices: 175 us -> none
    dot_general x31 -> x0, matrix products: 137 us -> none  [the longest x1 9.78 us: attend_backward(): jnp.einsum('nqhd,nkhd->nhqk', grad_heads, value_slots, preferred_element_...]
    reshape x15 -> x20, local copies, waits for them, and re-layouts: 136 us -> 16.3 us  [the longest x9 9.58 us: local_pair(): table = jnp.concatenate([a.reshape(dp_size, -1) for a in vectors], axis=1)]
    pallas_call x0 -> x12, Pallas kernels: none -> 114 us  [the longest x1 26.8 us: attn_bwd(): pl.pallas_call(attn_bwd_body, grid_spec=pltpu.PrefetchScalarGridSpec(num_...]
    unnamed x1 -> x0, blocking collectives: 77.1 us -> none
    scatter-add x2 -> x0, other arithmetic: 40 us -> none  [the longest x1 20.2 us: attend_backward(): jax.ops.segment_sum(grad_key_slots.reshape(-1, slot_width), flat_ids, num...]
    ppermute x0 -> x31, starting transfers between devices: none -> 39.3 us  [the longest x12 25.5 us: sum_rest(): got = lax.ppermute(pick(parts, (high + s) % groups, 0), 'dp', perm)]
  transfers between devices with their start and end apart: 18 -> 31, of which waited for: 14 -> 7; matrix products, arithmetic and copies ran while one was open for 28% -> 23% of each run, Pallas kernels for 0% -> 27%
where the time goes in v1:
time: 242 us; the launch traced here: 240 us
  Pallas kernels  114 us (47%)
  local copies, waits for them, and re-layouts  45.2 us (19%)
  starting transfers between devices  39.3 us (16%)
  other arithmetic  20.9 us (9%)
  waiting for transfers between devices  18.9 us (8%)
    pallas_call x1, Pallas kernels, attn_bwd(): pl.pallas_call(attn_bwd_body, grid_spec=pltpu.PrefetchScalarGridSpec(num_...  26.8 us
    pallas_call x1, Pallas kernels, attn_fwd(): pl.pallas_call(attn_fwd_body, grid_spec=pltpu.PrefetchScalarGridSpec(num_...  26 us
    ppermute x12, starting transfers between devices, sum_rest(): got = lax.ppermute(pick(parts, (high + s) % groups, 0), 'dp', perm)  25.5 us
    pallas_call x2, Pallas kernels, ffn_fwd(): pl.pallas_call(ffn_fwd_body, grid=(rows // t,), in_specs=[row(width), who...  14.2 us
    pallas_call x2, Pallas kernels, ffn_bwd(): pl.pallas_call(ffn_bwd_body, grid=(rows // t,), in_specs=[row(width), row...  14.2 us
    pallas_call x2, Pallas kernels, ffn_weights(): pl.pallas_call(ffn_weights_body, grid=(width // t,), in_specs=[lhs, lhs,...  12.6 us
    ppermute x8, starting transfers between devices, halve(): got = lax.ppermute(pick(parts, 1 - mine, bit_axis), 'dp', pairs)  11 us
    ppermute x12, waiting for transfers between devices, sum_rest(): got = lax.ppermute(pick(parts, (high + s) % groups, 0), 'dp', perm)  9.86 us
  transfers between devices with their start and end apart: 31, of which 7 were waited for; matrix products, arithmetic and copies ran while one was open for 23% of the time, Pallas kernels for 27%

profile of v1, /device:TPU:0, one launch (start us, length us, event | category | flops | bytes accessed | tf_op | source)
XLA Modules:
  0.0 240.3 jit_solution(5779507230855383933)
XLA Ops:
  7.3 26.0 %attn_fwd.1 = (bf16[1024,384]{1,0:T(8,128)(2,1)}, bf16[1024,384]{1,0:T(8,128)(2,1)}, bf16[1024,384]{1,0:T(8,128)(2,1)}, bf16[6,1024,1024]{2,1,0:T(8,128)(2,1)}, ...) custom-call(s32[2]{0:T(128)} %pad_add_fusion.1.sc, bf16[512,768]{1,0:T(8,128)(2,1)} %bitcast.124, ...), custom_call_target="tpu_custom_call" | custom-call | flops 20000000000 | bytes 20000000 | tf_op jit(solution)/shard_map/attn_fwd/pallas_call | solution.py:117
  36.4 5.2 %proj_norm.1 = (f32[512,768]{1,0:T(8,128)}, f32[512,768]{1,0:T(8,128)}, bf16[512,768]{1,0:T(8,128)(2,1)}) custom-call(s32[2]{0:T(128)} %pad_add_fusion.1.sc, bf16[512,384]{1,0:T(8,128)(2,1)} %get-tuple-element.58.a0.ao, bf16[512,384]{1,0:T(8,128)(2,1)} %copy-done.2, bf16[512,768]{1,0:T(8,128)(2,1)} %bitcast.125, bf16[768,768]{1,0:T(8,128)(2,1)} %w1.3, ...), custom_call_target="tpu_custom_call" | custom-call | flops 603979776 | bytes 8000000 | tf_op jit(solution)/shard_map/proj_norm/pallas_call | solution.py:268
  45.0 7.0 %ffn_fwd.3 = (bf16[512,1536]{1,0:T(8,128)(2,1)}, bf16[512,1536]{1,0:T(8,128)(2,1)}, bf16[512,768]{1,0:T(8,128)(2,1)}) custom-call(bf16[512,768]{1,0:T(8,128)(2,1)} %copy-done.21, bf16[768,1536]{1,0:T(8,128)(2,1)} %w_in.7, bf16[1,1536]{1,0:T(2,128)(2,1)} %reshape.140.b_in, bf16[768,1536]{1,0:T(8,128)(2,1)} %w_out.7), custom_call_target="tpu_custom_call" | custom-call | flops 2415919104 | bytes 8000000 | tf_op jit(solution)/shard_map/ffn_fwd/pallas_call | solution.py:395
  53.9 7.2 %ffn_fwd.2 = (bf16[512,1536]{1,0:T(8,128)(2,1)}, bf16[512,1536]{1,0:T(8,128)(2,1)}, f32[512,768]{1,0:T(8,128)}) custom-call(bf16[512,768]{1,0:T(8,128)(2,1)} %get-tuple-element.61.x.a0, bf16[768,1536]{1,0:T(8,128)(2,1)} %w_in.7, bf16[1,1536]{1,0:T(2,128)(2,1)} %reshape.140.b_in, bf16[768,1536]{1,0:T(8,128)(2,1)} %w_out.7), custom_call_target="tpu_custom_call" | custom-call | flops 2415919104 | bytes 8000000 | tf_op jit(solution)/shard_map/ffn_fwd/pallas_call | solution.py:395
  62.1 4.4 %norm_two.1 = (bf16[512,768]{1,0:T(8,128)(2,1)}, f32[512,768]{1,0:T(8,128)}, bf16[512,768]{1,0:T(8,128)(2,1)}, f32[1,768]{1,0:T(1,128)}, f32[1,768]{1,0:T(1,128)}, /*index=5*/f32[1,768]{1,0:T(1,128)}) custom-call(f32[512,768]{1,0:T(8,128)} %get-tuple-element.60.first, f32[512,768]{1,0:T(8,128)} %get-tuple-element.62.f0, bf16[512,768]{1,0:T(8,128)(2,1)} %copy-done.8, ...), custom_call_target="tpu_custom_call" | custom-call | flops 11796480 | bytes 8000000 | tf_op jit(solution)/shard_map/norm_two/pallas_call | solution.py:435
  70.9 7.1 %ffn_bwd.2 = (bf16[512,1536]{1,0:T(8,128)(2,1)}, f32[512,768]{1,0:T(8,128)}, f32[1,1536]{1,0:T(1,128)}) custom-call(bf16[512,768]{1,0:T(8,128)(2,1)} %get-tuple-element.66.gf.a0, bf16[512,1536]{1,0:T(8,128)(2,1)} %get-tuple-element.67.slope, bf16[768,1536]{1,0:T(8,128)(2,1)} %w_in.7, bf16[768,1536]{1,0:T(8,128)(2,1)} %w_out.7), custom_call_target="tpu_custom_call" | custom-call | flops 2415919104 | bytes 8000000 | tf_op jit(solution)/shard_map/ffn_bwd/pallas_call | solution.py:470
  78.9 7.1 %ffn_bwd.3 = (bf16[512,1536]{1,0:T(8,128)(2,1)}, bf16[512,768]{1,0:T(8,128)(2,1)}, f32[1,1536]{1,0:T(1,128)}) custom-call(bf16[512,768]{1,0:T(8,128)(2,1)} %copy-done.22, bf16[512,1536]{1,0:T(8,128)(2,1)} %get-tuple-element.69.slope, bf16[768,1536]{1,0:T(8,128)(2,1)} %w_in.7, bf16[768,1536]{1,0:T(8,128)(2,1)} %w_out.7), custom_call_target="tpu_custom_call" | custom-call | flops 2415919104 | bytes 8000000 | tf_op jit(solution)/shard_map/ffn_bwd/pallas_call | solution.py:470
  86.2 6.3 %ffn_weights.3 = bf16[768,1536]{1,0:T(8,128)(2,1)} custom-call(bf16[512,768]{1,0:T(8,128)(2,1)} %get-tuple-element.66.gf.a0, bf16[512,768]{1,0:T(8,128)(2,1)} %copy-done.22, bf16[512,1536]{1,0:T(8,128)(2,1)} %get-tuple-element.97.b0, bf16[512,1536]{1,0:T(8,128)(2,1)} %get-tuple-element.98.b1), custom_call_target="tpu_custom_call" | custom-call | flops 2415919104 | bytes 8000000 | tf_op jit(solution)/shard_map/ffn_weights/pallas_call | solution.py:492
  92.5 1.8 constant_dynamic-slice_fusion.1
  95.4 2.8 %collective-permute-start.26 = (bf16[4,2,48,1536]{3,2,0,1:T(8,128)(2,1)}, bf16[4,2,48,1536]{3,2,0,1:T(8,128)(2,1)S(1)}, u32[]{:S(2)}, u32[]{:S(2)}) collective-permute-start(bf16[4,2,48,1536]{3,2,0,1:T(8,128)(2,1)} %bitcast.112), channel_id=1, source_target_pairs={{0,2},{2,0},{4,6},{6,4},{8,10},{10,8},{12,14},{14,12},{16,18},{18,... | collective-permute-start | bytes 3538952 | tf_op jit(solution)/shard_map/ppermute | solution.py:512
  98.2 6.3 %ffn_weights.2 = bf16[768,1536]{1,0:T(8,128)(2,1)} custom-call(bf16[512,768]{1,0:T(8,128)(2,1)} %get-tuple-element.61.x.a0, bf16[512,768]{1,0:T(8,128)(2,1)} %copy-done.21, bf16[512,1536]{1,0:T(8,128)(2,1)} %get-tuple-element.95.b0, bf16[512,1536]{1,0:T(8,128)(2,1)} %get-tuple-element.96.b1), custom_call_target="tpu_custom_call" | custom-call | flops 2415919104 | bytes 8000000 | tf_op jit(solution)/shard_map/ffn_weights/pallas_call | solution.py:492
  104.5 1.8 constant_dynamic-slice_fusion.3
  109.9 6.6 %norm_one_back.1 = (f32[512,768]{1,0:T(8,128)}, bf16[512,768]{1,0:T(8,128)(2,1)}, bf16[512,384]{1,0:T(8,128)(2,1)}, bf16[512,384]{1,0:T(8,128)(2,1)}, f32[1,768]...) custom-call(s32[2]{0:T(128)} %pad_add_fusion.1.sc, f32[512,768]{1,0:T(8,128)} %get-tuple-element.65.gtwo, ...), custom_call_target="tpu_custom_call" | custom-call | flops 603979776 | bytes 10000000 | tf_op jit(solution)/shard_map/norm_one_back/pallas_call | solution.py:319
  119.2 4.3 %w_output_grad.1 = (f32[768,384]{1,0:T(8,128)}, bf16[768,384]{1,0:T(8,128)(2,1)}) custom-call(s32[2]{0:T(128)} %pad_add_fusion.1.sc, bf16[512,384]{1,0:T(8,128)(2,1)} %get-tuple-element.58.a0.ao, bf16[512,384]{1,0:T(8,128)(2,1)} %copy-done.2, bf16[512,768]{1,0:T(8,128)(2,1)} %get-tuple-element.82.keep_cols.send_cols, ...), custom_call_target="tpu_custom_call" | custom-call | flops 603979776 | bytes 5000000 | tf_op jit(solution)/shard_map/w_output_grad/pallas_call | solution.py:355
  131.9 26.8 %attn_bwd.1 = (bf16[768,1152]{1,0:T(8,128)(2,1)}, f32[1,384]{1,0:T(1,128)}, f32[1,384]{1,0:T(1,128)}, f32[512,768]{1,0:T(8,128)}, bf16[512,768]{1,0:T(8,128)(2,1)}) custom-call(s32[2]{0:T(128)} %pad_add_fusion.1.sc, bf16[512,768]{1,0:T(8,128)(2,1)} %bitcast.126, bf16[512,768]{1,0:T(8,128)(2,1)} %copy-done.20, bf16[768,768]{1,0:T(8,128)(2,1)} %wq.3, ...), custom_call_target="tpu_custom_call" | custom-call | flops 40000000000 | bytes 20000000 | tf_op jit(solution)/shard_map/attn_bwd/pallas_call | solution.py:218
  158.7 2.4 %slice.53 = bf16[768,768]{1,0:T(8,128)(2,1)} slice(bf16[768,1152]{1,0:T(8,128)(2,1)} %get-tuple-element.81), slice={[0:768], [0:768]} | slice | bytes 2359296 | tf_op jit(solution)/shard_map/slice | solution.py:603
  161.1 1.9 slice.54
  179.4 2.1 collective-permute-start.9
  186.2 1.8 collective-permute-start.28
  188.0 2.6 %collective-permute-start.29 = (bf16[48,1536]{1,0:T(8,128)(2,1)S(1)}, bf16[48,1536]{1,0:T(8,128)(2,1)S(1)}, u32[]{:S(2)}, u32[]{:S(2)}) collective-permute-start(bf16[48,1536]{1,0:T(8,128)(2,1)S(1)} %get-tuple-element.112), channel_id=1, source_target_pairs={{0,16},{2,18},{4,20},{6,22},{8,24},{10,26},{12,28},{14,30},{16,0},... | collective-permute-start | bytes 442376 | tf_op jit(solution)/shard_map/ppermute | solution.py:523
  191.8 5.4 %collective-permute-done.9 = bf16[4,2,48,768]{3,2,0,1:T(8,128)(2,1)S(1)} collective-permute-done((bf16[4,2,48,768]{3,2,0,1:T(8,128)(2,1)S(1)}, bf16[4,2,48,768]{3,2,0,1:T(8,128)(2,1)S(1)}, u32[]{:S(2)}, u32[]{:S(2)}) %collective-permute-start.9) | collective-permute-done | bytes 589856 | tf_op jit(solution)/shard_map/ppermute | solution.py:512
  197.3 3.6 %collective-permute-start.30 = (bf16[48,1536]{1,0:T(8,128)(2,1)S(1)}, bf16[48,1536]{1,0:T(8,128)(2,1)S(1)}, u32[]{:S(2)}, u32[]{:S(2)}) collective-permute-start(bf16[48,1536]{1,0:T(8,128)(2,1)S(1)} %get-tuple-element.111), channel_id=1, source_target_pairs={{0,24},{2,26},{4,28},{6,30},{8,0},{10,2},{12,4},{14,6},{16,8},{18,... | collective-permute-start | bytes 442376 | tf_op jit(solution)/shard_map/ppermute | solution.py:523
  202.2 3.0 %collective-permute-done.30 = bf16[48,1536]{1,0:T(8,128)(2,1)S(1)} collective-permute-done((bf16[48,1536]{1,0:T(8,128)(2,1)S(1)}, bf16[48,1536]{1,0:T(8,128)(2,1)S(1)}, u32[]{:S(2)}, u32[]{:S(2)}) %collective-permute-start.30) | collective-permute-done | bytes 147488 | tf_op jit(solution)/shard_map/ppermute | solution.py:523
  205.2 4.3 %collective-permute-start.25 = (bf16[48,1536]{1,0:T(8,128)(2,1)S(1)}, bf16[48,1536]{1,0:T(8,128)(2,1)S(1)}, u32[]{:S(2)}, u32[]{:S(2)}) collective-permute-start(bf16[48,1536]{1,0:T(8,128)(2,1)S(1)} %get-tuple-element.114), channel_id=1, source_target_pairs={{0,24},{2,26},{4,28},{6,30},{8,0},{10,2},{12,4},{14,6},{16,8},{18,... | collective-permute-start | bytes 442376 | tf_op jit(solution)/shard_map/ppermute | solution.py:523
  211.9 2.2 collective-permute-done.24
  217.6 3.4 %collective-permute-start.11 = (bf16[48,768]{1,0:T(8,128)(2,1)S(1)}, bf16[48,768]{1,0:T(8,128)(2,1)S(1)}, u32[]{:S(2)}, u32[]{:S(2)}) collective-permute-start(bf16[48,768]{1,0:T(8,128)(2,1)S(1)} %get-tuple-element.119), channel_id=1, source_target_pairs={{0,8},{2,10},{4,12},{6,14},{8,16},{10,18},{12,20},{14,22},{16,24},... | collective-permute-start | bytes 221192 | tf_op jit(solution)/shard_map/ppermute | solution.py:523
  221.0 1.9 collective-permute-start.12
  223.4 1.9 collective-permute-done.17
  225.5 3.8 %collective-permute-start.18 = (bf16[48,896]{1,0:T(8,128)(2,1)S(1)}, bf16[48,896]{1,0:T(8,128)(2,1)S(1)}, u32[]{:S(2)}, u32[]{:S(2)}) collective-permute-start(bf16[48,896]{1,0:T(8,128)(2,1)S(1)} %get-tuple-element.116), channel_id=1, source_target_pairs={{0,8},{2,10},{4,12},{6,14},{8,16},{10,18},{12,20},{14,22},{16,24},... | collective-permute-start | bytes 258056 | tf_op jit(solution)/shard_map/ppermute | solution.py:523
  229.3 1.7 collective-permute-start.19
  231.8 1.9 collective-permute-done.18
  233.7 2.7 %collective-permute-done.19 = bf16[48,896]{1,0:T(8,128)(2,1)S(1)} collective-permute-done((bf16[48,896]{1,0:T(8,128)(2,1)S(1)}, bf16[48,896]{1,0:T(8,128)(2,1)S(1)}, u32[]{:S(2)}, u32[]{:S(2)}) %collective-permute-start.19) | collective-permute-done | bytes 86048 | tf_op jit(solution)/shard_map/ppermute | solution.py:523
  (174 shorter events, 71.1 us)
Async XLA Ops:
  0.7 5.8 %collective-permute-start = (bf16[512,768]{1,0:T(8,128)(2,1)}, bf16[512,768]{1,0:T(8,128)(2,1)S(1)}, u32[]{:S(2)}, u32[]{:S(2)}) collective-permute-start(bf16[512,768]{1,0:T(8,128)(2,1)} %bitcast.123), channel_id=1, source_target_pairs={{0,1},{1,0},{2,3},{3,2},{4,5},{5,4},{6,7},{7,6},{8,9},{9,8},{10,11... | collective-permute-start | bytes 2359304 | tf_op jit(solution)/shard_map/ppermute | solution.py:545
  1.9 3.8 %collective-permute-start.1 = (s32[8,3]{0,1:T(4,128)S(1)}, s32[8,3]{0,1:T(4,128)S(1)}, u32[]{:S(2)}, u32[]{:S(2)}) collective-permute-start(s32[8,3]{0,1:T(4,128)S(1)} %bitcast.135), channel_id=1, source_target_pairs={{0,1},{1,0},{2,3},{3,2},{4,5},{5,4},{6,7},{7,6},{8,9},{9,8},{10,11... | collective-permute-start | bytes 296 | tf_op jit(solution)/shard_map/ppermute | solution.py:545
  6.4 28.6 %copy-start.15 = (bf16[768]{0:T(1024)(128)(2,1)S(1)}, bf16[768]{0:T(1024)(128)(2,1)}, u32[]{:S(2)}) copy-start(bf16[768]{0:T(1024)(128)(2,1)} %param.31) | copy-start | bytes 4612
  33.3 2.3 collective-permute-start.2
  41.6 2.5 %collective-permute-start.3 = (bf16[512,768]{1,0:T(8,128)(2,1)}, bf16[512,768]{1,0:T(8,128)(2,1)S(1)}, u32[]{:S(2)}, u32[]{:S(2)}) collective-permute-start(bf16[512,768]{1,0:T(8,128)(2,1)} %get-tuple-element.61.x.a0), channel_id=1, source_target_pairs={{0,1},{1,0},{2,3},{3,2},{4,5},{5,4},{6,7},{7,6},{8,9},{9,8},{10,11... | collective-permute-start | bytes 2359304 | tf_op jit(solution)/shard_map/ppermute | solution.py:545
  52.0 9.1 %collective-permute-start.4 = (bf16[512,768]{1,0:T(8,128)(2,1)}, bf16[512,768]{1,0:T(8,128)(2,1)S(1)}, u32[]{:S(2)}, u32[]{:S(2)}) collective-permute-start(bf16[512,768]{1,0:T(8,128)(2,1)} %get-tuple-element.63), channel_id=1, source_target_pairs={{0,1},{1,0},{2,3},{3,2},{4,5},{5,4},{6,7},{7,6},{8,9},{9,8},{10,11... | collective-permute-start | bytes 2359304 | tf_op jit(solution)/shard_map/ppermute | solution.py:545
  66.4 11.6 %collective-permute-start.5 = (bf16[512,768]{1,0:T(8,128)(2,1)}, bf16[512,768]{1,0:T(8,128)(2,1)S(1)}, u32[]{:S(2)}, u32[]{:S(2)}) collective-permute-start(bf16[512,768]{1,0:T(8,128)(2,1)} %get-tuple-element.66.gf.a0), channel_id=1, source_target_pairs={{0,1},{1,0},{2,3},{3,2},{4,5},{5,4},{6,7},{7,6},{8,9},{9,8},{10,11... | collective-permute-start | bytes 2359304 | tf_op jit(solution)/shard_map/ppermute | solution.py:545
  86.0 23.0 %collective-permute-start.6 = (bf16[512,768]{1,0:T(8,128)(2,1)}, bf16[512,768]{1,0:T(8,128)(2,1)S(1)}, u32[]{:S(2)}, u32[]{:S(2)}) collective-permute-start(bf16[512,768]{1,0:T(8,128)(2,1)} %get-tuple-element.70), channel_id=1, source_target_pairs={{0,1},{1,0},{2,3},{3,2},{4,5},{5,4},{6,7},{7,6},{8,9},{9,8},{10,11... | collective-permute-start | bytes 2359304 | tf_op jit(solution)/shard_map/ppermute | solution.py:545
  95.4 67.6 %collective-permute-start.26 = (bf16[4,2,48,1536]{3,2,0,1:T(8,128)(2,1)}, bf16[4,2,48,1536]{3,2,0,1:T(8,128)(2,1)S(1)}, u32[]{:S(2)}, u32[]{:S(2)}) collective-permute-start(bf16[4,2,48,1536]{3,2,0,1:T(8,128)(2,1)} %bitcast.112), channel_id=1, source_target_pairs={{0,2},{2,0},{4,6},{6,4},{8,10},{10,8},{12,14},{14,12},{16,18},{18,... | collective-permute-start | bytes 3538952 | tf_op jit(solution)/shard_map/ppermute | solution.py:512
  107.4 59.6 %collective-permute-start.21 = (bf16[4,2,48,1536]{3,2,0,1:T(8,128)(2,1)}, bf16[4,2,48,1536]{3,2,0,1:T(8,128)(2,1)}, u32[]{:S(2)}, u32[]{:S(2)}) collective-permute-start(bf16[4,2,48,1536]{3,2,0,1:T(8,128)(2,1)} %bitcast.113), channel_id=1, source_target_pairs={{0,4},{2,6},{4,0},{6,2},{8,12},{10,14},{12,8},{14,10},{16,20},{18,... | collective-permute-start | bytes 3538952 | tf_op jit(solution)/shard_map/ppermute | solution.py:512
  116.5 15.4 %collective-permute-start.7 = (bf16[512,384]{1,0:T(8,128)(2,1)}, bf16[512,384]{1,0:T(8,128)(2,1)}, u32[]{:S(2)}, u32[]{:S(2)}) collective-permute-start(bf16[512,384]{1,0:T(8,128)(2,1)} %get-tuple-element.78), channel_id=1, source_target_pairs={{0,1},{1,0},{2,3},{3,2},{4,5},{5,4},{6,7},{7,6},{8,9},{9,8},{10,11... | collective-permute-start | bytes 1179656 | tf_op jit(solution)/shard_map/ppermute | solution.py:545
  123.4 58.3 %collective-permute-start.14 = (bf16[768,384]{1,0:T(8,128)(2,1)}, bf16[768,384]{1,0:T(8,128)(2,1)}, u32[]{:S(2)}, u32[]{:S(2)}) collective-permute-start(bf16[768,384]{1,0:T(8,128)(2,1)} %get-tuple-element.84), channel_id=1, source_target_pairs={{0,1},{1,0},{2,3},{3,2},{4,5},{5,4},{6,7},{7,6},{8,9},{9,8},{10,11... | collective-permute-start | bytes 1769480 | tf_op jit(solution)/shard_map/ppermute | solution.py:545
  166.5 18.4 %collective-permute-start.27 = (bf16[4,48,1536]{2,1,0:T(8,128)(2,1)}, bf16[4,48,1536]{2,1,0:T(8,128)(2,1)}, u32[]{:S(2)}, u32[]{:S(2)}) collective-permute-start(bf16[4,48,1536]{2,1,0:T(8,128)(2,1)} %dynamic-slice_bitcast_fusion), channel_id=1, source_target_pairs={{0,4},{2,6},{4,0},{6,2},{8,12},{10,14},{12,8},{14,10},{16,20},{18,... | collective-permute-start | bytes 1769480 | tf_op jit(solution)/shard_map/ppermute | solution.py:512
  169.5 18.6 %collective-permute-start.22 = (bf16[4,48,1536]{2,1,0:T(8,128)(2,1)}, bf16[4,48,1536]{2,1,0:T(8,128)(2,1)}, u32[]{:S(2)}, u32[]{:S(2)}) collective-permute-start(bf16[4,48,1536]{2,1,0:T(8,128)(2,1)} %dynamic-slice_bitcast_fusion.1), channel_id=1, source_target_pairs={{0,2},{2,0},{4,6},{6,4},{8,10},{10,8},{12,14},{14,12},{16,18},{18,... | collective-permute-start | bytes 1769480 | tf_op jit(solution)/shard_map/ppermute | solution.py:512
  179.2 2.2 collective-permute-start.15
  179.4 17.9 %collective-permute-start.9 = (bf16[4,2,48,768]{3,2,0,1:T(8,128)(2,1)S(1)}, bf16[4,2,48,768]{3,2,0,1:T(8,128)(2,1)S(1)}, u32[]{:S(2)}, u32[]{:S(2)}) collective-permute-start(bf16[4,2,48,768]{3,2,0,1:T(8,128)(2,1)S(1)} %bitcast.130), channel_id=1, source_target_pairs={{0,2},{2,0},{4,6},{6,4},{8,10},{10,8},{12,14},{14,12},{16,18},{18,... | collective-permute-start | bytes 1769480 | tf_op jit(solution)/shard_map/ppermute | solution.py:512
  181.5 33.4 %collective-permute-start.8 = (bf16[512,768]{1,0:T(8,128)(2,1)S(1)}, bf16[512,768]{1,0:T(8,128)(2,1)S(1)}, u32[]{:S(2)}, u32[]{:S(2)}) collective-permute-start(bf16[512,768]{1,0:T(8,128)(2,1)S(1)} %copy-done.23), channel_id=1, source_target_pairs={{0,1},{1,0},{2,3},{3,2},{4,5},{5,4},{6,7},{7,6},{8,9},{9,8},{10,11... | collective-permute-start | bytes 2359304 | tf_op jit(solution)/shard_map/ppermute | solution.py:545
  183.3 32.9 %collective-permute-start.16 = (bf16[4,2,48,896]{3,2,0,1:T(8,128)(2,1)S(1)}, bf16[4,2,48,896]{3,2,0,1:T(8,128)(2,1)S(1)}, u32[]{:S(2)}, u32[]{:S(2)}) collective-permute-start(bf16[4,2,48,896]{3,2,0,1:T(8,128)(2,1)S(1)} %bitcast.129), channel_id=1, source_target_pairs={{0,4},{2,6},{4,0},{6,2},{8,12},{10,14},{12,8},{14,10},{16,20},{18,... | collective-permute-start | bytes 2064392 | tf_op jit(solution)/shard_map/ppermute | solution.py:512
  186.2 14.9 %collective-permute-start.28 = (bf16[48,1536]{1,0:T(8,128)(2,1)S(1)}, bf16[48,1536]{1,0:T(8,128)(2,1)S(1)}, u32[]{:S(2)}, u32[]{:S(2)}) collective-permute-start(bf16[48,1536]{1,0:T(8,128)(2,1)S(1)} %get-tuple-element.110), channel_id=1, source_target_pairs={{0,8},{2,10},{4,12},{6,14},{8,16},{10,18},{12,20},{14,22},{16,24},... | collective-permute-start | bytes 442376 | tf_op jit(solution)/shard_map/ppermute | solution.py:523
  188.0 13.2 %collective-permute-start.29 = (bf16[48,1536]{1,0:T(8,128)(2,1)S(1)}, bf16[48,1536]{1,0:T(8,128)(2,1)S(1)}, u32[]{:S(2)}, u32[]{:S(2)}) collective-permute-start(bf16[48,1536]{1,0:T(8,128)(2,1)S(1)} %get-tuple-element.112), channel_id=1, source_target_pairs={{0,16},{2,18},{4,20},{6,22},{8,24},{10,26},{12,28},{14,30},{16,0},... | collective-permute-start | bytes 442376 | tf_op jit(solution)/shard_map/ppermute | solution.py:523
  197.3 8.0 %collective-permute-start.30 = (bf16[48,1536]{1,0:T(8,128)(2,1)S(1)}, bf16[48,1536]{1,0:T(8,128)(2,1)S(1)}, u32[]{:S(2)}, u32[]{:S(2)}) collective-permute-start(bf16[48,1536]{1,0:T(8,128)(2,1)S(1)} %get-tuple-element.111), channel_id=1, source_target_pairs={{0,24},{2,26},{4,28},{6,30},{8,0},{10,2},{12,4},{14,6},{16,8},{18,... | collective-permute-start | bytes 442376 | tf_op jit(solution)/shard_map/ppermute | solution.py:523
  201.1 9.2 %collective-permute-start.23 = (bf16[48,1536]{1,0:T(8,128)(2,1)S(1)}, bf16[48,1536]{1,0:T(8,128)(2,1)S(1)}, u32[]{:S(2)}, u32[]{:S(2)}) collective-permute-start(bf16[48,1536]{1,0:T(8,128)(2,1)S(1)} %get-tuple-element.113), channel_id=1, source_target_pairs={{0,8},{2,10},{4,12},{6,14},{8,16},{10,18},{12,20},{14,22},{16,24},... | collective-permute-start | bytes 442376 | tf_op jit(solution)/shard_map/ppermute | solution.py:523
  201.2 12.9 %collective-permute-start.24 = (bf16[48,1536]{1,0:T(8,128)(2,1)S(1)}, bf16[48,1536]{1,0:T(8,128)(2,1)S(1)}, u32[]{:S(2)}, u32[]{:S(2)}) collective-permute-start(bf16[48,1536]{1,0:T(8,128)(2,1)S(1)} %get-tuple-element.115), channel_id=1, source_target_pairs={{0,16},{2,18},{4,20},{6,22},{8,24},{10,26},{12,28},{14,30},{16,0},... | collective-permute-start | bytes 442376 | tf_op jit(solution)/shard_map/ppermute | solution.py:523
  205.2 8.9 %collective-permute-start.25 = (bf16[48,1536]{1,0:T(8,128)(2,1)S(1)}, bf16[48,1536]{1,0:T(8,128)(2,1)S(1)}, u32[]{:S(2)}, u32[]{:S(2)}) collective-permute-start(bf16[48,1536]{1,0:T(8,128)(2,1)S(1)} %get-tuple-element.114), channel_id=1, source_target_pairs={{0,24},{2,26},{4,28},{6,30},{8,0},{10,2},{12,4},{14,6},{16,8},{18,... | collective-permute-start | bytes 442376 | tf_op jit(solution)/shard_map/ppermute | solution.py:523
  210.4 7.1 %collective-permute-start.10 = (bf16[4,48,768]{2,1,0:T(8,128)(2,1)S(1)}, bf16[4,48,768]{2,1,0:T(8,128)(2,1)S(1)}, u32[]{:S(2)}, u32[]{:S(2)}) collective-permute-start(bf16[4,48,768]{2,1,0:T(8,128)(2,1)S(1)} %dynamic-slice_bitcast_fusion.3), channel_id=1, source_target_pairs={{0,4},{2,6},{4,0},{6,2},{8,12},{10,14},{12,8},{14,10},{16,20},{18,... | collective-permute-start | bytes 884744 | tf_op jit(solution)/shard_map/ppermute | solution.py:512
  216.5 8.8 %collective-permute-start.17 = (bf16[4,48,896]{2,1,0:T(8,128)(2,1)S(1)}, bf16[4,48,896]{2,1,0:T(8,128)(2,1)S(1)}, u32[]{:S(2)}, u32[]{:S(2)}) collective-permute-start(bf16[4,48,896]{2,1,0:T(8,128)(2,1)S(1)} %dynamic-slice_bitcast_fusion.2), channel_id=1, source_target_pairs={{0,2},{2,0},{4,6},{6,4},{8,10},{10,8},{12,14},{14,12},{16,18},{18,... | collective-permute-start | bytes 1032200 | tf_op jit(solution)/shard_map/ppermute | solution.py:512
  217.6 13.4 %collective-permute-start.11 = (bf16[48,768]{1,0:T(8,128)(2,1)S(1)}, bf16[48,768]{1,0:T(8,128)(2,1)S(1)}, u32[]{:S(2)}, u32[]{:S(2)}) collective-permute-start(bf16[48,768]{1,0:T(8,128)(2,1)S(1)} %get-tuple-element.119), channel_id=1, source_target_pairs={{0,8},{2,10},{4,12},{6,14},{8,16},{10,18},{12,20},{14,22},{16,24},... | collective-permute-start | bytes 221192 | tf_op jit(solution)/shard_map/ppermute | solution.py:523
  221.0 10.7 %collective-permute-start.12 = (bf16[48,768]{1,0:T(8,128)(2,1)S(1)}, bf16[48,768]{1,0:T(8,128)(2,1)S(1)}, u32[]{:S(2)}, u32[]{:S(2)}) collective-permute-start(bf16[48,768]{1,0:T(8,128)(2,1)S(1)} %get-tuple-element.121), channel_id=1, source_target_pairs={{0,16},{2,18},{4,20},{6,22},{8,24},{10,26},{12,28},{14,30},{16,0},... | collective-permute-start | bytes 221192 | tf_op jit(solution)/shard_map/ppermute | solution.py:523
  223.0 8.8 %collective-permute-start.13 = (bf16[48,768]{1,0:T(8,128)(2,1)S(1)}, bf16[48,768]{1,0:T(8,128)(2,1)S(1)}, u32[]{:S(2)}, u32[]{:S(2)}) collective-permute-start(bf16[48,768]{1,0:T(8,128)(2,1)S(1)} %get-tuple-element.120), channel_id=1, source_target_pairs={{0,24},{2,26},{4,28},{6,30},{8,0},{10,2},{12,4},{14,6},{16,8},{18,... | collective-permute-start | bytes 221192 | tf_op jit(solution)/shard_map/ppermute | solution.py:523
  225.5 8.2 %collective-permute-start.18 = (bf16[48,896]{1,0:T(8,128)(2,1)S(1)}, bf16[48,896]{1,0:T(8,128)(2,1)S(1)}, u32[]{:S(2)}, u32[]{:S(2)}) collective-permute-start(bf16[48,896]{1,0:T(8,128)(2,1)S(1)} %get-tuple-element.116), channel_id=1, source_target_pairs={{0,8},{2,10},{4,12},{6,14},{8,16},{10,18},{12,20},{14,22},{16,24},... | collective-permute-start | bytes 258056 | tf_op jit(solution)/shard_map/ppermute | solution.py:523
  229.3 7.1 %collective-permute-start.19 = (bf16[48,896]{1,0:T(8,128)(2,1)S(1)}, bf16[48,896]{1,0:T(8,128)(2,1)S(1)}, u32[]{:S(2)}, u32[]{:S(2)}) collective-permute-start(bf16[48,896]{1,0:T(8,128)(2,1)S(1)} %get-tuple-element.118), channel_id=1, source_target_pairs={{0,16},{2,18},{4,20},{6,22},{8,24},{10,26},{12,28},{14,30},{16,0},... | collective-permute-start | bytes 258056 | tf_op jit(solution)/shard_map/ppermute | solution.py:523
  231.0 5.4 %collective-permute-start.20 = (bf16[48,896]{1,0:T(8,128)(2,1)S(1)}, bf16[48,896]{1,0:T(8,128)(2,1)S(1)}, u32[]{:S(2)}, u32[]{:S(2)}) collective-permute-start(bf16[48,896]{1,0:T(8,128)(2,1)S(1)} %get-tuple-element.117), channel_id=1, source_target_pairs={{0,24},{2,26},{4,28},{6,30},{8,0},{10,2},{12,4},{14,6},{16,8},{18,... | collective-permute-start | bytes 258056 | tf_op jit(solution)/shard_map/ppermute | solution.py:523
  (23 other events, 161.5 us)

commit v2 on v1

--- a/solution.py
+++ b/solution.py
@@ -251,254 +251,288 @@
     )(sc, xo, xt, wq, wk, wv, q, k, v, probs, ao, at, go, gt)
 
 
-def proj_body(sc, a0, a1, x, w0, w1, b, g, s, u_o, f_o, fl_o):
-    u = x[...].astype(F32) + (mm(a0[...], w0[...]) + mm(a1[...], w1[...])) + b[...].astype(F32)
-    n, _ = row_stats(u)
-    first = n * g[...].astype(F32) + s[...].astype(F32)
-    u_o[...] = u
-    f_o[...] = first
-    fl_o[...] = first.astype(BF16)
-
-
-def proj_norm(sc, a_own, a_got, x, w_output, b, g, s):
-    rows, width = x.shape
-    t = 256
-    row = lambda w: pl.BlockSpec((t, w), lambda i, c: (i, 0))
-    vec = pl.BlockSpec((1, width), lambda i, c: (0, 0))
-    return pl.pallas_call(
-        proj_body,
-        grid_spec=pltpu.PrefetchScalarGridSpec(
-            num_scalar_prefetch=1,
-            grid=(rows // t,),
-            in_specs=[
-                row(width // 2),
-                row(width // 2),
-                row(width),
-                pl.BlockSpec((width // 2, width), lambda i, c: (c[0], 0)),
-                pl.BlockSpec((width // 2, width), lambda i, c: (1 - c[0], 0)),
-                vec,
-                vec,
-                vec,
-            ],
-            out_specs=[row(width)] * 3,
-        ),
-        out_shape=[shape((rows, width), F32), shape((rows, width), F32), shape((rows, width), BF16)],
-        compiler_params=params(),
-        cost_estimate=cost(2 * rows * width * width, 8e6),
-        name="proj_norm",
-    )(sc, a_own, a_got, x, w_output, w_output, b, g, s)
-
-
-def norm_one_back_body(sc, gtwo, p0, p1, u, g, w0, w1, gs_o, gb_o, ga0, ga1, gg, sg, bg):
-    e = gtwo[...] + p0[...] + p1[...].astype(F32)
-    n, rs = row_stats(u[...])
-    eg = e * g[...].astype(F32)
-    d = (eg - jnp.mean(eg, -1, keepdims=True) - n * jnp.mean(eg * n, -1, keepdims=True)) * rs
-    low = d.astype(BF16)
-    gs_o[...] = d
-    gb_o[...] = low
-    ga0[...] = mm(low, w0[...], NT).astype(BF16)
-    ga1[...] = mm(low, w1[...], NT).astype(BF16)
-
-    @pl.when(pl.program_id(0) == 0)
-    def _():
-        gg[...] = jnp.zeros_like(gg)
-        sg[...] = jnp.zeros_like(sg)
-        bg[...] = jnp.zeros_like(bg)
-
-    gg[...] += jnp.sum(e * n, 0, keepdims=True)
-    sg[...] += jnp.sum(e, 0, keepdims=True)
-    bg[...] += jnp.sum(low.astype(F32), 0, keepdims=True)
-
-
-def norm_one_back(sc, gtwo, p0, p1, u, g, w_output):
-    rows, width = u.shape
-    t = 256
-    row = lambda w: pl.BlockSpec((t, w), lambda i, c: (i, 0))
-    vec = pl.BlockSpec((1, width), lambda i, c: (0, 0))
-    return pl.pallas_call(
-        norm_one_back_body,
-        grid_spec=pltpu.PrefetchScalarGridSpec(
-            num_scalar_prefetch=1,
-            grid=(rows // t,),
-            in_specs=[row(width)] * 4
-            + [
-                vec,
-                pl.BlockSpec((width // 2, width), lambda i, c: (c[0], 0)),
-                pl.BlockSpec((width // 2, width), lambda i, c: (1 - c[0], 0)),
-            ],
-            out_specs=[row(width)] * 2 + [row(width // 2)] * 2 + [vec] * 3,
-        ),
-        out_shape=[shape((rows, width), F32), shape((rows, width), BF16)]
-        + [shape((rows, width // 2), BF16)] * 2
-        + [shape((1, width), F32)] * 3,
-        compiler_params=params(),
-        cost_estimate=cost(2 * rows * width * width, 10e6),
-        name="norm_one_back",
-    )(sc, gtwo, p0, p1, u, g, w_output, w_output)
-
-
-def w_output_body(sc, a0, a1, keep_cols, send_cols, keep, send):
-    for i, a in enumerate((a0, a1)):
-
-        @pl.when(pl.program_id(0) == i)
-        def _(a=a):
-            keep[...] = mm(a[...], keep_cols[...], TN)
-            send[...] = mm(a[...], send_cols[...], TN).astype(BF16)
-
-
-def w_output_grad(sc, a_own, a_got, gb):
-    rows, width = gb.shape
-    hw = width // 2
-    whole = pl.BlockSpec((rows, hw), lambda i, c: (0, 0))
-    out = pl.BlockSpec((hw, hw), lambda i, c: (i + c[0] - 2 * i * c[0], 0))
-    return pl.pallas_call(
-        w_output_body,
-        grid_spec=pltpu.PrefetchScalarGridSpec(
-            num_scalar_prefetch=1,
-            grid=(2,),
-            in_specs=[
-                whole,
-                whole,
-                pl.BlockSpec((rows, hw), lambda i, c: (0, c[0])),
-                pl.BlockSpec((rows, hw), lambda i, c: (0, 1 - c[0])),
-            ],
-            out_specs=[out, out],
-        ),
-        out_shape=[shape((width, hw), F32), shape((width, hw), BF16)],
-        compiler_params=params(),
-        cost_estimate=cost(2 * rows * width * width, 5e6),
-        name="w_output_grad",
-    )(sc, a_own, a_got, gb, gb)
-
-
-def ffn_fwd_body(x, w_in, b_in, w_out, act_o, slope_o, feed_o):
-    v = mm(x[...], w_in[...]) + b_in[...].astype(F32)
+def partner_copy(src, dst, send, recv, me):
+    return pltpu.make_async_remote_copy(
+        src_ref=src, dst_ref=dst, send_sem=send, recv_sem=recv,
+        device_id={"mp": 1 - me}, device_id_type=pl.DeviceIdType.MESH,
+    )
+
+
+def gelu_and_slope(v):
     k0 = 0.7978845608028654
     k1 = 0.044715
     v2 = v * v
     t = jnp.tanh(v * (k0 + (k0 * k1) * v2))
     hp = 0.5 * t + 0.5
-    act = (v * hp).astype(BF16)
-    slope = hp + (0.5 * v) * (1.0 - t * t) * (k0 + (3 * k0 * k1) * v2)
-    act_o[...] = act
-    slope_o[...] = slope.astype(BF16)
-    feed_o[...] = mm(act, w_out[...], NT).astype(feed_o.dtype)
-
-
-def ffn_fwd(x, w_in, b_in, w_out, dtype):
-    rows, width = x.shape
+    return v * hp, hp + (0.5 * v) * (1.0 - t * t) * (k0 + (3 * k0 * k1) * v2)
+
+
+def norm_back(e, n, rs, gain):
+    eg = e * gain
+    return (eg - jnp.mean(eg, -1, keepdims=True) - n * jnp.mean(eg * n, -1, keepdims=True)) * rs
+
+
+def middle_body(
+    a_own, a_send, x, gout, b_output, gain1, shift1, b_in, b_out, gain2, shift2,
+    w_o_h, w_in_h, w_out_h,
+    out_o, gsum_o, ga_o, gat_o, wout_g, win_g, wo_g, vec_o, bi_o,
+    a_got, fl, feed_s, feed_g, gf, part_s, part_g, gat_s, gb, wo_s, wo_r, vec_s, vec_r, bi_s,
+    w_o, w_in, w_out, act, slope, gh, u_s, first_s, own_s, gtwo_s,
+    load_sem, send_sem, recv_sem,
+):
+    me = lax.axis_index("mp")
+    half, width = x.shape
+    hw = width // 2
+    tile = 256
+    tiles = half // tile
+    barrier = pltpu.get_barrier_semaphore()
+    pl.semaphore_signal(
+        barrier, inc=1, device_id={"mp": 1 - me}, device_id_type=pl.DeviceIdType.MESH
+    )
+    loads = []
+    for i, (src, dst) in enumerate(((w_o_h, w_o), (w_in_h, w_in), (w_out_h, w_out))):
+        loads.append(pltpu.make_async_copy(src, dst, load_sem.at[i]))
+        loads[-1].start()
+    pl.semaphore_wait(barrier, 1)
+
+    def copy(src, dst, i):
+        return partner_copy(src, dst, send_sem.at[i], recv_sem.at[i], me)
+
+    a_copy = copy(a_send, a_got, 0)
+    a_copy.start()
+    loads[0].wait()
+    a_copy.wait_recv()
+
+    def rows(t):
+        return pl.ds(pl.multiple_of(t * tile, tile), tile)
+
+    def fl_copy(t):
+        return copy(fl.at[0, rows(t)], fl.at[1, rows(t)], 1 + t)
+
+    def feed_copy(t):
+        return copy(feed_s.at[rows(t)], feed_g.at[rows(t)], 3 + t)
+
+    def gf_copy(t):
+        return copy(gf.at[0, rows(t)], gf.at[1, rows(t)], 5 + t)
+
+    def part_copy(t):
+        return copy(part_s.at[rows(t)], part_g.at[rows(t)], 7 + t)
+
+    def ga_copy(t):
+        return copy(gat_s.at[rows(t)], gat_o.at[rows(t)], 9 + t)
+
+    own_o = pl.ds(pl.multiple_of(me * hw, hw), hw)
+    got_o = pl.ds(pl.multiple_of((1 - me) * hw, hw), hw)
+
+    def project(t, carry):
+        r = rows(t)
+        u = x[r, :].astype(F32) + (
+            mm(a_own[r, :], w_o[own_o, :]) + mm(a_got[r, :], w_o[got_o, :])
+        ) + b_output[...].astype(F32)
+        n, _ = row_stats(u)
+        first = n * gain1[...].astype(F32) + shift1[...].astype(F32)
+        u_s[r, :] = u
+        first_s[r, :] = first
+        fl[0, r, :] = first.astype(BF16)
+        fl_copy(t).start()
+        return carry
+
+    lax.fori_loop(0, tiles, project, 0)
+    loads[1].wait()
+    loads[2].wait()
+
+    def feed_forward(i, t):
+        r = rows(t)
+        v = mm(fl[i, r, :], w_in[...]) + b_in[...].astype(F32)
+        a, s = gelu_and_slope(v)
+        a = a.astype(BF16)
+        act[i, r, :] = a
+        slope[i, r, :] = s.astype(BF16)
+        return mm(a, w_out[...], NT)
+
+    def forward_own(t, carry):
+        own_s[rows(t), :] = feed_forward(0, t)
+        return carry
+
+    def forward_got(t, carry):
+        fl_copy(t).wait_recv()
+        feed_s[rows(t), :] = feed_forward(1, t).astype(BF16)
+        feed_copy(t).start()
+        return carry
+
+    lax.fori_loop(0, tiles, forward_own, 0)
+    lax.fori_loop(0, tiles, forward_got, 0)
+
+    vec_s[...] = jnp.zeros_like(vec_s)
+
+    def add_vec(i, value):
+        vec_s[i : i + 1, :] += jnp.sum(value, 0, keepdims=True)
+
+    def second_norm(t, carry):
+        r = rows(t)
+        feed_copy(t).wait_recv()
+        u = first_s[r, :] + (own_s[r, :] + feed_g[r, :].astype(F32)) + b_out[...].astype(F32)
+        n, rs = row_stats(u)
+        gain = gain2[...].astype(F32)
+        out_o[r, :] = (n * gain + shift2[...].astype(F32)).astype(BF16)
+        e = gout[r, :].astype(F32)
+        d = norm_back(e, n, rs, gain)
+        low = d.astype(BF16)
+        gtwo_s[r, :] = d
+        gf[0, r, :] = low
+        gf_copy(t).start()
+        add_vec(4, e * n)
+        add_vec(5, e)
+        add_vec(3, low.astype(F32))
+        return carry
+
+    lax.fori_loop(0, tiles, second_norm, 0)
+    bi_s[...] = jnp.zeros_like(bi_s)
+
+    def feed_back(i, t):
+        r = rows(t)
+        g = (mm(gf[i, r, :], w_out[...]) * slope[i, r, :].astype(F32)).astype(BF16)
+        gh[i, r, :] = g
+        bi_s[0:1, :] += jnp.sum(g.astype(F32), 0, keepdims=True)
+        return mm(g, w_in[...], NT)
+
+    def back_own(t, carry):
+        own_s[rows(t), :] = feed_back(0, t)
+        return carry
+
+    def back_got(t, carry):
+        gf_copy(t).wait_recv()
+        part_s[rows(t), :] = feed_back(1, t).astype(BF16)
+        part_copy(t).start()
+        return carry
+
+    lax.fori_loop(0, tiles, back_own, 0)
+    lax.fori_loop(0, tiles, back_got, 0)
+
+    def weights(out, lhs, rhs):
+        def step(j, carry):
+            c = pl.ds(pl.multiple_of(j * tile, tile), tile)
+            out[c, :] = (
+                mm(lhs[0, :, c], rhs[0], TN) + mm(lhs[1, :, c], rhs[1], TN)
+            ).astype(BF16)
+            return carry
+
+        lax.fori_loop(0, width // tile, step, 0)
+
+    weights(wout_g, gf, act)
+    weights(win_g, fl, gh)
+
+    def first_norm(t, carry):
+        r = rows(t)
+        part_copy(t).wait_recv()
+        e = gtwo_s[r, :] + own_s[r, :] + part_g[r, :].astype(F32)
+        n, rs = row_stats(u_s[r, :])
+        d = norm_back(e, n, rs, gain1[...].astype(F32))
+        low = d.astype(BF16)
+        gsum_o[r, :] = d
+        gb[r, :] = low
+        gat_s[r, :] = mm(low, w_o[got_o, :], NT).astype(BF16)
+        ga_copy(t).start()
+        ga_o[r, :] = mm(low, w_o[own_o, :], NT).astype(BF16)
+        add_vec(1, e * n)
+        add_vec(2, e)
+        add_vec(0, low.astype(F32))
+        return carry
+
+    lax.fori_loop(0, tiles, first_norm, 0)
+    vec_copy = copy(vec_s, vec_r, 11)
+    vec_copy.start()
+    bi_copy = copy(bi_s, bi_o.at[1], 12)
+    bi_copy.start()
+    cols_own = own_o
+    cols_got = got_o
+    wo_s[own_o, :] = mm(a_own[...], gb[:, cols_got], TN).astype(BF16)
+    wo_s[got_o, :] = mm(a_got[...], gb[:, cols_got], TN).astype(BF16)
+    wo_copy = copy(wo_s, wo_r, 13)
+    wo_copy.start()
+    own_part = mm(a_own[...], gb[:, cols_own], TN)
+    got_part = mm(a_got[...], gb[:, cols_own], TN)
+    bi_o[0] = bi_s[...]
+    wo_copy.wait_recv()
+    wo_g[own_o, :] = (own_part + wo_r[own_o, :].astype(F32)).astype(BF16)
+    wo_g[got_o, :] = (got_part + wo_r[got_o, :].astype(F32)).astype(BF16)
+    vec_copy.wait_recv()
+    vec_o[...] = vec_s[...] + vec_r[...]
+    bi_copy.wait_recv()
+
+    def finish(t, carry):
+        ga_copy(t).wait_recv()
+        fl_copy(t).wait_send()
+        feed_copy(t).wait_send()
+        gf_copy(t).wait_send()
+        part_copy(t).wait_send()
+        ga_copy(t).wait_send()
+        return carry
+
+    lax.fori_loop(0, tiles, finish, 0)
+    a_copy.wait_send()
+    vec_copy.wait_send()
+    bi_copy.wait_send()
+    wo_copy.wait_send()
+
+
+def middle(a_own, a_send, x, gout, b_output, gain1, shift1, b_in, b_out, gain2, shift2, w_o, w_in, w_out):
+    half, width = x.shape
+    hw = width // 2
     ff = w_in.shape[1]
-    t = 256
-    whole = lambda a: pl.BlockSpec(a.shape, lambda i: (0, 0))
-    row = lambda w: pl.BlockSpec((t, w), lambda i: (i, 0))
+    vm = pl.BlockSpec(memory_space=pltpu.VMEM)
+    hbm = pl.BlockSpec(memory_space=pl.ANY)
+    V = pltpu.VMEM
     return pl.pallas_call(
-        ffn_fwd_body,
-        grid=(rows // t,),
-        in_specs=[row(width), whole(w_in), whole(b_in), whole(w_out)],
-        out_specs=[row(ff), row(ff), row(width)],
-        out_shape=[shape((rows, ff), BF16)] * 2 + [shape((rows, width), dtype)],
-        compiler_params=params(),
-        cost_estimate=cost(4 * rows * width * ff, 8e6, rows * ff),
-        name="ffn_fwd",
-    )(x, w_in, b_in, w_out)
-
-
-def norm_two_body(first, f0, f1, b, g, s, go, out_o, gtwo_o, gf_o, gg, sg, bg):
-    u = first[...] + (f0[...] + f1[...].astype(F32)) + b[...].astype(F32)
-    n, rs = row_stats(u)
-    gain = g[...].astype(F32)
-    out_o[...] = (n * gain + s[...].astype(F32)).astype(BF16)
-    e = go[...].astype(F32)
-    eg = e * gain
-    d = (eg - jnp.mean(eg, -1, keepdims=True) - n * jnp.mean(eg * n, -1, keepdims=True)) * rs
-    low = d.astype(BF16)
-    gtwo_o[...] = d
-    gf_o[...] = low
-
-    @pl.when(pl.program_id(0) == 0)
-    def _():
-        gg[...] = jnp.zeros_like(gg)
-        sg[...] = jnp.zeros_like(sg)
-        bg[...] = jnp.zeros_like(bg)
-
-    gg[...] += jnp.sum(e * n, 0, keepdims=True)
-    sg[...] += jnp.sum(e, 0, keepdims=True)
-    bg[...] += jnp.sum(low.astype(F32), 0, keepdims=True)
-
-
-def norm_two(first, f0, f1, b, g, s, go):
-    rows, width = first.shape
-    t = 256
-    row = pl.BlockSpec((t, width), lambda i: (i, 0))
-    vec = pl.BlockSpec((1, width), lambda i: (0, 0))
-    return pl.pallas_call(
-        norm_two_body,
-        grid=(rows // t,),
-        in_specs=[row] * 3 + [vec] * 3 + [row],
-        out_specs=[row] * 3 + [vec] * 3,
+        middle_body,
+        in_specs=[vm] * 11 + [hbm] * 3,
+        out_specs=[vm] * 9,
         out_shape=[
-            shape((rows, width), BF16),
-            shape((rows, width), F32),
-            shape((rows, width), BF16),
-        ]
-        + [shape((1, width), F32)] * 3,
-        compiler_params=params(),
-        cost_estimate=cost(30 * rows * width, 8e6),
-        name="norm_two",
-    )(first, f0, f1, b, g, s, go)
-
-
-def ffn_bwd_body(gf, slope, w_in, w_out, gh_o, part_o, bg):
-    gh = (mm(gf[...], w_out[...]) * slope[...].astype(F32)).astype(BF16)
-    gh_o[...] = gh
-    part_o[...] = mm(gh, w_in[...], NT).astype(part_o.dtype)
-
-    @pl.when(pl.program_id(0) == 0)
-    def _():
-        bg[...] = jnp.zeros_like(bg)
-
-    bg[...] += jnp.sum(gh.astype(F32), 0, keepdims=True)
-
-
-def ffn_bwd(gf, slope, w_in, w_out, dtype):
-    rows, width = gf.shape
-    ff = w_in.shape[1]
-    t = 256
-    whole = lambda a: pl.BlockSpec(a.shape, lambda i: (0, 0))
-    row = lambda w: pl.BlockSpec((t, w), lambda i: (i, 0))
-    return pl.pallas_call(
-        ffn_bwd_body,
-        grid=(rows // t,),
-        in_specs=[row(width), row(ff), whole(w_in), whole(w_out)],
-        out_specs=[row(ff), row(width), pl.BlockSpec((1, ff), lambda i: (0, 0))],
-        out_shape=[shape((rows, ff), BF16), shape((rows, width), dtype), shape((1, ff), F32)],
-        compiler_params=params(),
-        cost_estimate=cost(4 * rows * width * ff, 8e6),
-        name="ffn_bwd",
-    )(gf, slope, w_in, w_out)
-
-
-def ffn_weights_body(a0, a1, b0, b1, out):
-    out[...] = (mm(a0[...], b0[...], TN) + mm(a1[...], b1[...], TN)).astype(BF16)
-
-
-def ffn_weights(a0, a1, b0, b1):
-    rows, width = a0.shape
-    ff = b0.shape[1]
-    t = 256
-    whole = pl.BlockSpec((rows, ff), lambda i: (0, 0))
-    lhs = pl.BlockSpec((rows, t), lambda i: (0, i))
-    return pl.pallas_call(
-        ffn_weights_body,
-        grid=(width // t,),
-        in_specs=[lhs, lhs, whole, whole],
-        out_specs=pl.BlockSpec((t, ff), lambda i: (i, 0)),
-        out_shape=shape((width, ff), BF16),
-        compiler_params=params(),
-        cost_estimate=cost(4 * rows * width * ff, 8e6),
-        name="ffn_weights",
-    )(a0, a1, b0, b1)
+            shape((half, width), BF16),
+            shape((half, width), F32),
+            shape((half, hw), BF16),
+            shape((half, hw), BF16),
+            shape((width, ff), BF16),
+            shape((width, ff), BF16),
+            shape((width, hw), BF16),
+            shape((8, width), F32),
+            shape((2, 8, ff), F32),
+        ],
+        scratch_shapes=[
+            V((half, hw), BF16),
+            V((2, half, width), BF16),
+            V((half, width), BF16),
+            V((half, width), BF16),
+            V((2, half, width), BF16),
+            V((half, width), BF16),
+            V((half, width), BF16),
+            V((half, hw), BF16),
+            V((half, width), BF16),
+            V((width, hw), BF16),
+            V((width, hw), BF16),
+            V((8, width), F32),
+            V((8, width), F32),
+            V((8, ff), F32),
+            V((width, width), BF16),
+            V((width, ff), BF16),
+            V((width, ff), BF16),
+            V((2, half, ff), BF16),
+            V((2, half, ff), BF16),
+            V((2, half, ff), BF16),
+            V((half, width), F32),
+            V((half, width), F32),
+            V((half, width), F32),
+            V((half, width), F32),
+            pltpu.SemaphoreType.DMA((3,)),
+            pltpu.SemaphoreType.DMA((14,)),
+            pltpu.SemaphoreType.DMA((14,)),
+        ],
+        compiler_params=pltpu.CompilerParams(
+            vmem_limit_bytes=60 << 20, collective_id=1, has_side_effects=True
+        ),
+        cost_estimate=cost(17e9, 20e6),
+        name="middle",
+    )(a_own, a_send, x, gout, b_output, gain1, shift1, b_in, b_out, gain2, shift2, w_o, w_in, w_out)
 
 
 def pick(a, index, axis):
@@ -552,28 +586,10 @@
     q, k, v, probs, a_own, a_send = attn_fwd(
         sc, x, x_got, w_query, w_key, w_value, vec(b_query), vec(b_value), rand
     )
-    a_got = swap(a_send)
-    u_one, first, first_low = proj_norm(
-        sc, a_own, a_got, x, w_output, vec(b_output), vec(gain_one), vec(shift_one)
-    )
-    first_got = swap(first_low)
-    act0, slope0, feed0 = ffn_fwd(first_low, w_in, vec(b_in), w_out, F32)
-    act1, slope1, feed1 = ffn_fwd(first_got, w_in, vec(b_in), w_out, BF16)
-    out, grad_two, grad_feed, gain_two_g, shift_two_g, b_out_g = norm_two(
-        first, feed0, swap(feed1), vec(b_out), vec(gain_two), vec(shift_two), grad_out[0]
-    )
-    gf_got = swap(grad_feed)
-    gh0, part0, bi0 = ffn_bwd(grad_feed, slope0, w_in, w_out, F32)
-    gh1, part1, bi1 = ffn_bwd(gf_got, slope1, w_in, w_out, BF16)
-    part_got = swap(part1)
-    w_out_g = ffn_weights(grad_feed, gf_got, act0, act1)
-    w_in_g = ffn_weights(first_low, first_got, gh0, gh1)
-    gsum, gb, ga0, ga1, gain_one_g, shift_one_g, b_output_g = norm_one_back(
-        sc, grad_two, part0, part_got, u_one, vec(gain_one), w_output
-    )
-    ga_got = swap(ga1)
-    wo_keep, wo_send = w_output_grad(sc, a_own, a_got, gb)
-    w_output_g = (wo_keep + swap(wo_send).astype(F32)).astype(BF16)
+    out, gsum, ga0, ga_got, w_out_g, w_in_g, w_output_g, vec_g, bi_g = middle(
+        a_own, a_send, x, grad_out[0], vec(b_output), vec(gain_one), vec(shift_one), vec(b_in),
+        vec(b_out), vec(gain_two), vec(shift_two), w_output, w_in, w_out,
+    )
     wqkv_g, bq_g, bv_g, ig_own, ig_send = attn_bwd(
         sc, x, x_got, w_query, w_key, w_value, q, k, v, probs, a_own, a_send, ga0, ga_got
     )
@@ -585,12 +601,11 @@
         )
 
     ff_all = 2 * w_in.shape[1]
-    vectors = [
-        spread(bq_g, width), spread(bv_g, width), b_output_g, gain_one_g, shift_one_g, b_out_g,
-        gain_two_g, shift_two_g, spread(bi0 + bi1, ff_all),
-    ]
-    table = jnp.concatenate([a.reshape(dp_size, -1) for a in vectors], axis=1)
-    table = table + swap(table)
+    bqv = jnp.concatenate([spread(bq_g, width), spread(bv_g, width)], axis=0)
+    bqv = bqv + swap(bqv)
+    bi_all = jnp.where(core == 0, bi_g[:, 0], bi_g[::-1, 0]).reshape(dp_size, -1)
+    eight = jnp.concatenate([bqv, vec_g[:6]], axis=0).reshape(8, dp_size, -1)
+    table = jnp.concatenate([eight.transpose(1, 0, 2).reshape(dp_size, -1), bi_all], axis=1)
     rows = width // dp_size
     lanes = 2 * HD
     table = jnp.pad(table, ((0, 0), (0, rows * lanes - table.shape[1])))

time: 242 us -> 228 us (0.942)
  waiting for transfers between devices: 18.9 us -> 70.3 us
  Pallas kernels: 114 us -> 89 us
  local copies, waits for them, and re-layouts: 45.2 us -> 26.4 us
  other arithmetic: 20.9 us -> 10.1 us
  starting transfers between devices: 39.3 us -> 29.9 us
    ppermute x8, waiting for transfers between devices: 7.35 us -> 45.3 us  [halve(): got = lax.ppermute(pick(parts, 1 - mine, bit_axis), 'dp', pairs)]
    pallas_call x10 -> x1, Pallas kernels: 61.4 us -> 36.1 us  [middle(): pl.pallas_call(middle_body, in_specs=[vm] * 11 + [hbm] * 3, out_specs=[vm...]
    ppermute x12, waiting for transfers between devices: 9.86 us -> 24.9 us  [sum_rest(): got = lax.ppermute(pick(parts, (high + s) % groups, 0), 'dp', perm)]
    ppermute x12, starting transfers between devices: 25.5 us -> 15.8 us  [sum_rest(): got = lax.ppermute(pick(parts, (high + s) % groups, 0), 'dp', perm)]
    reshape x9 -> x3, local copies, waits for them, and re-layouts: 9.58 us -> 0.2 us  [the longest x2 0.11 us: local_pair(): eight = jnp.concatenate([bqv, vec_g[:6]], axis=0).reshape(8, dp_size, -1)]
    pallas_call x6 -> x0, other arithmetic: 5.93 us -> none  [the longest x3 3.86 us: norm_one_back(): pl.pallas_call(norm_one_back_body, grid_spec=pltpu.PrefetchScalarGridSpec...]
    reshape x9, local copies, waits for them, and re-layouts: 6.61 us -> 11.4 us  [local_pair(): vec = lambda a: a.reshape(1, -1)]
    unnamed x53 -> x23, local copies, waits for them, and re-layouts: 7.75 us -> 3.2 us
  transfers between devices with their start and end apart: 31 -> 24, of which waited for: 7 -> 10; matrix products, arithmetic and copies ran while one was open for 23% -> 13% of each run, Pallas kernels for 27% -> 0%
where the time goes in v2:
time: 228 us; the launch traced here: 227 us
  Pallas kernels  89 us (39%)
  waiting for transfers between devices  70.3 us (31%)
  starting transfers between devices  29.9 us (13%)
  local copies, waits for them, and re-layouts  26.4 us (12%)
  other arithmetic  10.1 us (4%)
    ppermute x8, waiting for transfers between devices, halve(): got = lax.ppermute(pick(parts, 1 - mine, bit_axis), 'dp', pairs)  45.3 us
    pallas_call x1, Pallas kernels, middle(): pl.pallas_call(middle_body, in_specs=[vm] * 11 + [hbm] * 3, out_specs=[vm...  36.1 us
    pallas_call x1, Pallas kernels, attn_bwd(): pl.pallas_call(attn_bwd_body, grid_spec=pltpu.PrefetchScalarGridSpec(num_...  26.8 us
    pallas_call x1, Pallas kernels, attn_fwd(): pl.pallas_call(attn_fwd_body, grid_spec=pltpu.PrefetchScalarGridSpec(num_...  26.1 us
    ppermute x12, waiting for transfers between devices, sum_rest(): got = lax.ppermute(pick(parts, (high + s) % groups, 0), 'dp', perm)  24.9 us
    ppermute x12, starting transfers between devices, sum_rest(): got = lax.ppermute(pick(parts, (high + s) % groups, 0), 'dp', perm)  15.8 us
    ppermute x8, starting transfers between devices, halve(): got = lax.ppermute(pick(parts, 1 - mine, bit_axis), 'dp', pairs)  13 us
    reshape x9, local copies, waits for them, and re-layouts, local_pair(): vec = lambda a: a.reshape(1, -1)  11.4 us
  transfers between devices with their start and end apart: 24, of which 10 were waited for; matrix products, arithmetic and copies ran while one was open for 13% of the time, Pallas kernels for 0%

profile of v2, /device:TPU:0, one launch (start us, length us, event | category | flops | bytes accessed | tf_op | source)
XLA Modules:
  0.0 227.4 jit_solution(1584876018055906077)
XLA Ops:
  2.6 1.3 reshape.120.bq
  5.1 1.3 reshape.125.b_in
  10.2 1.3 reshape.126.b_out
  12.7 1.3 reshape.128.shift2
  16.2 26.1 %attn_fwd.1 = (bf16[1024,384]{1,0:T(8,128)(2,1)}, bf16[1024,384]{1,0:T(8,128)(2,1)}, bf16[1024,384]{1,0:T(8,128)(2,1)}, bf16[6,1024,1024]{2,1,0:T(8,128)(2,1)}, ...) custom-call(s32[2]{0:T(128)} %pad_add_fusion.1.sc, bf16[512,768]{1,0:T(8,128)(2,1)} %bitcast.138, ...), custom_call_target="tpu_custom_call" | custom-call | flops 20000000000 | bytes 20000000 | tf_op jit(solution)/shard_map/attn_fwd/pallas_call | solution.py:117
  42.3 36.1 %middle.1 = (bf16[512,768]{1,0:T(8,128)(2,1)}, f32[512,768]{1,0:T(8,128)}, bf16[512,384]{1,0:T(8,128)(2,1)}, bf16[512,384]{1,0:T(8,128)(2,1)}, bf16[768,1536]{1,...) custom-call(bf16[512,384]{1,0:T(8,128)(2,1)} %get-tuple-element.37.a, ...), custom_call_target="tpu_custom_call" | custom-call | flops 16999999488 | bytes 20000000 | tf_op jit(solution)/shard_map/middle/pallas_call | solution.py:486
  78.4 26.8 %attn_bwd.1 = (bf16[768,1152]{1,0:T(8,128)(2,1)}, f32[1,384]{1,0:T(1,128)}, f32[1,384]{1,0:T(1,128)}, f32[512,768]{1,0:T(8,128)}, bf16[512,768]{1,0:T(8,128)(2,1)}) custom-call(s32[2]{0:T(128)} %pad_add_fusion.1.sc, bf16[512,768]{1,0:T(8,128)(2,1)} %bitcast.140, bf16[512,768]{1,0:T(8,128)(2,1)} %copy-done.8, bf16[768,768]{1,0:T(8,128)(2,1)} %wq.3, ...), custom_call_target="tpu_custom_call" | custom-call | flops 40000000000 | bytes 20000000 | tf_op jit(solution)/shard_map/attn_bwd/pallas_call | solution.py:218
  105.2 1.5 slice.61
  109.2 2.9 %collective-permute-start.19 = (bf16[4,2,48,1536]{3,2,0,1:T(8,128)(2,1)}, bf16[4,2,48,1536]{3,2,0,1:T(8,128)(2,1)}, u32[]{:S(2)}, u32[]{:S(2)}) collective-permute-start(bf16[4,2,48,1536]{3,2,0,1:T(8,128)(2,1)} %bitcast.114), channel_id=1, source_target_pairs={{0,2},{2,0},{4,6},{6,4},{8,10},{10,8},{12,14},{14,12},{16,18},{18,... | collective-permute-start | bytes 3538952 | tf_op jit(solution)/shard_map/ppermute | solution.py:546
  116.6 2.1 collective-permute-start.9
  120.0 1.4 collective-permute-start.14
  121.4 29.7 %collective-permute-done.3 = bf16[4,2,48,768]{3,2,0,1:T(8,128)(2,1)S(1)} collective-permute-done((bf16[4,2,48,768]{3,2,0,1:T(8,128)(2,1)}, bf16[4,2,48,768]{3,2,0,1:T(8,128)(2,1)S(1)}, u32[]{:S(2)}, u32[]{:S(2)}) %collective-permute-start.3) | collective-permute-done | bytes 589856 | tf_op jit(solution)/shard_map/ppermute | solution.py:546
  151.3 1.8 collective-permute-start.4
  153.4 1.6 collective-permute-start.10
  155.0 2.6 %add_bitcast_fusion = f32[1,512,768]{2,1,0:T(8,128)} fusion(f32[512,768]{1,0:T(8,128)S(1)} %copy-done.2, f32[512,768]{1,0:T(8,128)S(1)} %copy-done.3, bf16[512,768]{1,0:T(8,128)(2,1)} %collective-permute-done.2), kind=kLoop, calls=%fused_computation.4 | loop fusion | flops 1179648 | bytes 5505024 | tf_op jit(solution)/shard_map/broadcast_in_dim | solution.py:629
  157.6 8.3 %collective-permute-done.4 = bf16[4,48,768]{2,1,0:T(8,128)(2,1)S(1)} collective-permute-done((bf16[4,48,768]{2,1,0:T(8,128)(2,1)S(1)}, bf16[4,48,768]{2,1,0:T(8,128)(2,1)S(1)}, u32[]{:S(2)}, u32[]{:S(2)}) %collective-permute-start.4) | collective-permute-done | bytes 294944 | tf_op jit(solution)/shard_map/ppermute | solution.py:546
  166.0 1.9 collective-permute-start.5
  167.9 2.6 %collective-permute-start.6 = (bf16[48,768]{1,0:T(8,128)(2,1)S(1)}, bf16[48,768]{1,0:T(8,128)(2,1)S(1)}, u32[]{:S(2)}, u32[]{:S(2)}) collective-permute-start(bf16[48,768]{1,0:T(8,128)(2,1)S(1)} %get-tuple-element.79), channel_id=1, source_target_pairs={{0,16},{2,18},{4,20},{6,22},{8,24},{10,26},{12,28},{14,30},{16,0},... | collective-permute-start | bytes 221192 | tf_op jit(solution)/shard_map/ppermute | solution.py:557
  170.4 1.3 collective-permute-start.7
  173.1 4.1 %collective-permute-done.6 = bf16[48,768]{1,0:T(8,128)(2,1)S(1)} collective-permute-done((bf16[48,768]{1,0:T(8,128)(2,1)S(1)}, bf16[48,768]{1,0:T(8,128)(2,1)S(1)}, u32[]{:S(2)}, u32[]{:S(2)}) %collective-permute-start.6) | collective-permute-done | bytes 73760 | tf_op jit(solution)/shard_map/ppermute | solution.py:557
  177.2 2.8 %collective-permute-start.13 = (bf16[48,896]{1,0:T(8,128)(2,1)S(1)}, bf16[48,896]{1,0:T(8,128)(2,1)S(1)}, u32[]{:S(2)}, u32[]{:S(2)}) collective-permute-start(bf16[48,896]{1,0:T(8,128)(2,1)S(1)} %get-tuple-element.75), channel_id=1, source_target_pairs={{0,24},{2,26},{4,28},{6,30},{8,0},{10,2},{12,4},{14,6},{16,8},{18,... | collective-permute-start | bytes 258056 | tf_op jit(solution)/shard_map/ppermute | solution.py:557
  180.0 3.4 %collective-permute-done.12 = bf16[48,896]{1,0:T(8,128)(2,1)S(1)} collective-permute-done((bf16[48,896]{1,0:T(8,128)(2,1)S(1)}, bf16[48,896]{1,0:T(8,128)(2,1)S(1)}, u32[]{:S(2)}, u32[]{:S(2)}) %collective-permute-start.12) | collective-permute-done | bytes 86048 | tf_op jit(solution)/shard_map/ppermute | solution.py:557
  187.8 1.6 fusion
  189.4 1.6 collective-permute-start.20
  191.0 1.6 fusion.1
  192.7 1.6 collective-permute-start.15
  194.2 7.3 %collective-permute-done.20 = bf16[4,48,1536]{2,1,0:T(8,128)(2,1)S(1)} collective-permute-done((bf16[4,48,1536]{2,1,0:T(8,128)(2,1)S(1)}, bf16[4,48,1536]{2,1,0:T(8,128)(2,1)S(1)}, u32[]{:S(2)}, u32[]{:S(2)}) %collective-permute-start.20) | collective-permute-done | bytes 589856 | tf_op jit(solution)/shard_map/ppermute | solution.py:546
  202.5 2.6 %collective-permute-start.22 = (bf16[48,1536]{1,0:T(8,128)(2,1)S(1)}, bf16[48,1536]{1,0:T(8,128)(2,1)S(1)}, u32[]{:S(2)}, u32[]{:S(2)}) collective-permute-start(bf16[48,1536]{1,0:T(8,128)(2,1)S(1)} %get-tuple-element.70), channel_id=1, source_target_pairs={{0,16},{2,18},{4,20},{6,22},{8,24},{10,26},{12,28},{14,30},{16,0},... | collective-permute-start | bytes 442376 | tf_op jit(solution)/shard_map/ppermute | solution.py:557
  205.8 1.7 collective-permute-start.16
  208.1 2.3 %collective-permute-done.21 = bf16[48,1536]{1,0:T(8,128)(2,1)S(1)} collective-permute-done((bf16[48,1536]{1,0:T(8,128)(2,1)S(1)}, bf16[48,1536]{1,0:T(8,128)(2,1)S(1)}, u32[]{:S(2)}, u32[]{:S(2)}) %collective-permute-start.21) | collective-permute-done | bytes 147488 | tf_op jit(solution)/shard_map/ppermute | solution.py:557
  211.4 8.2 %collective-permute-done.22 = bf16[48,1536]{1,0:T(8,128)(2,1)S(1)} collective-permute-done((bf16[48,1536]{1,0:T(8,128)(2,1)S(1)}, bf16[48,1536]{1,0:T(8,128)(2,1)S(1)}, u32[]{:S(2)}, u32[]{:S(2)}) %collective-permute-start.22) | collective-permute-done | bytes 147488 | tf_op jit(solution)/shard_map/ppermute | solution.py:557
  220.4 5.3 %collective-permute-done.17 = bf16[48,1536]{1,0:T(8,128)(2,1)S(1)} collective-permute-done((bf16[48,1536]{1,0:T(8,128)(2,1)S(1)}, bf16[48,1536]{1,0:T(8,128)(2,1)S(1)}, u32[]{:S(2)}, u32[]{:S(2)}) %collective-permute-start.17) | collective-permute-done | bytes 147488 | tf_op jit(solution)/shard_map/ppermute | solution.py:557
  (108 shorter events, 29.9 us)
Async XLA Ops:
  0.7 14.7 %collective-permute-start = (bf16[512,768]{1,0:T(8,128)(2,1)}, bf16[512,768]{1,0:T(8,128)(2,1)S(1)}, u32[]{:S(2)}, u32[]{:S(2)}) collective-permute-start(bf16[512,768]{1,0:T(8,128)(2,1)} %bitcast.137), channel_id=1, source_target_pairs={{0,1},{1,0},{2,3},{3,2},{4,5},{5,4},{6,7},{7,6},{8,9},{9,8},{10,11... | collective-permute-start | bytes 2359304 | tf_op jit(solution)/shard_map/ppermute | solution.py:579
  1.9 12.7 %collective-permute-start.1 = (s32[8,3]{0,1:T(4,128)S(1)}, s32[8,3]{0,1:T(4,128)S(1)}, u32[]{:S(2)}, u32[]{:S(2)}) collective-permute-start(s32[8,3]{0,1:T(4,128)S(1)} %bitcast.134), channel_id=1, source_target_pairs={{0,1},{1,0},{2,3},{3,2},{4,5},{5,4},{6,7},{7,6},{8,9},{9,8},{10,11... | collective-permute-start | bytes 296 | tf_op jit(solution)/shard_map/ppermute | solution.py:579
  105.2 2.6 %copy-start.1 = (bf16[768,1536]{1,0:T(8,128)(2,1)S(1)}, bf16[768,1536]{1,0:T(8,128)(2,1)}, u32[]{:S(2)}) copy-start(bf16[768,1536]{1,0:T(8,128)(2,1)} %get-tuple-element.56) | copy-start | bytes 7077892
  109.2 78.6 %collective-permute-start.19 = (bf16[4,2,48,1536]{3,2,0,1:T(8,128)(2,1)}, bf16[4,2,48,1536]{3,2,0,1:T(8,128)(2,1)}, u32[]{:S(2)}, u32[]{:S(2)}) collective-permute-start(bf16[4,2,48,1536]{3,2,0,1:T(8,128)(2,1)} %bitcast.114), channel_id=1, source_target_pairs={{0,2},{2,0},{4,6},{6,4},{8,10},{10,8},{12,14},{14,12},{16,18},{18,... | collective-permute-start | bytes 3538952 | tf_op jit(solution)/shard_map/ppermute | solution.py:546
  112.2 0.9 copy-start.7
  112.2 0.9 copy-start.6
  112.2 2.0 copy-start.5
  113.1 38.0 %collective-permute-start.3 = (bf16[4,2,48,768]{3,2,0,1:T(8,128)(2,1)}, bf16[4,2,48,768]{3,2,0,1:T(8,128)(2,1)S(1)}, u32[]{:S(2)}, u32[]{:S(2)}) collective-permute-start(bf16[4,2,48,768]{3,2,0,1:T(8,128)(2,1)} %bitcast.117), channel_id=1, source_target_pairs={{0,2},{2,0},{4,6},{6,4},{8,10},{10,8},{12,14},{14,12},{16,18},{18,... | collective-permute-start | bytes 1769480 | tf_op jit(solution)/shard_map/ppermute | solution.py:546
  113.2 1.6 collective-permute-start.8
  114.3 40.6 %collective-permute-start.2 = (bf16[512,768]{1,0:T(8,128)(2,1)}, bf16[512,768]{1,0:T(8,128)(2,1)}, u32[]{:S(2)}, u32[]{:S(2)}) collective-permute-start(bf16[512,768]{1,0:T(8,128)(2,1)} %get-tuple-element.48), channel_id=1, source_target_pairs={{0,1},{1,0},{2,3},{3,2},{4,5},{5,4},{6,7},{7,6},{8,9},{9,8},{10,11... | collective-permute-start | bytes 2359304 | tf_op jit(solution)/shard_map/ppermute | solution.py:579
  116.4 2.3 %copy-start = (bf16[768,1536]{1,0:T(8,128)(2,1)S(1)}, bf16[768,1536]{1,0:T(8,128)(2,1)}, u32[]{:S(2)}) copy-start(bf16[768,1536]{1,0:T(8,128)(2,1)} %get-tuple-element.55) | copy-start | bytes 7077892
  116.6 36.6 %collective-permute-start.9 = (bf16[4,2,48,896]{3,2,0,1:T(8,128)(2,1)S(1)}, bf16[4,2,48,896]{3,2,0,1:T(8,128)(2,1)S(1)}, u32[]{:S(2)}, u32[]{:S(2)}) collective-permute-start(bf16[4,2,48,896]{3,2,0,1:T(8,128)(2,1)S(1)} %bitcast.127), channel_id=1, source_target_pairs={{0,4},{2,6},{4,0},{6,2},{8,12},{10,14},{12,8},{14,10},{16,20},{18,... | collective-permute-start | bytes 2064392 | tf_op jit(solution)/shard_map/ppermute | solution.py:546
  120.0 71.0 %collective-permute-start.14 = (bf16[4,2,48,1536]{3,2,0,1:T(8,128)(2,1)}, bf16[4,2,48,1536]{3,2,0,1:T(8,128)(2,1)}, u32[]{:S(2)}, u32[]{:S(2)}) collective-permute-start(bf16[4,2,48,1536]{3,2,0,1:T(8,128)(2,1)} %bitcast.115), channel_id=1, source_target_pairs={{0,4},{2,6},{4,0},{6,2},{8,12},{10,14},{12,8},{14,10},{16,20},{18,... | collective-permute-start | bytes 3538952 | tf_op jit(solution)/shard_map/ppermute | solution.py:546
  151.3 3.7 %copy-start.3 = (f32[512,768]{1,0:T(8,128)S(1)}, f32[512,768]{1,0:T(8,128)}, u32[]{:S(2)}) copy-start(f32[512,768]{1,0:T(8,128)} %get-tuple-element.47) | copy-start | bytes 4718596
  151.3 14.6 %collective-permute-start.4 = (bf16[4,48,768]{2,1,0:T(8,128)(2,1)S(1)}, bf16[4,48,768]{2,1,0:T(8,128)(2,1)S(1)}, u32[]{:S(2)}, u32[]{:S(2)}) collective-permute-start(bf16[4,48,768]{2,1,0:T(8,128)(2,1)S(1)} %dynamic-slice_bitcast_fusion.3), channel_id=1, source_target_pairs={{0,4},{2,6},{4,0},{6,2},{8,12},{10,14},{12,8},{14,10},{16,20},{18,... | collective-permute-start | bytes 884744 | tf_op jit(solution)/shard_map/ppermute | solution.py:546
  153.2 1.8 copy-start.2
  153.4 17.1 %collective-permute-start.10 = (bf16[4,48,896]{2,1,0:T(8,128)(2,1)S(1)}, bf16[4,48,896]{2,1,0:T(8,128)(2,1)S(1)}, u32[]{:S(2)}, u32[]{:S(2)}) collective-permute-start(bf16[4,48,896]{2,1,0:T(8,128)(2,1)S(1)} %dynamic-slice_bitcast_fusion.2), channel_id=1, source_target_pairs={{0,2},{2,0},{4,6},{6,4},{8,10},{10,8},{12,14},{14,12},{16,18},{18,... | collective-permute-start | bytes 1032200 | tf_op jit(solution)/shard_map/ppermute | solution.py:546
  166.0 7.1 %collective-permute-start.5 = (bf16[48,768]{1,0:T(8,128)(2,1)S(1)}, bf16[48,768]{1,0:T(8,128)(2,1)S(1)}, u32[]{:S(2)}, u32[]{:S(2)}) collective-permute-start(bf16[48,768]{1,0:T(8,128)(2,1)S(1)} %get-tuple-element.77), channel_id=1, source_target_pairs={{0,8},{2,10},{4,12},{6,14},{8,16},{10,18},{12,20},{14,22},{16,24},... | collective-permute-start | bytes 221192 | tf_op jit(solution)/shard_map/ppermute | solution.py:557
  167.9 9.3 %collective-permute-start.6 = (bf16[48,768]{1,0:T(8,128)(2,1)S(1)}, bf16[48,768]{1,0:T(8,128)(2,1)S(1)}, u32[]{:S(2)}, u32[]{:S(2)}) collective-permute-start(bf16[48,768]{1,0:T(8,128)(2,1)S(1)} %get-tuple-element.79), channel_id=1, source_target_pairs={{0,16},{2,18},{4,20},{6,22},{8,24},{10,26},{12,28},{14,30},{16,0},... | collective-permute-start | bytes 221192 | tf_op jit(solution)/shard_map/ppermute | solution.py:557
  170.4 6.8 %collective-permute-start.7 = (bf16[48,768]{1,0:T(8,128)(2,1)S(1)}, bf16[48,768]{1,0:T(8,128)(2,1)S(1)}, u32[]{:S(2)}, u32[]{:S(2)}) collective-permute-start(bf16[48,768]{1,0:T(8,128)(2,1)S(1)} %get-tuple-element.78), channel_id=1, source_target_pairs={{0,24},{2,26},{4,28},{6,30},{8,0},{10,2},{12,4},{14,6},{16,8},{18,... | collective-permute-start | bytes 221192 | tf_op jit(solution)/shard_map/ppermute | solution.py:557
  173.1 6.9 %collective-permute-start.11 = (bf16[48,896]{1,0:T(8,128)(2,1)S(1)}, bf16[48,896]{1,0:T(8,128)(2,1)S(1)}, u32[]{:S(2)}, u32[]{:S(2)}) collective-permute-start(bf16[48,896]{1,0:T(8,128)(2,1)S(1)} %get-tuple-element.74), channel_id=1, source_target_pairs={{0,8},{2,10},{4,12},{6,14},{8,16},{10,18},{12,20},{14,22},{16,24},... | collective-permute-start | bytes 258056 | tf_op jit(solution)/shard_map/ppermute | solution.py:557
  177.2 6.3 %collective-permute-start.12 = (bf16[48,896]{1,0:T(8,128)(2,1)S(1)}, bf16[48,896]{1,0:T(8,128)(2,1)S(1)}, u32[]{:S(2)}, u32[]{:S(2)}) collective-permute-start(bf16[48,896]{1,0:T(8,128)(2,1)S(1)} %get-tuple-element.76), channel_id=1, source_target_pairs={{0,16},{2,18},{4,20},{6,22},{8,24},{10,26},{12,28},{14,30},{16,0},... | collective-permute-start | bytes 258056 | tf_op jit(solution)/shard_map/ppermute | solution.py:557
  177.2 6.7 %collective-permute-start.13 = (bf16[48,896]{1,0:T(8,128)(2,1)S(1)}, bf16[48,896]{1,0:T(8,128)(2,1)S(1)}, u32[]{:S(2)}, u32[]{:S(2)}) collective-permute-start(bf16[48,896]{1,0:T(8,128)(2,1)S(1)} %get-tuple-element.75), channel_id=1, source_target_pairs={{0,24},{2,26},{4,28},{6,30},{8,0},{10,2},{12,4},{14,6},{16,8},{18,... | collective-permute-start | bytes 258056 | tf_op jit(solution)/shard_map/ppermute | solution.py:557
  189.4 12.0 %collective-permute-start.20 = (bf16[4,48,1536]{2,1,0:T(8,128)(2,1)S(1)}, bf16[4,48,1536]{2,1,0:T(8,128)(2,1)S(1)}, u32[]{:S(2)}, u32[]{:S(2)}) collective-permute-start(bf16[4,48,1536]{2,1,0:T(8,128)(2,1)S(1)} %dynamic-slice_bitcast_fusion), channel_id=1, source_target_pairs={{0,4},{2,6},{4,0},{6,2},{8,12},{10,14},{12,8},{14,10},{16,20},{18,... | collective-permute-start | bytes 1769480 | tf_op jit(solution)/shard_map/ppermute | solution.py:546
  192.7 12.9 %collective-permute-start.15 = (bf16[4,48,1536]{2,1,0:T(8,128)(2,1)S(1)}, bf16[4,48,1536]{2,1,0:T(8,128)(2,1)S(1)}, u32[]{:S(2)}, u32[]{:S(2)}) collective-permute-start(bf16[4,48,1536]{2,1,0:T(8,128)(2,1)S(1)} %dynamic-slice_bitcast_fusion.1), channel_id=1, source_target_pairs={{0,2},{2,0},{4,6},{6,4},{8,10},{10,8},{12,14},{14,12},{16,18},{18,... | collective-permute-start | bytes 1769480 | tf_op jit(solution)/shard_map/ppermute | solution.py:546
  201.7 8.7 %collective-permute-start.21 = (bf16[48,1536]{1,0:T(8,128)(2,1)S(1)}, bf16[48,1536]{1,0:T(8,128)(2,1)S(1)}, u32[]{:S(2)}, u32[]{:S(2)}) collective-permute-start(bf16[48,1536]{1,0:T(8,128)(2,1)S(1)} %get-tuple-element.68), channel_id=1, source_target_pairs={{0,8},{2,10},{4,12},{6,14},{8,16},{10,18},{12,20},{14,22},{16,24},... | collective-permute-start | bytes 442376 | tf_op jit(solution)/shard_map/ppermute | solution.py:557
  202.5 17.1 %collective-permute-start.22 = (bf16[48,1536]{1,0:T(8,128)(2,1)S(1)}, bf16[48,1536]{1,0:T(8,128)(2,1)S(1)}, u32[]{:S(2)}, u32[]{:S(2)}) collective-permute-start(bf16[48,1536]{1,0:T(8,128)(2,1)S(1)} %get-tuple-element.70), channel_id=1, source_target_pairs={{0,16},{2,18},{4,20},{6,22},{8,24},{10,26},{12,28},{14,30},{16,0},... | collective-permute-start | bytes 442376 | tf_op jit(solution)/shard_map/ppermute | solution.py:557
  205.2 14.4 %collective-permute-start.23 = (bf16[48,1536]{1,0:T(8,128)(2,1)S(1)}, bf16[48,1536]{1,0:T(8,128)(2,1)S(1)}, u32[]{:S(2)}, u32[]{:S(2)}) collective-permute-start(bf16[48,1536]{1,0:T(8,128)(2,1)S(1)} %get-tuple-element.69), channel_id=1, source_target_pairs={{0,24},{2,26},{4,28},{6,30},{8,0},{10,2},{12,4},{14,6},{16,8},{18,... | collective-permute-start | bytes 442376 | tf_op jit(solution)/shard_map/ppermute | solution.py:557
  205.7 20.8 %copy-start.4 = (bf16[512,768]{1,0:T(8,128)(2,1)S(1)}, bf16[512,768]{1,0:T(8,128)(2,1)}, u32[]{:S(2)}) copy-start(bf16[512,768]{1,0:T(8,128)(2,1)} %get-tuple-element.39) | copy-start | bytes 2359300
  205.8 14.6 %collective-permute-start.16 = (bf16[48,1536]{1,0:T(8,128)(2,1)S(1)}, bf16[48,1536]{1,0:T(8,128)(2,1)S(1)}, u32[]{:S(2)}, u32[]{:S(2)}) collective-permute-start(bf16[48,1536]{1,0:T(8,128)(2,1)S(1)} %get-tuple-element.71), channel_id=1, source_target_pairs={{0,8},{2,10},{4,12},{6,14},{8,16},{10,18},{12,20},{14,22},{16,24},... | collective-permute-start | bytes 442376 | tf_op jit(solution)/shard_map/ppermute | solution.py:557
  207.5 18.2 %collective-permute-start.17 = (bf16[48,1536]{1,0:T(8,128)(2,1)S(1)}, bf16[48,1536]{1,0:T(8,128)(2,1)S(1)}, u32[]{:S(2)}, u32[]{:S(2)}) collective-permute-start(bf16[48,1536]{1,0:T(8,128)(2,1)S(1)} %get-tuple-element.73), channel_id=1, source_target_pairs={{0,16},{2,18},{4,20},{6,22},{8,24},{10,26},{12,28},{14,30},{16,0},... | collective-permute-start | bytes 442376 | tf_op jit(solution)/shard_map/ppermute | solution.py:557
  210.4 15.3 %collective-permute-start.18 = (bf16[48,1536]{1,0:T(8,128)(2,1)S(1)}, bf16[48,1536]{1,0:T(8,128)(2,1)S(1)}, u32[]{:S(2)}, u32[]{:S(2)}) collective-permute-start(bf16[48,1536]{1,0:T(8,128)(2,1)S(1)} %get-tuple-element.72), channel_id=1, source_target_pairs={{0,24},{2,26},{4,28},{6,30},{8,0},{10,2},{12,4},{14,6},{16,8},{18,... | collective-permute-start | bytes 442376 | tf_op jit(solution)/shard_map/ppermute | solution.py:557
  (1 other events, 0.9 us)

commit v3 on v2

--- a/solution.py
+++ b/solution.py
@@ -134,128 +134,77 @@
     )(sc, xo, xt, wq, wk, wv, bq, bv, rand)
 
 
-def attn_bwd_body(
-    sc, xo, xt, wq, wk, wv, q_i, k_i, v_i, p_i, ao, at, go, gt,
-    wg, bqg, bvg, igo, igt, g_s, gT, qT, dkT, dvT, dqkv, wcat, xT, acc,
-):
-    half = xo.shape[0]
-    rows = 2 * half
-    pw = 2 * HD
-    tile = 256
-    step_id = pl.program_id(0)
-
-    @pl.when(step_id == 0)
-    def _():
-        xT[:, :half] = xo[...].T
-        xT[:, half:] = xt[...].T
-
-    for i, w in enumerate((wq, wk, wv)):
-        wcat[:, i * pw : (i + 1) * pw] = w[...]
-    g_s[:half, :] = go[...]
-    g_s[half:, :] = gt[...]
-    gT[...] = g_s[...].T
-    qT[...] = q_i[...].T
-    dkT[...] = jnp.zeros_like(dkT)
-    dvT[...] = jnp.zeros_like(dvT)
-    lane = lax.broadcasted_iota(jnp.int32, (tile, pw), 1)
-    low = lane < HD
-
-    for i, a_ref in enumerate((ao, at)):
-
-        def step(t, carry, i=i, a_ref=a_ref):
-            r0 = pl.multiple_of(i * half + t * tile, tile)
-            a0 = pl.multiple_of(t * tile, tile)
-            g = g_s[pl.ds(r0, tile), :]
-            ga = g.astype(F32) * a_ref[pl.ds(a0, tile), :].astype(F32)
-            outs = []
-            for h in range(2):
-                mine = low if h == 0 else ~low
-                hs = slice(h * HD, (h + 1) * HD)
-                dp = mm(jnp.where(mine, g, BF16(0)), v_i[...], NT)
-                delta = jnp.sum(jnp.where(mine, ga, 0.0), axis=-1, keepdims=True)
-                p = p_i[h, pl.ds(r0, tile), :]
-                ds = (p.astype(F32) * (dp - delta)).astype(BF16)
-                outs.append(mm(ds, k_i[...]))
-                dvT[hs, :] += mm(gT[hs, pl.ds(r0, tile)], p)
-                dkT[hs, :] += mm(qT[hs, pl.ds(r0, tile)], ds)
-            dq = jnp.where(low, outs[0], outs[1]) * HD**-0.5
-            dqkv[pl.ds(r0, tile), 0:pw] = dq.astype(BF16)
-            return carry
-
-        lax.fori_loop(0, half // tile, step, 0)
-
-    dqkv[:, pw : 2 * pw] = (dkT[...].T * HD**-0.5).astype(BF16)
-    dqkv[:, 2 * pw : 3 * pw] = dvT[...].T.astype(BF16)
-    d = dqkv[...]
-    wg[...] = mm(xT[...], d).astype(BF16)
-    bqg[...] = jnp.sum(d[:, 0:pw].astype(F32), axis=0, keepdims=True)
-    bvg[...] = jnp.sum(d[:, 2 * pw :].astype(F32), axis=0, keepdims=True)
-    part = mm(d, wcat[...], NT)
-
-    @pl.when(step_id == 0)
-    def _():
-        acc[...] = part
-
-    @pl.when((step_id > 0) & (step_id < pl.num_programs(0) - 1))
-    def _():
-        acc[...] += part
-
-    @pl.when(step_id == pl.num_programs(0) - 1)
-    def _():
-        total = acc[...] + part
-        igo[...] = total[:half]
-        igt[...] = total[half:].astype(BF16)
-
-
-def attn_bwd(sc, xo, xt, wq, wk, wv, q, k, v, probs, ao, at, go, gt):
-    half, width = xo.shape
-    rows = 2 * half
-    pairs = HEADS // 4
-    pw = 2 * HD
-    whole = lambda a: pl.BlockSpec(a.shape, lambda p, s: (0,) * a.ndim)
-    wspec = pl.BlockSpec((width, pw), lambda p, s: (0, s[0] * pairs + p))
-    col = lambda r, w: pl.BlockSpec((r, w), lambda p, s: (0, p))
-    return pl.pallas_call(
-        attn_bwd_body,
-        grid_spec=pltpu.PrefetchScalarGridSpec(
-            num_scalar_prefetch=1,
-            grid=(pairs,),
-            in_specs=[whole(xo), whole(xt), wspec, wspec, wspec]
-            + [col(rows, pw)] * 3
-            + [pl.BlockSpec((2, rows, rows), lambda p, s: (p, 0, 0))]
-            + [col(half, pw)] * 4,
-            out_specs=[col(width, 3 * pw), col(1, pw), col(1, pw)]
-            + [pl.BlockSpec((half, width), lambda p, s: (0, 0))] * 2,
-            scratch_shapes=[
-                pltpu.VMEM((rows, pw), BF16),
-                pltpu.VMEM((pw, rows), BF16),
-                pltpu.VMEM((pw, rows), BF16),
-                pltpu.VMEM((pw, rows), F32),
-                pltpu.VMEM((pw, rows), F32),
-                pltpu.VMEM((rows, 3 * pw), BF16),
-                pltpu.VMEM((width, 3 * pw), BF16),
-                pltpu.VMEM((width, rows), BF16),
-                pltpu.VMEM((rows, width), F32),
-            ],
-        ),
-        out_shape=[
-            shape((width, 3 * pw * pairs), BF16),
-            shape((1, pw * pairs), F32),
-            shape((1, pw * pairs), F32),
-            shape((half, width), F32),
-            shape((half, width), BF16),
-        ],
-        compiler_params=params(),
-        cost_estimate=cost(40e9, 20e6),
-        name="attn_bwd",
-    )(sc, xo, xt, wq, wk, wv, q, k, v, probs, ao, at, go, gt)
-
-
 def partner_copy(src, dst, send, recv, me):
     return pltpu.make_async_remote_copy(
         src_ref=src, dst_ref=dst, send_sem=send, recv_sem=recv,
         device_id={"mp": 1 - me}, device_id_type=pl.DeviceIdType.MESH,
     )
+
+
+class Piece:
+    def __init__(self, x_first, sems, base, refs, dp_size):
+        self.x_first = x_first
+        self.send, self.recv = sems
+        self.base = base
+        self.half, self.got1, self.mine, self.got2, self.got3 = refs
+        me = lax.axis_index("dp")
+        bits = (me % 2, (me // 2) % 2)
+        steps = (1, 2)
+        self.groups = dp_size // 4
+        self.high = me // 4
+        first, second = (0, 1) if x_first else (1, 0)
+        self.bit1, self.bit2 = bits[first], bits[second]
+        self.peer1 = me + steps[first] * (1 - 2 * bits[first])
+        self.peer2 = me + steps[second] * (1 - 2 * bits[second])
+        self.peers3 = [
+            ((self.high + s) % self.groups, ((self.high + s) % self.groups) * 4 + me % 4)
+            for s in range(1, self.groups)
+        ]
+
+    def copy(self, src, dst, i, peer):
+        return pltpu.make_async_remote_copy(
+            src_ref=src, dst_ref=dst, send_sem=self.send.at[self.base + i],
+            recv_sem=self.recv.at[self.base + i], device_id={"dp": peer},
+            device_id_type=pl.DeviceIdType.MESH,
+        )
+
+    def side(self, src, bit):
+        return src.at[:, :, bit] if self.x_first else src.at[:, bit]
+
+    def stage1(self, src):
+        return self.copy(self.side(src, 1 - self.bit1), self.got1, 0, self.peer1)
+
+    def stage2(self, src=None):
+        src = self.half if src is None else src
+        return self.copy(src.at[:, 1 - self.bit2], self.got2, 1, self.peer2)
+
+    def stage3(self):
+        return [
+            self.copy(self.mine.at[z], self.got3.at[s], 2 + s, peer)
+            for s, (z, peer) in enumerate(self.peers3)
+        ]
+
+    def add1(self, own):
+        def step(z, carry):
+            total = own(z).astype(F32) + self.got1[z].astype(F32)
+            self.half[z] = total.astype(BF16)
+            return carry
+
+        lax.fori_loop(0, self.groups, step, 0)
+
+    def add2(self, own=None):
+        def step(z, carry):
+            kept = self.half[z, self.bit2] if own is None else own(z)
+            self.mine[z] = (kept.astype(F32) + self.got2[z].astype(F32)).astype(BF16)
+            return carry
+
+        lax.fori_loop(0, self.groups, step, 0)
+
+    def result(self):
+        total = self.mine[self.high].astype(F32)
+        for s in range(self.groups - 1):
+            total = total + self.got3[s].astype(F32)
+        return total
 
 
 def gelu_and_slope(v):
@@ -273,27 +222,32 @@
 
 
 def middle_body(
-    a_own, a_send, x, gout, b_output, gain1, shift1, b_in, b_out, gain2, shift2,
+    dp_size, a_own, a_send, x, gout, b_output, gain1, shift1, b_in, b_out, gain2, shift2,
     w_o_h, w_in_h, w_out_h,
-    out_o, gsum_o, ga_o, gat_o, wout_g, win_g, wo_g, vec_o, bi_o,
-    a_got, fl, feed_s, feed_g, gf, part_s, part_g, gat_s, gb, wo_s, wo_r, vec_s, vec_r, bi_s,
+    out_o, gsum_o, ga_o, gat_o, sa1, sa2, win_g, wo_g, vec_o, bi_o,
+    a_got, fl, feed_s, feed_g, gf, part_s, part_g, gat_s, gb, wo_s, wo_r, vec_s, vec_r, bi_s, bi_s2, bi_r, wout_g, got_a1, got_a2,
     w_o, w_in, w_out, act, slope, gh, u_s, first_s, own_s, gtwo_s,
-    load_sem, send_sem, recv_sem,
+    load_sem, send_sem, recv_sem, a_send_sem, a_recv_sem,
 ):
     me = lax.axis_index("mp")
     half, width = x.shape
     hw = width // 2
     tile = 256
     tiles = half // tile
+    cut = sa1.shape[-1]
+    sems = (a_send_sem, a_recv_sem)
+    A1 = Piece(True, sems, 0, (sa1, got_a1, None, None, None), dp_size)
+    A2 = Piece(False, sems, 1, (sa2, got_a2, None, None, None), dp_size)
+    A1_copy = A1.stage1(wout_g.at[:, :, :, :, :cut])
+    A2_copy = A2.stage1(wout_g.at[:, :, :, :, cut:])
     barrier = pltpu.get_barrier_semaphore()
-    pl.semaphore_signal(
-        barrier, inc=1, device_id={"mp": 1 - me}, device_id_type=pl.DeviceIdType.MESH
-    )
+    for device in ({"mp": 1 - me}, {"dp": A1.peer1}, {"dp": A2.peer1}):
+        pl.semaphore_signal(barrier, inc=1, device_id=device, device_id_type=pl.DeviceIdType.MESH)
     loads = []
     for i, (src, dst) in enumerate(((w_o_h, w_o), (w_in_h, w_in), (w_out_h, w_out))):
         loads.append(pltpu.make_async_copy(src, dst, load_sem.at[i]))
         loads[-1].start()
-    pl.semaphore_wait(barrier, 1)
+    pl.semaphore_wait(barrier, 3)
 
     def copy(src, dst, i):
         return partner_copy(src, dst, send_sem.at[i], recv_sem.at[i], me)
@@ -328,9 +282,9 @@
         r = rows(t)
         u = x[r, :].astype(F32) + (
             mm(a_own[r, :], w_o[own_o, :]) + mm(a_got[r, :], w_o[got_o, :])
-        ) + b_output[...].astype(F32)
+        ) + b_output[...].astype(F32)[None, :]
         n, _ = row_stats(u)
-        first = n * gain1[...].astype(F32) + shift1[...].astype(F32)
+        first = n * gain1[...].astype(F32)[None, :] + shift1[...].astype(F32)[None, :]
         u_s[r, :] = u
         first_s[r, :] = first
         fl[0, r, :] = first.astype(BF16)
@@ -343,7 +297,7 @@
 
     def feed_forward(i, t):
         r = rows(t)
-        v = mm(fl[i, r, :], w_in[...]) + b_in[...].astype(F32)
+        v = mm(fl[i, r, :], w_in[...]) + b_in[...].astype(F32)[None, :]
         a, s = gelu_and_slope(v)
         a = a.astype(BF16)
         act[i, r, :] = a
@@ -371,19 +325,19 @@
     def second_norm(t, carry):
         r = rows(t)
         feed_copy(t).wait_recv()
-        u = first_s[r, :] + (own_s[r, :] + feed_g[r, :].astype(F32)) + b_out[...].astype(F32)
+        u = first_s[r, :] + (own_s[r, :] + feed_g[r, :].astype(F32)) + b_out[...].astype(F32)[None, :]
         n, rs = row_stats(u)
-        gain = gain2[...].astype(F32)
-        out_o[r, :] = (n * gain + shift2[...].astype(F32)).astype(BF16)
+        gain = gain2[...].astype(F32)[None, :]
+        out_o[r, :] = (n * gain + shift2[...].astype(F32)[None, :]).astype(BF16)
         e = gout[r, :].astype(F32)
         d = norm_back(e, n, rs, gain)
         low = d.astype(BF16)
         gtwo_s[r, :] = d
         gf[0, r, :] = low
         gf_copy(t).start()
-        add_vec(4, e * n)
-        add_vec(5, e)
-        add_vec(3, low.astype(F32))
+        add_vec(6, e * n)
+        add_vec(7, e)
+        add_vec(5, low.astype(F32))
         return carry
 
     lax.fori_loop(0, tiles, second_norm, 0)
@@ -400,13 +354,28 @@
         own_s[rows(t), :] = feed_back(0, t)
         return carry
 
+    def wait_gf(t, carry):
+        gf_copy(t).wait_recv()
+        return carry
+
     def back_got(t, carry):
-        gf_copy(t).wait_recv()
         part_s[rows(t), :] = feed_back(1, t).astype(BF16)
         part_copy(t).start()
         return carry
 
     lax.fori_loop(0, tiles, back_own, 0)
+    lax.fori_loop(0, tiles, wait_gf, 0)
+
+    def out_weights(j, carry):
+        c = pl.ds(pl.multiple_of(j * hw, hw), hw)
+        total = mm(gf[0, :, c], act[0], TN) + mm(gf[1, :, c], act[1], TN)
+        zs = wout_g.shape[0] // 2
+        wout_g[pl.ds(j * zs, zs)] = total.astype(BF16).reshape((zs,) + wout_g.shape[1:])
+        return carry
+
+    lax.fori_loop(0, 2, out_weights, 0)
+    A1_copy.start()
+    A2_copy.start()
     lax.fori_loop(0, tiles, back_got, 0)
 
     def weights(out, lhs, rhs):
@@ -419,7 +388,6 @@
 
         lax.fori_loop(0, width // tile, step, 0)
 
-    weights(wout_g, gf, act)
     weights(win_g, fl, gh)
 
     def first_norm(t, carry):
@@ -427,22 +395,24 @@
         part_copy(t).wait_recv()
         e = gtwo_s[r, :] + own_s[r, :] + part_g[r, :].astype(F32)
         n, rs = row_stats(u_s[r, :])
-        d = norm_back(e, n, rs, gain1[...].astype(F32))
+        d = norm_back(e, n, rs, gain1[...].astype(F32)[None, :])
         low = d.astype(BF16)
         gsum_o[r, :] = d
         gb[r, :] = low
         gat_s[r, :] = mm(low, w_o[got_o, :], NT).astype(BF16)
         ga_copy(t).start()
         ga_o[r, :] = mm(low, w_o[own_o, :], NT).astype(BF16)
-        add_vec(1, e * n)
-        add_vec(2, e)
-        add_vec(0, low.astype(F32))
+        add_vec(3, e * n)
+        add_vec(4, e)
+        add_vec(2, low.astype(F32))
         return carry
 
     lax.fori_loop(0, tiles, first_norm, 0)
     vec_copy = copy(vec_s, vec_r, 11)
     vec_copy.start()
-    bi_copy = copy(bi_s, bi_o.at[1], 12)
+    bi_s2[0:1, :] = bi_s[0:1, :width]
+    bi_s2[1:2, :] = bi_s[0:1, width:]
+    bi_copy = copy(bi_s2, bi_r, 12)
     bi_copy.start()
     cols_own = own_o
     cols_got = got_o
@@ -452,13 +422,20 @@
     wo_copy.start()
     own_part = mm(a_own[...], gb[:, cols_own], TN)
     got_part = mm(a_got[...], gb[:, cols_own], TN)
-    bi_o[0] = bi_s[...]
     wo_copy.wait_recv()
     wo_g[own_o, :] = (own_part + wo_r[own_o, :].astype(F32)).astype(BF16)
     wo_g[got_o, :] = (got_part + wo_r[got_o, :].astype(F32)).astype(BF16)
     vec_copy.wait_recv()
     vec_o[...] = vec_s[...] + vec_r[...]
     bi_copy.wait_recv()
+    bi_o[...] = jnp.zeros_like(bi_o)
+    first_core = me == 0
+    bi_o[0:2, :] = jnp.where(first_core, bi_s2[0:2, :], bi_r[0:2, :])
+    bi_o[2:4, :] = jnp.where(first_core, bi_r[0:2, :], bi_s2[0:2, :])
+    A1_copy.wait_recv()
+    A1.add1(lambda z: wout_g[z, :, A1.bit1, :, :cut])
+    A2_copy.wait_recv()
+    A2.add1(lambda z: wout_g[z, A2.bit1, :, :, cut:])
 
     def finish(t, carry):
         ga_copy(t).wait_recv()
@@ -471,32 +448,37 @@
 
     lax.fori_loop(0, tiles, finish, 0)
     a_copy.wait_send()
+    A1_copy.wait_send()
+    A2_copy.wait_send()
     vec_copy.wait_send()
     bi_copy.wait_send()
     wo_copy.wait_send()
 
 
-def middle(a_own, a_send, x, gout, b_output, gain1, shift1, b_in, b_out, gain2, shift2, w_o, w_in, w_out):
+def middle(dp_size, a_own, a_send, x, gout, b_output, gain1, shift1, b_in, b_out, gain2, shift2, w_o, w_in, w_out):
     half, width = x.shape
     hw = width // 2
     ff = w_in.shape[1]
+    groups = dp_size // 4
+    n = width // dp_size
     vm = pl.BlockSpec(memory_space=pltpu.VMEM)
     hbm = pl.BlockSpec(memory_space=pl.ANY)
     V = pltpu.VMEM
     return pl.pallas_call(
-        middle_body,
+        functools.partial(middle_body, dp_size),
         in_specs=[vm] * 11 + [hbm] * 3,
-        out_specs=[vm] * 9,
+        out_specs=[vm] * 10,
         out_shape=[
             shape((half, width), BF16),
             shape((half, width), F32),
             shape((half, hw), BF16),
             shape((half, hw), BF16),
-            shape((width, ff), BF16),
+            shape((groups, 2, n, ff // 2), BF16),
+            shape((groups, 2, n, ff // 2), BF16),
             shape((width, ff), BF16),
             shape((width, hw), BF16),
             shape((8, width), F32),
-            shape((2, 8, ff), F32),
+            shape((8, width), F32),
         ],
         scratch_shapes=[
             V((half, hw), BF16),
@@ -513,6 +495,11 @@
             V((8, width), F32),
             V((8, width), F32),
             V((8, ff), F32),
+            V((8, width), F32),
+            V((8, width), F32),
+            V((groups, 2, 2, n, ff), BF16),
+            V((groups, 2, n, ff // 2), BF16),
+            V((groups, 2, n, ff // 2), BF16),
             V((width, width), BF16),
             V((width, ff), BF16),
             V((width, ff), BF16),
@@ -526,49 +513,362 @@
             pltpu.SemaphoreType.DMA((3,)),
             pltpu.SemaphoreType.DMA((14,)),
             pltpu.SemaphoreType.DMA((14,)),
+            pltpu.SemaphoreType.DMA((2,)),
+            pltpu.SemaphoreType.DMA((2,)),
         ],
         compiler_params=pltpu.CompilerParams(
-            vmem_limit_bytes=60 << 20, collective_id=1, has_side_effects=True
+            vmem_limit_bytes=62 << 20, collective_id=1, has_side_effects=True
         ),
         cost_estimate=cost(17e9, 20e6),
         name="middle",
     )(a_own, a_send, x, gout, b_output, gain1, shift1, b_in, b_out, gain2, shift2, w_o, w_in, w_out)
 
 
-def pick(a, index, axis):
-    return lax.dynamic_index_in_dim(a, index, axis, keepdims=False)
-
-
-def halve(parts, size, bit_axis, stride):
-    me = lax.axis_index("dp")
-    mine = (me // stride) % 2
-    pairs = [(i, i ^ stride) for i in range(size)]
-    got = lax.ppermute(pick(parts, 1 - mine, bit_axis), "dp", pairs)
-    return (pick(parts, mine, bit_axis).astype(F32) + got.astype(F32)).astype(parts.dtype)
-
-
-def sum_rest(parts, size):
-    groups = size // 4
-    me = lax.axis_index("dp")
-    high = me // 4
-    total = pick(parts, high, 0).astype(F32)
-    for s in range(1, groups):
-        perm = [(i, (i + 4 * s) % size) for i in range(size)]
-        got = lax.ppermute(pick(parts, (high + s) % groups, 0), "dp", perm)
-        total = total + got.astype(F32)
-    return total
-
-
-def sum_sequences(grad, size, x_first):
-    rows = grad.shape[0]
-    parts = grad.reshape(size // 4, 2, 2, rows // size, grad.shape[1])
-    if x_first:
-        parts = halve(parts, size, 2, 1)
-        parts = halve(parts, size, 1, 2)
-    else:
-        parts = halve(parts, size, 1, 2)
-        parts = halve(parts, size, 1, 1)
-    return sum_rest(parts, size)
+def back_body(
+    dp_size, xo, xt, q_i, k_i, v_i, p_i, ao, at, go, gt, gsum, vec, bi,
+    wq, wk, wv, sa1, sa2, win, wo,
+    ig_o, wq_o, wk_o, wv_o, wo_o, win_o, wout_o, o0, o1, o2, o3, o4, o5, o6, o7, bi_o,
+    g_s, gT, qT, dkT, dvT, dqkv, wcat, xT, acc, ig_s, ig_r, wsrc,
+    a1, a2, b1, b2, w1, c0, c1, c2, c3,
+    tb, tb_m, t0, t1, t2, r0_, r1_, r2_,
+    send, recv, lsem, vsend, vrecv, wsem,
+):
+    half, width = xo.shape
+    rows = 2 * half
+    pw = 2 * HD
+    tile = 256
+    p = pl.program_id(0)
+    me = lax.axis_index("mp")
+    dev = lax.axis_index("dp")
+    groups = dp_size // 4
+    per = 2 + groups - 1
+    sems = (send, recv)
+    cut = win.shape[-1] // 2
+    piece = lambda i, xf, refs: Piece(xf, sems, i * per, refs, dp_size)
+    A1, A2 = piece(0, True, (None, None) + a1), piece(1, False, (None, None) + a2)
+    B1, B2 = piece(2, True, b1), piece(3, False, b2)
+    WO = piece(4, False, w1)
+    C0, C1 = piece(5, True, c0), piece(6, False, c1)
+    C2, C3 = piece(7, True, c2), piece(8, False, c3)
+    win1, win2 = win.at[:, :, :, :, :cut], win.at[:, :, :, :, cut:]
+    src2 = wsrc.at[2, :, :, :, :, : 2 * pw]
+    src3 = wsrc.at[2, :, :, :, :, 2 * pw :]
+    locals_ = [
+        (sa1.at[:, A1.bit2], A1.mine),
+        (sa2.at[:, A2.bit2], A2.mine),
+        (B1.side(win1, B1.bit1), B1.half),
+        (B2.side(win2, B2.bit1), B2.half),
+        (WO.side(wo, WO.bit1), WO.half),
+    ]
+    local = [pltpu.make_async_copy(s, d, lsem.at[i]) for i, (s, d) in enumerate(locals_)]
+    ig_copy = partner_copy(ig_s, ig_r, vsend.at[0], vrecv.at[0], me)
+    tb_copy = partner_copy(tb, tb_m, vsend.at[1], vrecv.at[1], me)
+
+    def vec_copy(src, dst, i, peer):
+        return pltpu.make_async_remote_copy(
+            src_ref=src, dst_ref=dst, send_sem=vsend.at[i], recv_sem=vrecv.at[i],
+            device_id={"dp": peer}, device_id_type=pl.DeviceIdType.MESH,
+        )
+
+    t0_copy = vec_copy(t0, r0_, 2, C2.peer1)
+    t1_copy = vec_copy(t1, r1_, 3, C2.peer2)
+    t2_copies = [vec_copy(t2, r2_.at[s], 4 + s, peer) for s, (_, peer) in enumerate(C2.peers3)]
+
+    @pl.when(p == 0)
+    def _():
+        barrier = pltpu.get_barrier_semaphore()
+        everyone = [{"mp": 1 - me}, {"dp": C0.peer1}, {"dp": C0.peer2}]
+        everyone += [{"dp": peer} for _, peer in C0.peers3]
+        for device in everyone:
+            pl.semaphore_signal(
+                barrier, inc=1, device_id=device, device_id_type=pl.DeviceIdType.MESH
+            )
+        for c in local:
+            c.start()
+        pl.semaphore_wait(barrier, len(everyone))
+        A1.stage2(sa1).start()
+        A2.stage2(sa2).start()
+        B1.stage1(win1).start()
+        B2.stage1(win2).start()
+        WO.stage1(wo).start()
+        xT[:, :half] = xo[...].T
+        xT[:, half:] = xt[...].T
+        tb[...] = jnp.zeros_like(tb)
+
+    c_off = pl.multiple_of(me * (width // 2) + p * pw, pw)
+    w_copies = [
+        pltpu.make_async_copy(
+            w.at[:, pl.ds(c_off, pw)], wcat.at[:, i * pw : (i + 1) * pw], wsem.at[i]
+        )
+        for i, w in enumerate((wq, wk, wv))
+    ]
+    for c in w_copies:
+        c.start()
+    g_s[:half, :] = go[...]
+    g_s[half:, :] = gt[...]
+    gT[...] = g_s[...].T
+    qT[...] = q_i[...].T
+    dkT[...] = jnp.zeros_like(dkT)
+    dvT[...] = jnp.zeros_like(dvT)
+    lane = lax.broadcasted_iota(jnp.int32, (tile, pw), 1)
+    low = lane < HD
+
+    for t in range(rows // tile):
+        rs = slice(t * tile, (t + 1) * tile)
+        a_ref = ao if t * tile < half else at
+        as_ = slice(t * tile % half, t * tile % half + tile)
+        g = g_s[rs, :]
+        ga = g.astype(F32) * a_ref[as_, :].astype(F32)
+        outs = []
+        for h in range(2):
+            mine = low if h == 0 else ~low
+            hs = slice(h * HD, (h + 1) * HD)
+            dp = mm(jnp.where(mine, g, BF16(0)), v_i[...], NT)
+            delta = jnp.sum(jnp.where(mine, ga, 0.0), axis=-1, keepdims=True)
+            pr = p_i[h, rs, :]
+            ds = (pr.astype(F32) * (dp - delta)).astype(BF16)
+            outs.append(mm(ds, k_i[...]))
+            dvT[hs, :] += mm(gT[hs, rs], pr)
+            dkT[hs, :] += mm(qT[hs, rs], ds)
+        dq = jnp.where(low, outs[0], outs[1]) * HD**-0.5
+        dqkv[rs, 0:pw] = dq.astype(BF16)
+
+        if t == 3:
+
+            @pl.when(p == 1)
+            def _():
+                local[0].wait()
+                local[1].wait()
+                for x in (A1, A2):
+                    x.stage2(sa1 if x is A1 else sa2).wait_recv()
+                    x.add2(lambda z, x=x: x.mine[z])
+                    for c in x.stage3():
+                        c.start()
+
+        if t == 1:
+
+            @pl.when(p == 2)
+            def _():
+                for j, (x, s) in enumerate(((B1, win1), (B2, win2), (WO, wo))):
+                    local[2 + j].wait()
+                    x.stage1(s).wait_recv()
+                    x.add1(lambda z, x=x: x.half[z])
+                    x.stage2().start()
+
+    dqkv[:, pw : 2 * pw] = (dkT[...].T * HD**-0.5).astype(BF16)
+    dqkv[:, 2 * pw : 3 * pw] = dvT[...].T.astype(BF16)
+    d = dqkv[...]
+    wg = mm(xT[...], d).astype(BF16).reshape(wsrc.shape[1:])
+    wsrc[p] = wg
+    tb[0:1, pl.ds(c_off, pw)] = jnp.sum(d[:, 0:pw].astype(F32), axis=0, keepdims=True)
+    tb[1:2, pl.ds(c_off, pw)] = jnp.sum(d[:, 2 * pw :].astype(F32), axis=0, keepdims=True)
+
+    @pl.when(p == 0)
+    def _():
+        C0.stage1(wsrc.at[0]).start()
+
+    @pl.when(p == 1)
+    def _():
+        C1.stage1(wsrc.at[1]).start()
+
+    @pl.when(p == 2)
+    def _():
+        C2.stage1(src2).start()
+        C3.stage1(src3).start()
+        tb_copy.start()
+
+    for c in w_copies:
+        c.wait()
+    part = mm(d, wcat[...], NT)
+
+    @pl.when(p == 0)
+    def _():
+        acc[...] = part
+
+    @pl.when(p == 1)
+    def _():
+        acc[...] += part
+
+    @pl.when(p == 2)
+    def _():
+        ig_s[...] = (acc[half:, :] + part[half:]).astype(BF16)
+        ig_copy.start()
+        acc[:half, :] += part[:half]
+
+        def own(j, piece):
+            def get(z):
+                return wsrc[j, z, :, piece.bit1] if piece.x_first else wsrc[j, z, piece.bit1]
+
+            return get
+
+        def forward2(x):
+            x.stage2().wait_recv()
+            x.add2()
+            for c in x.stage3():
+                c.start()
+
+        C0.stage1(wsrc.at[0]).wait_recv()
+        C0.add1(own(0, C0))
+        C0.stage2().start()
+        tb_copy.wait_recv()
+        t0[0:8, :] = tb[...] + tb_m[...] + vec[...]
+        t0[8:16, :] = bi[...]
+        t0_copy.start()
+        forward2(B1)
+        forward2(B2)
+        C1.stage1(wsrc.at[1]).wait_recv()
+        C1.add1(own(1, C1))
+        C1.stage2().start()
+        forward2(WO)
+        t0_copy.wait_recv()
+        t1[...] = t0[...] + r0_[...]
+        t1_copy.start()
+        forward2(C0)
+        C2.stage1(src2).wait_recv()
+        C2.add1(lambda z: wsrc[2, z, :, C2.bit1, :, : 2 * pw])
+        C2.stage2().start()
+        C3.stage1(src3).wait_recv()
+        C3.add1(lambda z: wsrc[2, z, C3.bit1, :, :, 2 * pw :])
+        C3.stage2().start()
+        forward2(C1)
+        t1_copy.wait_recv()
+        t2[...] = t1[...] + r1_[...]
+        for c in t2_copies:
+            c.start()
+        ig_copy.wait_recv()
+        ig_o[...] = gsum[...] + (acc[:half, :] + ig_r[...].astype(F32))
+        forward2(C2)
+        forward2(C3)
+
+        def arrived(x):
+            for c in x.stage3():
+                c.wait_recv()
+            return x.result()
+
+        wout_o[:, :cut] = arrived(A1)
+        wout_o[:, cut:] = arrived(A2)
+        win_o[:, :cut] = arrived(B1)
+        win_o[:, cut:] = arrived(B2)
+        wo_o[...] = arrived(WO)
+        for c in t2_copies:
+            c.wait_recv()
+        table = t2[...]
+        for s in range(groups - 1):
+            table = table + r2_[s]
+        n = width // dp_size
+        m = bi_o.shape[0]
+        vals = table[0:8, 0:n]
+        biv = table[8:9, 0:m]
+        for j in range(1, dp_size):
+            vals = jnp.where(dev == j, table[0:8, j * n : (j + 1) * n], vals)
+            r = 8 + (j * m) // width
+            k = (j * m) % width
+            biv = jnp.where(dev == j, table[r : r + 1, k : k + m], biv)
+        for j, o in enumerate((o0, o1, o2, o3, o4, o5, o6, o7)):
+            o[...] = vals[j]
+        bi_o[...] = biv[0]
+        for j, x in enumerate((C0, C1)):
+            v = arrived(x)
+            cs = slice(j * pw, (j + 1) * pw)
+            for i, o in enumerate((wq_o, wk_o, wv_o)):
+                o[:, cs] = v[:, i * pw : (i + 1) * pw]
+        v = arrived(C2)
+        cs = slice(2 * pw, 3 * pw)
+        wq_o[:, cs] = v[:, :pw]
+        wk_o[:, cs] = v[:, pw:]
+        wv_o[:, cs] = arrived(C3)
+
+        A1.stage2(sa1).wait_send()
+        A2.stage2(sa2).wait_send()
+        for x, s in ((B1, win1), (B2, win2), (WO, wo), (C0, wsrc.at[0]), (C1, wsrc.at[1]), (C2, src2), (C3, src3)):
+            x.stage1(s).wait_send()
+            x.stage2().wait_send()
+        for x in (A1, A2, B1, B2, WO, C0, C1, C2, C3):
+            for c in x.stage3():
+                c.wait_send()
+        ig_copy.wait_send()
+        tb_copy.wait_send()
+        t0_copy.wait_send()
+        t1_copy.wait_send()
+        for c in t2_copies:
+            c.wait_send()
+
+
+def back(dp_size, xo, xt, wq, wk, wv, q, k, v, probs, ao, at, go, gt, gsum, vec, bi, sa1, sa2, win, wo):
+    half, width = xo.shape
+    rows = 2 * half
+    pairs = HEADS // 4
+    pw = 2 * HD
+    ff = win.shape[1]
+    groups = dp_size // 4
+    n = width // dp_size
+    five = lambda a: a.reshape(groups, 2, 2, n, a.shape[-1])
+    whole = lambda a: pl.BlockSpec(
+        a.shape, lambda p: (0,) * a.ndim, pipeline_mode=pl.Buffered(1)
+    )
+    col = lambda r, w: pl.BlockSpec((r, w), lambda p: (0, p))
+    hbm = pl.BlockSpec(memory_space=pl.ANY)
+    vm = pl.BlockSpec(memory_space=pltpu.VMEM)
+    V = pltpu.VMEM
+
+    def late(w):
+        return (V((groups, n, w), BF16), V((groups, n, w), BF16), V((groups - 1, n, w), BF16))
+
+    def bufs(w):
+        return (V((groups, 2, n, w), BF16), V((groups, 2, n, w), BF16)) + late(w)
+
+    fw = ff // 2
+    pieces = 9
+    per = 2 + groups - 1
+    table = lambda: V((16, width), F32)
+    return pl.pallas_call(
+        functools.partial(back_body, dp_size),
+        grid_spec=pltpu.PrefetchScalarGridSpec(
+            num_scalar_prefetch=0,
+            grid=(pairs,),
+            in_specs=[whole(xo), whole(xt)]
+            + [col(rows, pw)] * 3
+            + [pl.BlockSpec((2, rows, rows), lambda p: (p, 0, 0))]
+            + [col(half, pw)] * 4
+            + [whole(gsum), whole(vec), whole(bi)]
+            + [hbm] * 7,
+            out_specs=[vm] * 16,
+            scratch_shapes=[
+                V((rows, pw), BF16),
+                V((pw, rows), BF16),
+                V((pw, rows), BF16),
+                V((pw, rows), F32),
+                V((pw, rows), F32),
+                V((rows, 3 * pw), BF16),
+                V((width, 3 * pw), BF16),
+                V((width, rows), BF16),
+                V((rows, width), F32),
+                V((half, width), BF16),
+                V((half, width), BF16),
+                V((pairs, groups, 2, 2, n, 3 * pw), BF16),
+                late(fw), late(fw), bufs(fw), bufs(fw), bufs(width // 2),
+                bufs(3 * pw), bufs(3 * pw), bufs(2 * pw), bufs(pw),
+                V((8, width), F32), V((8, width), F32),
+                table(), table(), table(), table(), table(), V((groups - 1, 16, width), F32),
+                pltpu.SemaphoreType.DMA((pieces * per,)),
+                pltpu.SemaphoreType.DMA((pieces * per,)),
+                pltpu.SemaphoreType.DMA((5,)),
+                pltpu.SemaphoreType.DMA((4 + groups - 1,)),
+                pltpu.SemaphoreType.DMA((4 + groups - 1,)),
+                pltpu.SemaphoreType.DMA((3,)),
+            ],
+        ),
+        out_shape=[shape((half, width), F32)]
+        + [shape((n, width // 2), F32)] * 4
+        + [shape((n, ff), F32)] * 2
+        + [shape((n,), F32)] * 8
+        + [shape((2 * ff // dp_size,), F32)],
+        compiler_params=pltpu.CompilerParams(
+            vmem_limit_bytes=60 << 20, collective_id=2, has_side_effects=True
+        ),
+        cost_estimate=cost(40e9, 20e6),
+        name="back",
+    )(xo, xt, q, k, v, probs, ao, at, go, gt, gsum, vec, bi, wq, wk, wv, sa1, sa2, five(win), five(wo))
 
 
 def local_pair(
@@ -586,48 +886,20 @@
     q, k, v, probs, a_own, a_send = attn_fwd(
         sc, x, x_got, w_query, w_key, w_value, vec(b_query), vec(b_value), rand
     )
-    out, gsum, ga0, ga_got, w_out_g, w_in_g, w_output_g, vec_g, bi_g = middle(
-        a_own, a_send, x, grad_out[0], vec(b_output), vec(gain_one), vec(shift_one), vec(b_in),
-        vec(b_out), vec(gain_two), vec(shift_two), w_output, w_in, w_out,
-    )
-    wqkv_g, bq_g, bv_g, ig_own, ig_send = attn_bwd(
-        sc, x, x_got, w_query, w_key, w_value, q, k, v, probs, a_own, a_send, ga0, ga_got
-    )
-    input_grad = gsum + (ig_own + swap(ig_send).astype(F32))
-
-    def spread(part, total):
-        return lax.dynamic_update_slice(
-            jnp.zeros((1, total), F32), part, (jnp.int32(0), core * part.shape[1])
-        )
-
-    ff_all = 2 * w_in.shape[1]
-    bqv = jnp.concatenate([spread(bq_g, width), spread(bv_g, width)], axis=0)
-    bqv = bqv + swap(bqv)
-    bi_all = jnp.where(core == 0, bi_g[:, 0], bi_g[::-1, 0]).reshape(dp_size, -1)
-    eight = jnp.concatenate([bqv, vec_g[:6]], axis=0).reshape(8, dp_size, -1)
-    table = jnp.concatenate([eight.transpose(1, 0, 2).reshape(dp_size, -1), bi_all], axis=1)
-    rows = width // dp_size
-    lanes = 2 * HD
-    table = jnp.pad(table, ((0, 0), (0, rows * lanes - table.shape[1])))
-    table = table.astype(BF16).reshape(width, lanes)
-
-    cut = 2 * width // 2
-    late = jnp.concatenate([wqkv_g[:, cut:], w_output_g, table], axis=1)
-    out_part = sum_sequences(w_out_g, dp_size, True)
-    in_part = sum_sequences(w_in_g, dp_size, False)
-    early_part = sum_sequences(wqkv_g[:, :cut], dp_size, True)
-    late_part = sum_sequences(late, dp_size, False)
-
-    qkv = jnp.concatenate([early_part, late_part[:, : wqkv_g.shape[1] - cut]], axis=1)
-    qkv = qkv.reshape(rows, HEADS // 4, 3, 2 * HD)
-    wq_p, wk_p, wv_p = (qkv[:, :, i].reshape(rows, width // 2) for i in range(3))
-    wo_p = late_part[:, wqkv_g.shape[1] - cut :][:, : width // 2]
-    flat = late_part[:, wqkv_g.shape[1] - cut + width // 2 :].reshape(-1)
-    vs = [flat[i * rows : (i + 1) * rows] for i in range(8)]
-    bi_p = flat[8 * rows : 8 * rows + ff_all // dp_size]
+    out, gsum, ga0, ga_got, sa1, sa2, w_in_g, w_output_g, vec_g, bi_g = middle(
+        dp_size, a_own, a_send, x, grad_out[0], b_output, gain_one, shift_one, b_in, b_out,
+        gain_two, shift_two, w_output, w_in, w_out,
+    )
+    (
+        input_grad, wq_p, wk_p, wv_p, wo_p, in_part, out_part, bq_p, bv_p, bo_p, g1_p, s1_p, b2_p,
+        g2_p, s2_p, bi_p,
+    ) = back(
+        dp_size, x, x_got, w_query, w_key, w_value, q, k, v, probs, a_own, a_send, ga0, ga_got,
+        gsum, vec_g, bi_g, sa1, sa2, w_in_g, w_output_g,
+    )
     return (
-        out[None], input_grad[None], wq_p, vs[0], wk_p, wv_p, vs[1], wo_p, vs[2], vs[3], vs[4],
-        in_part, bi_p, out_part, vs[5], vs[6], vs[7],
+        out[None], input_grad[None], wq_p, bq_p, wk_p, wv_p, bv_p, wo_p, bo_p, g1_p, s1_p,
+        in_part, bi_p, out_part, b2_p, g2_p, s2_p,
     )
 
 

time: 228 us -> 166 us (0.73)
  waiting for transfers between devices: 70.3 us -> 0.01 us
  Pallas kernels: 89 us -> 147 us
  starting transfers between devices: 29.9 us -> 0.58 us
  local copies, waits for them, and re-layouts: 26.4 us -> 16.3 us
  other arithmetic: 10.1 us -> 0.66 us
    ppermute x20 -> x0, waiting for transfers between devices: 70.3 us -> none  [the longest x8 45.3 us: halve(): got = lax.ppermute(pick(parts, 1 - mine, bit_axis), 'dp', pairs)]
    pallas_call x2, Pallas kernels: 62.9 us -> 121 us  [the longest x1 79.6 us: back(): pl.pallas_call(functools.partial(back_body, dp_size), grid_spec=pltpu.Pre...]
    ppermute x20 -> x0, starting transfers between devices: 28.7 us -> none  [the longest x12 15.8 us: sum_rest(): got = lax.ppermute(pick(parts, (high + s) % groups, 0), 'dp', perm)]
    unnamed x23 -> x54, local copies, waits for them, and re-layouts: 3.2 us -> 13.1 us
    reshape x9 -> x2, local copies, waits for them, and re-layouts: 11.4 us -> 2.53 us  [local_pair(): vec = lambda a: a.reshape(1, -1)]
    slice x8 -> x0, local copies, waits for them, and re-layouts: 5.98 us -> none  [the longest x1 1.5 us: local_pair(): early_part = sum_sequences(wqkv_g[:, :cut], dp_size, True)]
    convert_element_type x8 -> x0, other arithmetic: 3.91 us -> none  [halve(): (pick(parts, mine, bit_axis).astype(F32) + got.astype(F32)).astype(parts....]
    dynamic_slice x7 -> x0, local copies, waits for them, and re-layouts: 3.76 us -> none  [pick(): return lax.dynamic_index_in_dim(a, index, axis, keepdims=False)]
  transfers between devices with their start and end apart: 24 -> 2, of which waited for: 10 -> 0; matrix products, arithmetic and copies ran while one was open for 13% -> 3% of each run, Pallas kernels for 0% -> 0%
where the time goes in v3:
time: 166 us
  Pallas kernels  147 us (89%)
  local copies, waits for them, and re-layouts  16.3 us (10%)
    pallas_call x1, Pallas kernels, back(): pl.pallas_call(functools.partial(back_body, dp_size), grid_spec=pltpu.Pre...  79.6 us
    pallas_call x1, Pallas kernels, middle(): pl.pallas_call(functools.partial(middle_body, dp_size), in_specs=[vm] * 1...  41.7 us
    pallas_call x1, Pallas kernels, attn_fwd(): pl.pallas_call(attn_fwd_body, grid_spec=pltpu.PrefetchScalarGridSpec(num_...  26 us
    unnamed x54, local copies, waits for them, and re-layouts  13.1 us
  transfers between devices with their start and end apart: 2, of which 0 were waited for; matrix products, arithmetic and copies ran while one was open for 3% of the time, Pallas kernels for 0%

profile of v3, /device:TPU:0, one launch (start us, length us, event | category | flops | bytes accessed | tf_op | source)
XLA Modules:
  0.0 166.2 jit_solution(6288316789355003892)
XLA Ops:
  0.7 0.5 collective-permute-start
  1.2 0.7 copy.41
  1.9 0.1 collective-permute-start.1
  2.6 1.3 reshape.46.bq
  3.8 0.6 pad_add_fusion.1.sc
  4.4 1.3 reshape.47.bv
  5.7 0.0 collective-permute-done.1
  5.7 0.1 pad_add_fusion
  5.8 0.7 copy.38.rand
  6.4 0.0 collective-permute-done.xt
  6.4 0.9 copy-done.9
  7.3 26.0 %attn_fwd.1 = (bf16[1024,384]{1,0:T(8,128)(2,1)}, bf16[1024,384]{1,0:T(8,128)(2,1)}, bf16[1024,384]{1,0:T(8,128)(2,1)}, bf16[6,1024,1024]{2,1,0:T(8,128)(2,1)}, ...) custom-call(s32[2]{0:T(128)} %pad_add_fusion.1.sc, bf16[512,768]{1,0:T(8,128)(2,1)} %bitcast.16, ...), custom_call_target="tpu_custom_call" | custom-call | flops 20000000000 | bytes 20000000 | tf_op jit(solution)/shard_map/attn_fwd/pallas_call | solution.py:117
  33.3 41.7 %middle.1 = (bf16[512,768]{1,0:T(8,128)(2,1)}, f32[512,768]{1,0:T(8,128)}, bf16[512,384]{1,0:T(8,128)(2,1)}, bf16[512,384]{1,0:T(8,128)(2,1)}, bf16[4,2,48,768]{...) custom-call(bf16[512,384]{1,0:T(8,128)(2,1)} %get-tuple-element.49.a, ...), custom_call_target="tpu_custom_call" | custom-call | flops 16999999488 | bytes 20000000 | tf_op jit(solution)/shard_map/middle/pallas_call | solution.py:467
  75.0 79.6 %back.1 = (f32[512,768]{1,0:T(8,128)}, f32[48,384]{1,0:T(8,128)}, f32[48,384]{1,0:T(8,128)}, f32[48,384]{1,0:T(8,128)}, f32[48,384]{1,0:T(8,128)}, /*index=5*/f3...) custom-call(bf16[512,768]{1,0:T(8,128)(2,1)} %bitcast.18, ...), custom_call_target="tpu_custom_call" | custom-call | flops 40000000000 | bytes 20000000 | tf_op jit(solution)/shard_map/back/pallas_call | solution.py:824
  154.6 0.9 copy.60
  155.5 0.8 copy-done
  156.4 1.1 copy.61
  157.5 0.6 copy.62
  158.2 0.5 copy.63
  158.7 0.6 copy.64
  159.3 0.6 copy.65
  159.9 0.5 copy.66
  160.5 0.6 copy.67
  161.1 0.5 copy.68
  161.6 0.5 copy.69
  162.1 0.5 copy.70
  162.6 0.7 copy.71
  163.4 0.6 copy.72
  163.9 0.7 copy.73
  164.6 0.5 copy.74
  165.2 0.5 copy.75
  165.7 0.5 copy.76
  (34 shorter events, 0.1 us)
Async XLA Ops:
  0.7 5.8 %collective-permute-start = (bf16[512,768]{1,0:T(8,128)(2,1)}, bf16[512,768]{1,0:T(8,128)(2,1)S(1)}, u32[]{:S(2)}, u32[]{:S(2)}) collective-permute-start(bf16[512,768]{1,0:T(8,128)(2,1)} %bitcast.15), channel_id=1, source_target_pairs={{0,1},{1,0},{2,3},{3,2},{4,5},{5,4},{6,7},{7,6},{8,9},{9,8},{10,11... | collective-permute-start | bytes 2359304 | tf_op jit(solution)/shard_map/ppermute | solution.py:879
  1.9 3.8 %collective-permute-start.1 = (s32[8,3]{0,1:T(4,128)S(1)}, s32[8,3]{0,1:T(4,128)S(1)}, u32[]{:S(2)}, u32[]{:S(2)}) collective-permute-start(s32[8,3]{0,1:T(4,128)S(1)} %bitcast.12), channel_id=1, source_target_pairs={{0,1},{1,0},{2,3},{3,2},{4,5},{5,4},{6,7},{7,6},{8,9},{9,8},{10,11... | collective-permute-start | bytes 296 | tf_op jit(solution)/shard_map/ppermute | solution.py:879
  6.4 0.9 copy-start.9
  75.0 79.6 %copy-start.1 = (bf16[512,768]{1,0:T(8,128)(2,1)S(1)}, bf16[512,768]{1,0:T(8,128)(2,1)}, u32[]{:S(2)}) copy-start(bf16[512,768]{1,0:T(8,128)(2,1)} %get-tuple-element.51) | copy-start | bytes 2359300
  154.6 1.7 %copy-start = (f32[512,768]{1,0:T(8,128)S(1)}, f32[512,768]{1,0:T(8,128)}, u32[]{:S(2)}) copy-start(f32[512,768]{1,0:T(8,128)} %get-tuple-element.65) | copy-start | bytes 4718596
  156.3 1.2 copy-start.7
  156.3 1.9 %copy-start.17 = (f32[48]{0:T(128)S(1)}, f32[48]{0:T(128)}, u32[]{:S(2)}) copy-start(f32[48]{0:T(128)} %get-tuple-element.101) | copy-start | bytes 580
  156.3 2.4 %copy-start.6 = (f32[48,384]{1,0:T(8,128)S(1)}, f32[48,384]{1,0:T(8,128)}, u32[]{:S(2)}) copy-start(f32[48,384]{1,0:T(8,128)} %get-tuple-element.102) | copy-start | bytes 221188
  156.3 3.0 %copy-start.5 = (f32[48,384]{1,0:T(8,128)S(1)}, f32[48,384]{1,0:T(8,128)}, u32[]{:S(2)}) copy-start(f32[48,384]{1,0:T(8,128)} %get-tuple-element.103) | copy-start | bytes 221188
  156.3 3.7 %copy-start.16 = (f32[48]{0:T(128)S(1)}, f32[48]{0:T(128)}, u32[]{:S(2)}) copy-start(f32[48]{0:T(128)} %get-tuple-element.104) | copy-start | bytes 580
  156.3 4.2 %copy-start.4 = (f32[48,384]{1,0:T(8,128)S(1)}, f32[48,384]{1,0:T(8,128)}, u32[]{:S(2)}) copy-start(f32[48,384]{1,0:T(8,128)} %get-tuple-element.105) | copy-start | bytes 221188
  156.3 4.8 %copy-start.15 = (f32[48]{0:T(128)S(1)}, f32[48]{0:T(128)}, u32[]{:S(2)}) copy-start(f32[48]{0:T(128)} %get-tuple-element.106) | copy-start | bytes 580
  156.3 5.3 %copy-start.14 = (f32[48]{0:T(128)S(1)}, f32[48]{0:T(128)}, u32[]{:S(2)}) copy-start(f32[48]{0:T(128)} %get-tuple-element.107) | copy-start | bytes 580
  156.3 5.8 %copy-start.13 = (f32[48]{0:T(128)S(1)}, f32[48]{0:T(128)}, u32[]{:S(2)}) copy-start(f32[48]{0:T(128)} %get-tuple-element.108) | copy-start | bytes 580
  156.3 6.3 %copy-start.3 = (f32[48,1536]{1,0:T(8,128)S(1)}, f32[48,1536]{1,0:T(8,128)}, u32[]{:S(2)}) copy-start(f32[48,1536]{1,0:T(8,128)} %get-tuple-element.109) | copy-start | bytes 884740
  156.3 7.0 %copy-start.8 = (f32[192]{0:T(256)S(1)}, f32[192]{0:T(256)}, u32[]{:S(2)}) copy-start(f32[192]{0:T(256)} %get-tuple-element.110) | copy-start | bytes 2308
  156.4 7.6 %copy-start.2 = (f32[48,1536]{1,0:T(8,128)S(1)}, f32[48,1536]{1,0:T(8,128)}, u32[]{:S(2)}) copy-start(f32[48,1536]{1,0:T(8,128)} %get-tuple-element.111) | copy-start | bytes 884740
  157.5 7.1 %copy-start.12 = (f32[48]{0:T(128)S(1)}, f32[48]{0:T(128)}, u32[]{:S(2)}) copy-start(f32[48]{0:T(128)} %get-tuple-element.112) | copy-start | bytes 580
  157.5 7.6 %copy-start.11 = (f32[48]{0:T(128)S(1)}, f32[48]{0:T(128)}, u32[]{:S(2)}) copy-start(f32[48]{0:T(128)} %get-tuple-element.113) | copy-start | bytes 580
  157.5 8.2 %copy-start.10 = (f32[48]{0:T(128)S(1)}, f32[48]{0:T(128)}, u32[]{:S(2)}) copy-start(f32[48]{0:T(128)} %get-tuple-element.114) | copy-start | bytes 580

commit v4 on v3

--- a/solution.py
+++ b/solution.py
@@ -142,69 +142,80 @@
 
 
 class Piece:
-    def __init__(self, x_first, sems, base, refs, dp_size):
-        self.x_first = x_first
-        self.send, self.recv = sems
+    def __init__(self, bits, sems, base, src, got, kept, stage0=0):
+        self.bits = bits
+        self.send, self.recv, self.load = sems
         self.base = base
-        self.half, self.got1, self.mine, self.got2, self.got3 = refs
-        me = lax.axis_index("dp")
-        bits = (me % 2, (me // 2) % 2)
-        steps = (1, 2)
-        self.groups = dp_size // 4
-        self.high = me // 4
-        first, second = (0, 1) if x_first else (1, 0)
-        self.bit1, self.bit2 = bits[first], bits[second]
-        self.peer1 = me + steps[first] * (1 - 2 * bits[first])
-        self.peer2 = me + steps[second] * (1 - 2 * bits[second])
-        self.peers3 = [
-            ((self.high + s) % self.groups, ((self.high + s) % self.groups) * 4 + me % 4)
-            for s in range(1, self.groups)
-        ]
-
-    def copy(self, src, dst, i, peer):
+        self.src, self.got, self.kept = src, got, kept
+        self.stage0 = stage0
+        self.dev = lax.axis_index("dp")
+
+    def mine(self, k):
+        return (self.dev // 2 ** self.bits[k]) % 2
+
+    def peer(self, k):
+        return self.dev + 2 ** self.bits[k] * (1 - 2 * self.mine(k))
+
+    def side(self, k, bit, lead=None):
+        left = sorted(self.bits[k:], reverse=True)
+        where = left.index(self.bits[k])
+        idx = [slice(None)] * len(left) if lead is None else list(lead[:where]) + [None] + list(lead[where:])
+        idx[where] = bit
+        return tuple(idx)
+
+    def source(self, k):
+        return self.src if k == self.stage0 else self.kept[k - 1]
+
+    def copy(self, k):
+        i = self.base + k
         return pltpu.make_async_remote_copy(
-            src_ref=src, dst_ref=dst, send_sem=self.send.at[self.base + i],
-            recv_sem=self.recv.at[self.base + i], device_id={"dp": peer},
-            device_id_type=pl.DeviceIdType.MESH,
+            src_ref=self.source(k).at[self.side(k, 1 - self.mine(k))], dst_ref=self.got[k],
+            send_sem=self.send.at[i], recv_sem=self.recv.at[i],
+            device_id={"dp": self.peer(k)}, device_id_type=pl.DeviceIdType.MESH,
         )
 
-    def side(self, src, bit):
-        return src.at[:, :, bit] if self.x_first else src.at[:, bit]
-
-    def stage1(self, src):
-        return self.copy(self.side(src, 1 - self.bit1), self.got1, 0, self.peer1)
-
-    def stage2(self, src=None):
-        src = self.half if src is None else src
-        return self.copy(src.at[:, 1 - self.bit2], self.got2, 1, self.peer2)
-
-    def stage3(self):
-        return [
-            self.copy(self.mine.at[z], self.got3.at[s], 2 + s, peer)
-            for s, (z, peer) in enumerate(self.peers3)
-        ]
-
-    def add1(self, own):
-        def step(z, carry):
-            total = own(z).astype(F32) + self.got1[z].astype(F32)
-            self.half[z] = total.astype(BF16)
+    def load_own(self):
+        k = self.stage0
+        return pltpu.make_async_copy(
+            self.src.at[self.side(k, self.mine(k))], self.kept[k], self.load.at[self.base // len(self.bits)]
+        )
+
+    def total(self, k, lead, loaded):
+        if loaded:
+            own = self.kept[k][lead]
+        else:
+            own = self.source(k)[self.side(k, self.mine(k), lead)]
+        return own.astype(F32) + self.got[k][lead].astype(F32)
+
+    def add(self, k, loaded=False):
+        free = len(self.bits) - 1 - k
+
+        def step(i, carry):
+            lead = tuple((i // 2 ** (free - 1 - j)) % 2 for j in range(free))
+            self.kept[k][lead] = self.total(k, lead, loaded).astype(BF16)
             return carry
 
-        lax.fori_loop(0, self.groups, step, 0)
-
-    def add2(self, own=None):
-        def step(z, carry):
-            kept = self.half[z, self.bit2] if own is None else own(z)
-            self.mine[z] = (kept.astype(F32) + self.got2[z].astype(F32)).astype(BF16)
-            return carry
-
-        lax.fori_loop(0, self.groups, step, 0)
+        lax.fori_loop(0, 2**free, step, 0)
+
+    def forward(self, k, loaded=False):
+        self.copy(k).wait_recv()
+        self.add(k, loaded)
+        self.copy(k + 1).start()
 
     def result(self):
-        total = self.mine[self.high].astype(F32)
-        for s in range(self.groups - 1):
-            total = total + self.got3[s].astype(F32)
-        return total
+        k = len(self.bits) - 1
+        self.copy(k).wait_recv()
+        return self.total(k, (), False)
+
+    def drain(self):
+        for k in range(self.stage0, len(self.bits)):
+            self.copy(k).wait_send()
+
+
+def bit_orders(dp_size):
+    nb = dp_size.bit_length() - 1
+    rest = list(range(2, nb))
+    return [0, 1] + rest, [1, 0] + rest, rest + [0, 1]
 
 
 def gelu_and_slope(v):
@@ -224,8 +235,8 @@
 def middle_body(
     dp_size, a_own, a_send, x, gout, b_output, gain1, shift1, b_in, b_out, gain2, shift2,
     w_o_h, w_in_h, w_out_h,
-    out_o, gsum_o, ga_o, gat_o, sa1, sa2, win_g, wo_g, vec_o, bi_o,
-    a_got, fl, feed_s, feed_g, gf, part_s, part_g, gat_s, gb, wo_s, wo_r, vec_s, vec_r, bi_s, bi_s2, bi_r, wout_g, got_a1, got_a2,
+    out_o, gsum_o, ga_o, gat_o, sa1, sa2, sa3, win_g, wo_g, vec_o, bi_o,
+    a_got, fl, feed_s, feed_g, gf, part_s, part_g, gat_s, gb, wo_s, wo_r, vec_s, vec_r, bi_s, bi_s2, bi_r, wout_g, got_a1, got_a2, got_a3,
     w_o, w_in, w_out, act, slope, gh, u_s, first_s, own_s, gtwo_s,
     load_sem, send_sem, recv_sem, a_send_sem, a_recv_sem,
 ):
@@ -235,19 +246,26 @@
     tile = 256
     tiles = half // tile
     cut = sa1.shape[-1]
-    sems = (a_send_sem, a_recv_sem)
-    A1 = Piece(True, sems, 0, (sa1, got_a1, None, None, None), dp_size)
-    A2 = Piece(False, sems, 1, (sa2, got_a2, None, None, None), dp_size)
-    A1_copy = A1.stage1(wout_g.at[:, :, :, :, :cut])
-    A2_copy = A2.stage1(wout_g.at[:, :, :, :, cut:])
+    nb = dp_size.bit_length() - 1
+    sems = (a_send_sem, a_recv_sem, None)
+    chunks = [slice(None)] * (nb + 1)
+    outs_a = [
+        Piece(
+            bits, sems, i * nb, wout_g.at[tuple(chunks + [slice(i * cut, (i + 1) * cut)])],
+            (g,), (s,),
+        )
+        for i, (bits, g, s) in enumerate(
+            zip(bit_orders(dp_size), (got_a1, got_a2, got_a3), (sa1, sa2, sa3))
+        )
+    ]
     barrier = pltpu.get_barrier_semaphore()
-    for device in ({"mp": 1 - me}, {"dp": A1.peer1}, {"dp": A2.peer1}):
+    for device in [{"mp": 1 - me}] + [{"dp": a.peer(0)} for a in outs_a]:
         pl.semaphore_signal(barrier, inc=1, device_id=device, device_id_type=pl.DeviceIdType.MESH)
     loads = []
     for i, (src, dst) in enumerate(((w_o_h, w_o), (w_in_h, w_in), (w_out_h, w_out))):
         loads.append(pltpu.make_async_copy(src, dst, load_sem.at[i]))
         loads[-1].start()
-    pl.semaphore_wait(barrier, 3)
+    pl.semaphore_wait(barrier, 4)
 
     def copy(src, dst, i):
         return partner_copy(src, dst, send_sem.at[i], recv_sem.at[i], me)
@@ -369,13 +387,12 @@
     def out_weights(j, carry):
         c = pl.ds(pl.multiple_of(j * hw, hw), hw)
         total = mm(gf[0, :, c], act[0], TN) + mm(gf[1, :, c], act[1], TN)
-        zs = wout_g.shape[0] // 2
-        wout_g[pl.ds(j * zs, zs)] = total.astype(BF16).reshape((zs,) + wout_g.shape[1:])
+        wout_g[j] = total.astype(BF16).reshape(wout_g.shape[1:])
         return carry
 
     lax.fori_loop(0, 2, out_weights, 0)
-    A1_copy.start()
-    A2_copy.start()
+    for a in outs_a:
+        a.copy(0).start()
     lax.fori_loop(0, tiles, back_got, 0)
 
     def weights(out, lhs, rhs):
@@ -432,10 +449,9 @@
     first_core = me == 0
     bi_o[0:2, :] = jnp.where(first_core, bi_s2[0:2, :], bi_r[0:2, :])
     bi_o[2:4, :] = jnp.where(first_core, bi_r[0:2, :], bi_s2[0:2, :])
-    A1_copy.wait_recv()
-    A1.add1(lambda z: wout_g[z, :, A1.bit1, :, :cut])
-    A2_copy.wait_recv()
-    A2.add1(lambda z: wout_g[z, A2.bit1, :, :, cut:])
+    for a in outs_a:
+        a.copy(0).wait_recv()
+        a.add(0)
 
     def finish(t, carry):
         ga_copy(t).wait_recv()
@@ -448,8 +464,8 @@
 
     lax.fori_loop(0, tiles, finish, 0)
     a_copy.wait_send()
-    A1_copy.wait_send()
-    A2_copy.wait_send()
+    for a in outs_a:
+        a.copy(0).wait_send()
     vec_copy.wait_send()
     bi_copy.wait_send()
     wo_copy.wait_send()
@@ -459,22 +475,24 @@
     half, width = x.shape
     hw = width // 2
     ff = w_in.shape[1]
-    groups = dp_size // 4
+    nb = dp_size.bit_length() - 1
     n = width // dp_size
+    part = (2,) * (nb - 1) + (n, ff // 3)
     vm = pl.BlockSpec(memory_space=pltpu.VMEM)
     hbm = pl.BlockSpec(memory_space=pl.ANY)
     V = pltpu.VMEM
     return pl.pallas_call(
         functools.partial(middle_body, dp_size),
         in_specs=[vm] * 11 + [hbm] * 3,
-        out_specs=[vm] * 10,
+        out_specs=[vm] * 11,
         out_shape=[
             shape((half, width), BF16),
             shape((half, width), F32),
             shape((half, hw), BF16),
             shape((half, hw), BF16),
-            shape((groups, 2, n, ff // 2), BF16),
-            shape((groups, 2, n, ff // 2), BF16),
+            shape(part, BF16),
+            shape(part, BF16),
+            shape(part, BF16),
             shape((width, ff), BF16),
             shape((width, hw), BF16),
             shape((8, width), F32),
@@ -497,9 +515,10 @@
             V((8, ff), F32),
             V((8, width), F32),
             V((8, width), F32),
-            V((groups, 2, 2, n, ff), BF16),
-            V((groups, 2, n, ff // 2), BF16),
-            V((groups, 2, n, ff // 2), BF16),
+            V((2,) * nb + (n, ff), BF16),
+            V(part, BF16),
+            V(part, BF16),
+            V(part, BF16),
             V((width, width), BF16),
             V((width, ff), BF16),
             V((width, ff), BF16),
@@ -513,8 +532,8 @@
             pltpu.SemaphoreType.DMA((3,)),
             pltpu.SemaphoreType.DMA((14,)),
             pltpu.SemaphoreType.DMA((14,)),
-            pltpu.SemaphoreType.DMA((2,)),
-            pltpu.SemaphoreType.DMA((2,)),
+            pltpu.SemaphoreType.DMA((3 * nb,)),
+            pltpu.SemaphoreType.DMA((3 * nb,)),
         ],
         compiler_params=pltpu.CompilerParams(
             vmem_limit_bytes=62 << 20, collective_id=1, has_side_effects=True
@@ -524,14 +543,24 @@
     )(a_own, a_send, x, gout, b_output, gain1, shift1, b_in, b_out, gain2, shift2, w_o, w_in, w_out)
 
 
+PIECES = ("A1", "A2", "A3", "B1", "B2", "B3", "WO", "C0", "C1", "C2", "C3")
+
+
+def piece_plan(dp_size, width, ff):
+    x, y, z = bit_orders(dp_size)
+    third, pw = ff // 3, 2 * HD
+    return (
+        (x, third), (y, third), (z, third), (x, third), (y, third), (z, third), (y, width // 2),
+        (x, 3 * pw), (y, 3 * pw), (x, 2 * pw), (y, pw),
+    )
+
+
 def back_body(
     dp_size, xo, xt, q_i, k_i, v_i, p_i, ao, at, go, gt, gsum, vec, bi,
-    wq, wk, wv, sa1, sa2, win, wo,
-    ig_o, wq_o, wk_o, wv_o, wo_o, win_o, wout_o, o0, o1, o2, o3, o4, o5, o6, o7, bi_o,
-    g_s, gT, qT, dkT, dvT, dqkv, wcat, xT, acc, ig_s, ig_r, wsrc,
-    a1, a2, b1, b2, w1, c0, c1, c2, c3,
-    tb, tb_m, t0, t1, t2, r0_, r1_, r2_,
-    send, recv, lsem, vsend, vrecv, wsem,
+    wq, wk, wv, sa1, sa2, sa3, win, wo,
+    ig_o, wq_o, wk_o, wv_o, wo_o, win_o, wout_o, vals_o, bi_o,
+    g_s, gT, qT, dkT, dvT, dqkv, wcat, xT, acc, ig_s, ig_r, wsrc, gots, kepts,
+    tb, tb_m, ts, trs, send, recv, lsem, vsend, vrecv, wsem,
 ):
     half, width = xo.shape
     rows = 2 * half
@@ -540,57 +569,45 @@
     p = pl.program_id(0)
     me = lax.axis_index("mp")
     dev = lax.axis_index("dp")
-    groups = dp_size // 4
-    per = 2 + groups - 1
-    sems = (send, recv)
-    cut = win.shape[-1] // 2
-    piece = lambda i, xf, refs: Piece(xf, sems, i * per, refs, dp_size)
-    A1, A2 = piece(0, True, (None, None) + a1), piece(1, False, (None, None) + a2)
-    B1, B2 = piece(2, True, b1), piece(3, False, b2)
-    WO = piece(4, False, w1)
-    C0, C1 = piece(5, True, c0), piece(6, False, c1)
-    C2, C3 = piece(7, True, c2), piece(8, False, c3)
-    win1, win2 = win.at[:, :, :, :, :cut], win.at[:, :, :, :, cut:]
-    src2 = wsrc.at[2, :, :, :, :, : 2 * pw]
-    src3 = wsrc.at[2, :, :, :, :, 2 * pw :]
-    locals_ = [
-        (sa1.at[:, A1.bit2], A1.mine),
-        (sa2.at[:, A2.bit2], A2.mine),
-        (B1.side(win1, B1.bit1), B1.half),
-        (B2.side(win2, B2.bit1), B2.half),
-        (WO.side(wo, WO.bit1), WO.half),
-    ]
-    local = [pltpu.make_async_copy(s, d, lsem.at[i]) for i, (s, d) in enumerate(locals_)]
+    nb = dp_size.bit_length() - 1
+    sems = (send, recv, lsem)
+    chunks = [slice(None)] * (nb + 1)
+    third = sa1.shape[-1]
+
+    def columns(ref, a, b):
+        return ref.at[tuple(chunks + [slice(a, b)])]
+
+    srcs = [sa1, sa2, sa3] + [columns(win, i * third, (i + 1) * third) for i in range(3)] + [wo]
+    srcs += [wsrc.at[0], wsrc.at[1], columns(wsrc.at[2], 0, 2 * pw), columns(wsrc.at[2], 2 * pw, 3 * pw)]
+    P = {}
+    for i, (name, src) in enumerate(zip(PIECES, srcs)):
+        bits = piece_plan(dp_size, width, win.shape[-1])[i][0]
+        s0 = 1 if name[0] == "A" else 0
+        P[name] = Piece(bits, sems, i * nb, src, gots[i], kepts[i], s0)
+    from_hbm = PIECES[:7]
     ig_copy = partner_copy(ig_s, ig_r, vsend.at[0], vrecv.at[0], me)
     tb_copy = partner_copy(tb, tb_m, vsend.at[1], vrecv.at[1], me)
-
-    def vec_copy(src, dst, i, peer):
-        return pltpu.make_async_remote_copy(
-            src_ref=src, dst_ref=dst, send_sem=vsend.at[i], recv_sem=vrecv.at[i],
-            device_id={"dp": peer}, device_id_type=pl.DeviceIdType.MESH,
+    t_copies = [
+        pltpu.make_async_remote_copy(
+            src_ref=ts[k], dst_ref=trs[k], send_sem=vsend.at[2 + k], recv_sem=vrecv.at[2 + k],
+            device_id={"dp": P["C0"].peer(k)}, device_id_type=pl.DeviceIdType.MESH,
         )
-
-    t0_copy = vec_copy(t0, r0_, 2, C2.peer1)
-    t1_copy = vec_copy(t1, r1_, 3, C2.peer2)
-    t2_copies = [vec_copy(t2, r2_.at[s], 4 + s, peer) for s, (_, peer) in enumerate(C2.peers3)]
+        for k in range(nb)
+    ]
 
     @pl.when(p == 0)
     def _():
         barrier = pltpu.get_barrier_semaphore()
-        everyone = [{"mp": 1 - me}, {"dp": C0.peer1}, {"dp": C0.peer2}]
-        everyone += [{"dp": peer} for _, peer in C0.peers3]
+        everyone = [{"mp": 1 - me}] + [{"dp": P["C0"].peer(k)} for k in range(nb)]
         for device in everyone:
             pl.semaphore_signal(
                 barrier, inc=1, device_id=device, device_id_type=pl.DeviceIdType.MESH
             )
-        for c in local:
-            c.start()
+        for name in from_hbm:
+            P[name].load_own().start()
         pl.semaphore_wait(barrier, len(everyone))
-        A1.stage2(sa1).start()
-        A2.stage2(sa2).start()
-        B1.stage1(win1).start()
-        B2.stage1(win2).start()
-        WO.stage1(wo).start()
+        for name in from_hbm:
+            P[name].copy(P[name].stage0).start()
         xT[:, :half] = xo[...].T
         xT[:, half:] = xt[...].T
         tb[...] = jnp.zeros_like(tb)
@@ -612,6 +629,39 @@
     dvT[...] = jnp.zeros_like(dvT)
     lane = lax.broadcasted_iota(jnp.int32, (tile, pw), 1)
     low = lane < HD
+
+    def forward(k, *names):
+        for name in names:
+            x = P[name]
+            loaded = name in from_hbm and k == x.stage0
+            if loaded:
+                x.load_own().wait()
+            x.forward(k, loaded)
+
+    def at_tile(t):
+        if t == 3:
+
+            @pl.when(p == 0)
+            def _():
+                forward(1, "A1", "A2")
+
+            @pl.when(p == 1)
+            def _():
+                forward(1, "A3")
+                forward(0, "B3")
+                forward(2, "A1", "A2")
+
+        if t == 1:
+
+            @pl.when(p == 1)
+            def _():
+                forward(0, "B1", "B2")
+
+            @pl.when(p == 2)
+            def _():
+                forward(1, "B1", "B2")
+                forward(2, "A3")
+                forward(0, "WO")
 
     for t in range(rows // tile):
         rs = slice(t * tile, (t + 1) * tile)
@@ -633,27 +683,7 @@
         dq = jnp.where(low, outs[0], outs[1]) * HD**-0.5
         dqkv[rs, 0:pw] = dq.astype(BF16)
 
-        if t == 3:
-
-            @pl.when(p == 1)
-            def _():
-                local[0].wait()
-                local[1].wait()
-                for x in (A1, A2):
-                    x.stage2(sa1 if x is A1 else sa2).wait_recv()
-                    x.add2(lambda z, x=x: x.mine[z])
-                    for c in x.stage3():
-                        c.start()
-
-        if t == 1:
-
-            @pl.when(p == 2)
-            def _():
-                for j, (x, s) in enumerate(((B1, win1), (B2, win2), (WO, wo))):
-                    local[2 + j].wait()
-                    x.stage1(s).wait_recv()
-                    x.add1(lambda z, x=x: x.half[z])
-                    x.stage2().start()
+        at_tile(t)
 
     dqkv[:, pw : 2 * pw] = (dkT[...].T * HD**-0.5).astype(BF16)
     dqkv[:, 2 * pw : 3 * pw] = dvT[...].T.astype(BF16)
@@ -665,16 +695,16 @@
 
     @pl.when(p == 0)
     def _():
-        C0.stage1(wsrc.at[0]).start()
+        P["C0"].copy(0).start()
 
     @pl.when(p == 1)
     def _():
-        C1.stage1(wsrc.at[1]).start()
+        P["C1"].copy(0).start()
 
     @pl.when(p == 2)
     def _():
-        C2.stage1(src2).start()
-        C3.stage1(src3).start()
+        P["C2"].copy(0).start()
+        P["C3"].copy(0).start()
         tb_copy.start()
 
     for c in w_copies:
@@ -695,68 +725,43 @@
         ig_copy.start()
         acc[:half, :] += part[:half]
 
-        def own(j, piece):
-            def get(z):
-                return wsrc[j, z, :, piece.bit1] if piece.x_first else wsrc[j, z, piece.bit1]
-
-            return get
-
-        def forward2(x):
-            x.stage2().wait_recv()
-            x.add2()
-            for c in x.stage3():
-                c.start()
-
-        C0.stage1(wsrc.at[0]).wait_recv()
-        C0.add1(own(0, C0))
-        C0.stage2().start()
+        def next_table(k):
+            t_copies[k].wait_recv()
+            ts[k + 1][...] = ts[k][...] + trs[k][...]
+            if k + 1 < nb:
+                t_copies[k + 1].start()
+
+        forward(0, "C0")
         tb_copy.wait_recv()
-        t0[0:8, :] = tb[...] + tb_m[...] + vec[...]
-        t0[8:16, :] = bi[...]
-        t0_copy.start()
-        forward2(B1)
-        forward2(B2)
-        C1.stage1(wsrc.at[1]).wait_recv()
-        C1.add1(own(1, C1))
-        C1.stage2().start()
-        forward2(WO)
-        t0_copy.wait_recv()
-        t1[...] = t0[...] + r0_[...]
-        t1_copy.start()
-        forward2(C0)
-        C2.stage1(src2).wait_recv()
-        C2.add1(lambda z: wsrc[2, z, :, C2.bit1, :, : 2 * pw])
-        C2.stage2().start()
-        C3.stage1(src3).wait_recv()
-        C3.add1(lambda z: wsrc[2, z, C3.bit1, :, :, 2 * pw :])
-        C3.stage2().start()
-        forward2(C1)
-        t1_copy.wait_recv()
-        t2[...] = t1[...] + r1_[...]
-        for c in t2_copies:
-            c.start()
+        ts[0][0:8, :] = tb[...] + tb_m[...] + vec[...]
+        ts[0][8:16, :] = bi[...]
+        t_copies[0].start()
+        forward(1, "B3")
+        forward(2, "B1", "B2")
+        forward(0, "C1")
+        forward(1, "WO")
+        next_table(0)
+        forward(1, "C0")
+        forward(0, "C2", "C3")
         ig_copy.wait_recv()
         ig_o[...] = gsum[...] + (acc[:half, :] + ig_r[...].astype(F32))
-        forward2(C2)
-        forward2(C3)
-
-        def arrived(x):
-            for c in x.stage3():
-                c.wait_recv()
-            return x.result()
-
-        wout_o[:, :cut] = arrived(A1)
-        wout_o[:, cut:] = arrived(A2)
-        win_o[:, :cut] = arrived(B1)
-        win_o[:, cut:] = arrived(B2)
-        wo_o[...] = arrived(WO)
-        for c in t2_copies:
-            c.wait_recv()
-        table = t2[...]
-        for s in range(groups - 1):
-            table = table + r2_[s]
+        next_table(1)
+        forward(2, "B3")
+        forward(1, "C1")
+        forward(2, "WO", "C0")
+        for k in range(2, nb - 1):
+            next_table(k)
+        forward(1, "C2", "C3")
+        forward(2, "C1")
+        for i in range(3):
+            wout_o[:, i * third : (i + 1) * third] = P["A%d" % (i + 1)].result()
+            win_o[:, i * third : (i + 1) * third] = P["B%d" % (i + 1)].result()
+        forward(2, "C2", "C3")
+        wo_o[...] = P["WO"].result()
+        next_table(nb - 1)
+        table = ts[nb][...]
         n = width // dp_size
-        m = bi_o.shape[0]
+        m = bi_o.shape[1]
         vals = table[0:8, 0:n]
         biv = table[8:9, 0:m]
         for j in range(1, dp_size):
@@ -764,45 +769,32 @@
             r = 8 + (j * m) // width
             k = (j * m) % width
             biv = jnp.where(dev == j, table[r : r + 1, k : k + m], biv)
-        for j, o in enumerate((o0, o1, o2, o3, o4, o5, o6, o7)):
-            o[...] = vals[j]
-        bi_o[...] = biv[0]
-        for j, x in enumerate((C0, C1)):
-            v = arrived(x)
+        vals_o[...] = vals
+        bi_o[...] = biv
+        for j in range(3):
             cs = slice(j * pw, (j + 1) * pw)
-            for i, o in enumerate((wq_o, wk_o, wv_o)):
-                o[:, cs] = v[:, i * pw : (i + 1) * pw]
-        v = arrived(C2)
-        cs = slice(2 * pw, 3 * pw)
-        wq_o[:, cs] = v[:, :pw]
-        wk_o[:, cs] = v[:, pw:]
-        wv_o[:, cs] = arrived(C3)
-
-        A1.stage2(sa1).wait_send()
-        A2.stage2(sa2).wait_send()
-        for x, s in ((B1, win1), (B2, win2), (WO, wo), (C0, wsrc.at[0]), (C1, wsrc.at[1]), (C2, src2), (C3, src3)):
-            x.stage1(s).wait_send()
-            x.stage2().wait_send()
-        for x in (A1, A2, B1, B2, WO, C0, C1, C2, C3):
-            for c in x.stage3():
-                c.wait_send()
+            v = P["C%d" % j].result()
+            wq_o[:, cs] = v[:, :pw]
+            wk_o[:, cs] = v[:, pw : 2 * pw]
+            wv_o[:, cs] = v[:, 2 * pw :] if j < 2 else P["C3"].result()
+
+        for name in PIECES:
+            P[name].drain()
         ig_copy.wait_send()
         tb_copy.wait_send()
-        t0_copy.wait_send()
-        t1_copy.wait_send()
-        for c in t2_copies:
+        for c in t_copies:
             c.wait_send()
 
 
-def back(dp_size, xo, xt, wq, wk, wv, q, k, v, probs, ao, at, go, gt, gsum, vec, bi, sa1, sa2, win, wo):
+def back(dp_size, xo, xt, wq, wk, wv, q, k, v, probs, ao, at, go, gt, gsum, vec, bi, sa, win, wo):
     half, width = xo.shape
     rows = 2 * half
     pairs = HEADS // 4
     pw = 2 * HD
     ff = win.shape[1]
-    groups = dp_size // 4
+    nb = dp_size.bit_length() - 1
     n = width // dp_size
-    five = lambda a: a.reshape(groups, 2, 2, n, a.shape[-1])
+    split = lambda a: a.reshape((2,) * nb + (n, a.shape[-1]))
     whole = lambda a: pl.BlockSpec(
         a.shape, lambda p: (0,) * a.ndim, pipeline_mode=pl.Buffered(1)
     )
@@ -810,17 +802,19 @@
     hbm = pl.BlockSpec(memory_space=pl.ANY)
     vm = pl.BlockSpec(memory_space=pltpu.VMEM)
     V = pltpu.VMEM
-
-    def late(w):
-        return (V((groups, n, w), BF16), V((groups, n, w), BF16), V((groups - 1, n, w), BF16))
-
-    def bufs(w):
-        return (V((groups, 2, n, w), BF16), V((groups, 2, n, w), BF16)) + late(w)
-
-    fw = ff // 2
-    pieces = 9
-    per = 2 + groups - 1
+    plan = piece_plan(dp_size, width, ff)
+
+    def stages(last):
+        return tuple(
+            tuple(
+                V((2,) * (nb - 1 - k) + (n, w), BF16) if k < nb - last else V((16, 128), BF16)
+                for k in range(nb)
+            )
+            for _, w in plan
+        )
+
     table = lambda: V((16, width), F32)
+    sem = pltpu.SemaphoreType.DMA
     return pl.pallas_call(
         functools.partial(back_body, dp_size),
         grid_spec=pltpu.PrefetchScalarGridSpec(
@@ -831,8 +825,8 @@
             + [pl.BlockSpec((2, rows, rows), lambda p: (p, 0, 0))]
             + [col(half, pw)] * 4
             + [whole(gsum), whole(vec), whole(bi)]
-            + [hbm] * 7,
-            out_specs=[vm] * 16,
+            + [hbm] * 8,
+            out_specs=[vm] * 9,
             scratch_shapes=[
                 V((rows, pw), BF16),
                 V((pw, rows), BF16),
@@ -845,30 +839,55 @@
                 V((rows, width), F32),
                 V((half, width), BF16),
                 V((half, width), BF16),
-                V((pairs, groups, 2, 2, n, 3 * pw), BF16),
-                late(fw), late(fw), bufs(fw), bufs(fw), bufs(width // 2),
-                bufs(3 * pw), bufs(3 * pw), bufs(2 * pw), bufs(pw),
-                V((8, width), F32), V((8, width), F32),
-                table(), table(), table(), table(), table(), V((groups - 1, 16, width), F32),
-                pltpu.SemaphoreType.DMA((pieces * per,)),
-                pltpu.SemaphoreType.DMA((pieces * per,)),
-                pltpu.SemaphoreType.DMA((5,)),
-                pltpu.SemaphoreType.DMA((4 + groups - 1,)),
-                pltpu.SemaphoreType.DMA((4 + groups - 1,)),
-                pltpu.SemaphoreType.DMA((3,)),
+                V((pairs,) + (2,) * nb + (n, 3 * pw), BF16),
+                stages(0),
+                stages(1),
+                V((8, width), F32),
+                V((8, width), F32),
+                tuple(table() for _ in range(nb + 1)),
+                tuple(table() for _ in range(nb)),
+                sem((len(plan) * nb,)),
+                sem((len(plan) * nb,)),
+                sem((len(plan),)),
+                sem((2 + nb,)),
+                sem((2 + nb,)),
+                sem((3,)),
             ],
         ),
         out_shape=[shape((half, width), F32)]
         + [shape((n, width // 2), F32)] * 4
         + [shape((n, ff), F32)] * 2
-        + [shape((n,), F32)] * 8
-        + [shape((2 * ff // dp_size,), F32)],
+        + [shape((8, n), F32), shape((1, 2 * ff // dp_size), F32)],
         compiler_params=pltpu.CompilerParams(
             vmem_limit_bytes=60 << 20, collective_id=2, has_side_effects=True
         ),
         cost_estimate=cost(40e9, 20e6),
         name="back",
-    )(xo, xt, q, k, v, probs, ao, at, go, gt, gsum, vec, bi, wq, wk, wv, sa1, sa2, five(win), five(wo))
+    )(xo, xt, q, k, v, probs, ao, at, go, gt, gsum, vec, bi, wq, wk, wv, *sa, split(win), split(wo))
+
+
+def emit_body(big, *refs):
+    ins, outs = refs[: big + 2], refs[big + 2 :]
+    for i in range(big):
+        outs[i][...] = ins[i][...]
+    vals = ins[big][...]
+    for j in range(8):
+        outs[big + j][...] = vals[j]
+    outs[big + 8][...] = ins[big + 1][0]
+
+
+def emit(arrays, vals, bi):
+    vm = pl.BlockSpec(memory_space=pltpu.VMEM)
+    return pl.pallas_call(
+        functools.partial(emit_body, len(arrays)),
+        in_specs=[vm] * (len(arrays) + 2),
+        out_specs=[vm] * (len(arrays) + 9),
+        out_shape=[shape(a.shape, a.dtype) for a in arrays]
+        + [shape((vals.shape[1],), F32)] * 8
+        + [shape((bi.shape[1],), F32)],
+        compiler_params=params(60),
+        name="emit",
+    )(*arrays, vals, bi)
 
 
 def local_pair(
@@ -886,17 +905,18 @@
     q, k, v, probs, a_own, a_send = attn_fwd(
         sc, x, x_got, w_query, w_key, w_value, vec(b_query), vec(b_value), rand
     )
-    out, gsum, ga0, ga_got, sa1, sa2, w_in_g, w_output_g, vec_g, bi_g = middle(
+    out, gsum, ga0, ga_got, sa1, sa2, sa3, w_in_g, w_output_g, vec_g, bi_g = middle(
         dp_size, a_own, a_send, x, grad_out[0], b_output, gain_one, shift_one, b_in, b_out,
         gain_two, shift_two, w_output, w_in, w_out,
     )
+    *mats, vals, bi = back(
+        dp_size, x, x_got, w_query, w_key, w_value, q, k, v, probs, a_own, a_send, ga0, ga_got,
+        gsum, vec_g, bi_g, (sa1, sa2, sa3), w_in_g, w_output_g,
+    )
     (
-        input_grad, wq_p, wk_p, wv_p, wo_p, in_part, out_part, bq_p, bv_p, bo_p, g1_p, s1_p, b2_p,
-        g2_p, s2_p, bi_p,
-    ) = back(
-        dp_size, x, x_got, w_query, w_key, w_value, q, k, v, probs, a_own, a_send, ga0, ga_got,
-        gsum, vec_g, bi_g, sa1, sa2, w_in_g, w_output_g,
-    )
+        out, input_grad, wq_p, wk_p, wv_p, wo_p, in_part, out_part, bq_p, bv_p, bo_p, g1_p, s1_p,
+        b2_p, g2_p, s2_p, bi_p,
+    ) = emit([out] + mats, vals, bi)
     return (
         out[None], input_grad[None], wq_p, bq_p, wk_p, wv_p, bv_p, wo_p, bo_p, g1_p, s1_p,
         in_part, bi_p, out_part, b2_p, g2_p, s2_p,
@@ -1483,7 +1503,7 @@
         P("dp"),
     )
     sizes = dict(mesh.shape)
-    if sizes["mp"] == 2 and sizes["dp"] % 4 == 0:
+    if sizes["mp"] == 2 and sizes["dp"] in (4, 8, 16, 32):
         local_fn = functools.partial(local_pair, sizes["dp"])
     else:
         local_fn = local

time: 166 us -> 144 us (0.87)
  local copies, waits for them, and re-layouts: 16.3 us -> 4.77 us
  Pallas kernels: 147 us -> 136 us
    pallas_call x1, Pallas kernels: 79.6 us -> 67.2 us  [back(): pl.pallas_call(functools.partial(back_body, dp_size), grid_spec=pltpu.Pre...]
    unnamed x54 -> x3, local copies, waits for them, and re-layouts: 13.1 us -> 1.56 us
    pallas_call x0 -> x1, Pallas kernels: none -> 3.7 us  [emit(): pl.pallas_call(functools.partial(emit_body, len(arrays)), in_specs=[vm] *...]
    pallas_call x1, Pallas kernels: 41.7 us -> 38.9 us  [middle(): pl.pallas_call(functools.partial(middle_body, dp_size), in_specs=[vm] * 1...]
where the time goes in v4:
time: 144 us; the launch traced here: 143 us
  Pallas kernels  136 us (94%)
  local copies, waits for them, and re-layouts  4.77 us (3%)
  between operations  1.49 us (1%)
    pallas_call x1, Pallas kernels, back(): pl.pallas_call(functools.partial(back_body, dp_size), grid_spec=pltpu.Pre...  67.2 us
    pallas_call x1, Pallas kernels, middle(): pl.pallas_call(functools.partial(middle_body, dp_size), in_specs=[vm] * 1...  38.9 us
    pallas_call x1, Pallas kernels, attn_fwd(): pl.pallas_call(attn_fwd_body, grid_spec=pltpu.PrefetchScalarGridSpec(num_...  26 us
    pallas_call x1, Pallas kernels, emit(): pl.pallas_call(functools.partial(emit_body, len(arrays)), in_specs=[vm] *...  3.7 us
  transfers between devices with their start and end apart: 2, of which 0 were waited for; matrix products, arithmetic and copies ran while one was open for 3% of the time, Pallas kernels for 0%

profile of v4, /device:TPU:0, one launch (start us, length us, event | category | flops | bytes accessed | tf_op | source)
XLA Modules:
  0.0 143.3 jit_solution(14218316465370811717)
XLA Ops:
  0.7 0.5 collective-permute-start
  1.2 0.7 copy.41
  1.9 0.1 collective-permute-start.1
  2.6 1.3 reshape.46.bq
  3.8 0.6 pad_add_fusion.1.sc
  4.4 1.3 reshape.47.bv
  5.7 0.0 collective-permute-done.1
  5.7 0.1 pad_add_fusion
  5.8 0.7 copy.38.rand
  6.4 0.0 collective-permute-done.xt
  6.4 0.0 copy-start
  6.4 0.9 copy-done
  7.3 26.0 %attn_fwd.1 = (bf16[1024,384]{1,0:T(8,128)(2,1)}, bf16[1024,384]{1,0:T(8,128)(2,1)}, bf16[1024,384]{1,0:T(8,128)(2,1)}, bf16[6,1024,1024]{2,1,0:T(8,128)(2,1)}, ...) custom-call(s32[2]{0:T(128)} %pad_add_fusion.1.sc, bf16[512,768]{1,0:T(8,128)(2,1)} %bitcast.15, ...), custom_call_target="tpu_custom_call" | custom-call | flops 20000000000 | bytes 20000000 | tf_op jit(solution)/shard_map/attn_fwd/pallas_call | solution.py:117
  33.3 38.9 %middle.1 = (bf16[512,768]{1,0:T(8,128)(2,1)}, f32[512,768]{1,0:T(8,128)}, bf16[512,384]{1,0:T(8,128)(2,1)}, bf16[512,384]{1,0:T(8,128)(2,1)}, bf16[2,2,2,48,512...) custom-call(bf16[512,384]{1,0:T(8,128)(2,1)} %get-tuple-element.60.a, ...), custom_call_target="tpu_custom_call" | custom-call | flops 16999999488 | bytes 20000000 | tf_op jit(solution)/shard_map/middle/pallas_call | solution.py:484
  72.3 67.2 %back.1 = (f32[512,768]{1,0:T(8,128)}, f32[48,384]{1,0:T(8,128)}, f32[48,384]{1,0:T(8,128)}, f32[48,384]{1,0:T(8,128)}, f32[48,384]{1,0:T(8,128)}, /*index=5*/f3...) custom-call(bf16[512,768]{1,0:T(8,128)(2,1)} %bitcast.17, bf16[512,768]{1,0:T(8,128)(2,1)} %copy-done, ...), custom_call_target="tpu_custom_call" | custom-call | flops 40000000000 | bytes 20000000 | tf_op jit(solution)/shard_map/back/pallas_call | solution.py:818
  139.5 3.7 %emit.1 = (bf16[512,768]{1,0:T(8,128)(2,1)}, f32[512,768]{1,0:T(8,128)}, f32[48,384]{1,0:T(8,128)}, f32[48,384]{1,0:T(8,128)}, f32[48,384]{1,0:T(8,128)}, /*inde...) custom-call(bf16[512,768]{1,0:T(8,128)(2,1)} %get-tuple-element.62.r, ...), custom_call_target="tpu_custom_call" | custom-call | tf_op jit(solution)/shard_map/emit/pallas_call | solution.py:881
Async XLA Ops:
  0.7 5.8 %collective-permute-start = (bf16[512,768]{1,0:T(8,128)(2,1)}, bf16[512,768]{1,0:T(8,128)(2,1)S(1)}, u32[]{:S(2)}, u32[]{:S(2)}) collective-permute-start(bf16[512,768]{1,0:T(8,128)(2,1)} %bitcast.14), channel_id=1, source_target_pairs={{0,1},{1,0},{2,3},{3,2},{4,5},{5,4},{6,7},{7,6},{8,9},{9,8},{10,11... | collective-permute-start | bytes 2359304 | tf_op jit(solution)/shard_map/ppermute | solution.py:898
  1.9 3.8 %collective-permute-start.1 = (s32[8,3]{0,1:T(4,128)S(1)}, s32[8,3]{0,1:T(4,128)S(1)}, u32[]{:S(2)}, u32[]{:S(2)}) collective-permute-start(s32[8,3]{0,1:T(4,128)S(1)} %bitcast.10), channel_id=1, source_target_pairs={{0,1},{1,0},{2,3},{3,2},{4,5},{5,4},{6,7},{7,6},{8,9},{9,8},{10,11... | collective-permute-start | bytes 296 | tf_op jit(solution)/shard_map/ppermute | solution.py:898
  6.4 0.9 copy-start

commit v5 on v4

--- a/solution.py
+++ b/solution.py
@@ -49,96 +49,180 @@
     return cen * rs, rs
 
 
-def attn_fwd_body(sc, xo, xt, wq, wk, wv, bq, bv, rand, q_o, k_o, v_o, p_o, ao, at, bias):
-    half = xo.shape[0]
+def partner_copy(src, dst, send, recv, me):
+    return pltpu.make_async_remote_copy(
+        src_ref=src, dst_ref=dst, send_sem=send, recv_sem=recv,
+        device_id={"mp": 1 - me}, device_id_type=pl.DeviceIdType.MESH,
+    )
+
+
+def front_body(
+    lengths, x, rand, bq, bv, wq, wk, wv,
+    x_got, a_own, a_oth, a_got, q_o, k_o, v_o, p_o,
+    xg_s, ag_s, w_s, b_s, rand_s, rand_r, bias, wsem, send, recv,
+):
+    me = lax.axis_index("mp")
+    p = pl.program_id(0)
+    half, width = x.shape
     rows = 2 * half
+    hw = width // 2
+    pw = 2 * HD
     nb = rows // BLK
     tile = 256
-
-    @pl.when(pl.program_id(0) == 0)
+    x_copy = partner_copy(x, xg_s, send.at[0], recv.at[0], me)
+    rand_copy = partner_copy(rand_s, rand_r, send.at[1], recv.at[1], me)
+    own_cols = pl.ds(pl.multiple_of(me * hw, hw), hw)
+
+    @pl.when(p == 0)
     def _():
-        c = sc[0]
-        ln = sc[1]
+        barrier = pltpu.get_barrier_semaphore()
+        pl.semaphore_signal(
+            barrier, inc=1, device_id={"mp": 1 - me}, device_id_type=pl.DeviceIdType.MESH
+        )
+        loads = [
+            pltpu.make_async_copy(w.at[:, own_cols], w_s.at[i], wsem.at[i])
+            for i, w in enumerate((wq, wk, wv))
+        ]
+        for c in loads:
+            c.start()
+        rand_s[...] = jnp.zeros_like(rand_s)
+        rand_s[:, : rand.shape[2]] = rand[0]
+        b_s[0:1, :] = bq[...].astype(F32)[None, :]
+        b_s[1:2, :] = bv[...].astype(F32)[None, :]
+        pl.semaphore_wait(barrier, 1)
+        x_copy.start()
+        rand_copy.start()
+        for c in loads:
+            c.wait()
+
+    cols = pl.ds(pl.multiple_of(p * pw, pw), pw)
+    bias_cols = pl.ds(pl.multiple_of(me * hw + p * pw, pw), pw)
+
+    def project(i, xr):
+        rs = slice(i * half, (i + 1) * half)
+        q_o[rs, :] = (mm(xr[...], w_s[0, :, cols]) + b_s[0:1, bias_cols]).astype(BF16)
+        k_o[rs, :] = mm(xr[...], w_s[1, :, cols]).astype(BF16)
+        v_o[rs, :] = (mm(xr[...], w_s[2, :, cols]) + b_s[1:2, bias_cols]).astype(BF16)
+
+    project(0, x)
+
+    @pl.when(p == 0)
+    def _():
+        rand_copy.wait_recv()
+        ln = lengths[0]
         last = (ln + BLK - 1) // BLK - 1
         lb = lax.broadcasted_iota(jnp.int32, (nb, rows), 0)
         kp = lax.broadcasted_iota(jnp.int32, (nb, rows), 1)
-        qb = jnp.where(lb < nb // 2, lb + (nb // 2) * c, lb - (nb // 2) * c)
-        kpos = jnp.where(kp < half, kp + half * c, kp - half * c)
+        qb = jnp.where(lb < nb // 2, lb + (nb // 2) * me, lb - (nb // 2) * me)
+        kpos = jnp.where(kp < half, kp + half * me, kp - half * me)
         kb = kpos // BLK
         ok = (jnp.abs(kb - qb) <= 1) | (kb == 0) | (kb == last)
-        for j in range(rand.shape[1]):
-            ok = ok | (kb == rand[:, j : j + 1])
+        both = jnp.concatenate([rand_s[...], rand_r[...]], axis=0)
+        for j in range(rand.shape[2]):
+            ok = ok | (kb == both[:, j : j + 1])
         ok = ok | (qb == 0) | (qb == last)
         ok = ok & (kpos < ln)
         table = jnp.where(ok, 0.0, -1e30).astype(F32)
         for b in range(nb):
             bias[b] = jnp.broadcast_to(table[b : b + 1, :], (8, rows))
-
-    for i, xr in enumerate((xo, xt)):
-        rs = slice(i * half, (i + 1) * half)
-        q_o[rs, :] = (mm(xr[...], wq[...]) + bq[...].astype(F32)).astype(BF16)
-        k_o[rs, :] = mm(xr[...], wk[...]).astype(BF16)
-        v_o[rs, :] = (mm(xr[...], wv[...]) + bv[...].astype(F32)).astype(BF16)
-
-    lane = lax.broadcasted_iota(jnp.int32, (tile, 2 * HD), 1)
-    low = lane < HD
-    for i, a_ref in enumerate((ao, at)):
-
-        def step(t, carry, i=i, a_ref=a_ref):
-            r0 = pl.multiple_of(i * half + t * tile, tile)
-            q = q_o[pl.ds(r0, tile), :] * BF16(HD**-0.5)
-            outs = []
-            for h in range(2):
-                qh = jnp.where(low if h == 0 else ~low, q, BF16(0))
-                s = mm(qh, k_o[...], NT)
-                s = s.reshape(tile // BLK, BLK // 8, 8, rows)
-                s = s + bias[pl.ds(r0 // BLK, tile // BLK)][:, None]
-                s = s.reshape(tile, rows)
-                e = jnp.exp(s - jnp.max(s, axis=-1, keepdims=True))
-                p = (e * (1.0 / jnp.sum(e, axis=-1, keepdims=True))).astype(BF16)
-                p_o[h, pl.ds(r0, tile), :] = p
-                outs.append(mm(p, v_o[...]))
-            a = jnp.where(low, outs[0], outs[1]).astype(BF16)
-            a_ref[pl.ds(pl.multiple_of(t * tile, tile), tile), :] = a
-            return carry
-
-        lax.fori_loop(0, half // tile, step, 0)
-
-
-def attn_fwd(sc, xo, xt, wq, wk, wv, bq, bv, rand):
-    half, width = xo.shape
+        x_copy.wait_recv()
+        x_got[...] = xg_s[...]
+
+    project(1, xg_s)
+
+    low = lax.broadcasted_iota(jnp.int32, (tile, pw), 1) < HD
+    order = [half + t * tile for t in range(half // tile)] + [t * tile for t in range(half // tile)]
+    units = [(r0, h) for r0 in order for h in range(2)]
+    scores, probs, outs = {}, {}, {}
+
+    def score(i):
+        r0, h = units[i]
+        q = q_o[r0 : r0 + tile, :] * BF16(HD**-0.5)
+        s = mm(jnp.where(low if h == 0 else ~low, q, BF16(0)), k_o[...], NT)
+        b0 = r0 // BLK
+        s = s.reshape(tile // BLK, BLK // 8, 8, rows) + bias[b0 : b0 + tile // BLK][:, None]
+        scores[i] = s.reshape(tile, rows)
+
+    def attend(i):
+        r0, h = units[i]
+        outs[i] = mm(probs.pop(i), v_o[...])
+        if h == 1:
+            a = jnp.where(low, outs.pop(i - 1), outs.pop(i)).astype(BF16)
+            if r0 < half:
+                a_own[r0 : r0 + tile, cols] = a
+            else:
+                a_oth[r0 - half : r0 - half + tile, cols] = a
+                if r0 + tile == rows:
+                    partner_copy(
+                        a_oth.at[:, cols], ag_s.at[:, cols], send.at[2 + p], recv.at[2 + p], me
+                    ).start()
+
+    score(0)
+    for i, (r0, h) in enumerate(units):
+        if i + 1 < len(units):
+            score(i + 1)
+        s = scores.pop(i)
+        e = jnp.exp(s - jnp.max(s, axis=-1, keepdims=True))
+        pr = (e * (1.0 / jnp.sum(e, axis=-1, keepdims=True))).astype(BF16)
+        p_o[h, r0 : r0 + tile, :] = pr
+        probs[i] = pr
+        if i >= 1:
+            attend(i - 1)
+    attend(len(units) - 1)
+
+    @pl.when(p == pl.num_programs(0) - 1)
+    def _():
+        x_copy.wait_send()
+        rand_copy.wait_send()
+        for j in range(hw // pw):
+            cs = slice(j * pw, (j + 1) * pw)
+            c = partner_copy(a_oth.at[:, cs], ag_s.at[:, cs], send.at[2 + j], recv.at[2 + j], me)
+            c.wait_send()
+            c.wait_recv()
+        a_got[...] = ag_s[...]
+
+
+def front(lengths, x, rand, bq, bv, wq, wk, wv):
+    half, width = x.shape
     rows = 2 * half
     pairs = HEADS // 4
     pw = 2 * HD
-    whole = lambda a: pl.BlockSpec(a.shape, lambda p, s: (0,) * a.ndim)
-    wspec = pl.BlockSpec((width, pw), lambda p, s: (0, s[0] * pairs + p))
-    bspec = pl.BlockSpec((1, pw), lambda p, s: (0, s[0] * pairs + p))
-    ospec = lambda r: pl.BlockSpec((r, pw), lambda p, s: (0, p))
+    hw = width // 2
+    vm = pl.BlockSpec(memory_space=pltpu.VMEM)
+    hbm = pl.BlockSpec(memory_space=pl.ANY)
+    col = pl.BlockSpec((rows, pw), lambda p: (0, p))
+    V = pltpu.VMEM
+    sem = pltpu.SemaphoreType.DMA
     return pl.pallas_call(
-        attn_fwd_body,
+        front_body,
         grid_spec=pltpu.PrefetchScalarGridSpec(
-            num_scalar_prefetch=1,
+            num_scalar_prefetch=0,
             grid=(pairs,),
-            in_specs=[whole(xo), whole(xt), wspec, wspec, wspec, bspec, bspec, whole(rand)],
-            out_specs=[ospec(rows)] * 3
-            + [pl.BlockSpec((2, rows, rows), lambda p, s: (p, 0, 0))]
-            + [ospec(half)] * 2,
-            scratch_shapes=[pltpu.VMEM((rows // BLK, 8, rows), F32)],
+            in_specs=[pl.BlockSpec(memory_space=pltpu.SMEM)] + [vm] * 4 + [hbm] * 3,
+            out_specs=[vm] * 4 + [col] * 3 + [pl.BlockSpec((2, rows, rows), lambda p: (p, 0, 0))],
+            scratch_shapes=[
+                V((half, width), BF16),
+                V((half, hw), BF16),
+                V((3, width, hw), BF16),
+                V((8, width), F32),
+                V((rand.shape[1], 128), jnp.int32),
+                V((rand.shape[1], 128), jnp.int32),
+                V((rows // BLK, 8, rows), F32),
+                sem((3,)),
+                sem((2 + pairs,)),
+                sem((2 + pairs,)),
+            ],
         ),
-        out_shape=[shape((rows, pairs * pw), BF16)] * 3
-        + [shape((2 * pairs, rows, rows), BF16)]
-        + [shape((half, pairs * pw), BF16)] * 2,
-        compiler_params=params(),
+        out_shape=[shape((half, width), BF16)]
+        + [shape((half, hw), BF16)] * 3
+        + [shape((rows, hw), BF16)] * 3
+        + [shape((2 * pairs, rows, rows), BF16)],
+        compiler_params=pltpu.CompilerParams(
+            vmem_limit_bytes=60 << 20, collective_id=3, has_side_effects=True
+        ),
         cost_estimate=cost(20e9, 20e6, 6 * rows * rows),
-        name="attn_fwd",
-    )(sc, xo, xt, wq, wk, wv, bq, bv, rand)
-
-
-def partner_copy(src, dst, send, recv, me):
-    return pltpu.make_async_remote_copy(
-        src_ref=src, dst_ref=dst, send_sem=send, recv_sem=recv,
-        device_id={"mp": 1 - me}, device_id_type=pl.DeviceIdType.MESH,
-    )
+        name="front",
+    )(lengths, x, rand, bq, bv, wq, wk, wv)
 
 
 class Piece:
@@ -233,10 +317,10 @@
 
 
 def middle_body(
-    dp_size, a_own, a_send, x, gout, b_output, gain1, shift1, b_in, b_out, gain2, shift2,
+    dp_size, a_own, a_got, x, gout, b_output, gain1, shift1, b_in, b_out, gain2, shift2,
     w_o_h, w_in_h, w_out_h,
     out_o, gsum_o, ga_o, gat_o, sa1, sa2, sa3, win_g, wo_g, vec_o, bi_o,
-    a_got, fl, feed_s, feed_g, gf, part_s, part_g, gat_s, gb, wo_s, wo_r, vec_s, vec_r, bi_s, bi_s2, bi_r, wout_g, got_a1, got_a2, got_a3,
+    fl, feed_s, feed_g, gf, part_s, part_g, gat_s, gb, wo_s, wo_r, vec_s, vec_r, bi_s, bi_s2, bi_r, wout_g, got_a1, got_a2, got_a3,
     w_o, w_in, w_out, act, slope, gh, u_s, first_s, own_s, gtwo_s,
     load_sem, send_sem, recv_sem, a_send_sem, a_recv_sem,
 ):
@@ -270,10 +354,7 @@
     def copy(src, dst, i):
         return partner_copy(src, dst, send_sem.at[i], recv_sem.at[i], me)
 
-    a_copy = copy(a_send, a_got, 0)
-    a_copy.start()
     loads[0].wait()
-    a_copy.wait_recv()
 
     def rows(t):
         return pl.ds(pl.multiple_of(t * tile, tile), tile)
@@ -463,7 +544,6 @@
         return carry
 
     lax.fori_loop(0, tiles, finish, 0)
-    a_copy.wait_send()
     for a in outs_a:
         a.copy(0).wait_send()
     vec_copy.wait_send()
@@ -471,7 +551,7 @@
     wo_copy.wait_send()
 
 
-def middle(dp_size, a_own, a_send, x, gout, b_output, gain1, shift1, b_in, b_out, gain2, shift2, w_o, w_in, w_out):
+def middle(dp_size, a_own, a_got, x, gout, b_output, gain1, shift1, b_in, b_out, gain2, shift2, w_o, w_in, w_out):
     half, width = x.shape
     hw = width // 2
     ff = w_in.shape[1]
@@ -499,7 +579,6 @@
             shape((8, width), F32),
         ],
         scratch_shapes=[
-            V((half, hw), BF16),
             V((2, half, width), BF16),
             V((half, width), BF16),
             V((half, width), BF16),
@@ -540,7 +619,7 @@
         ),
         cost_estimate=cost(17e9, 20e6),
         name="middle",
-    )(a_own, a_send, x, gout, b_output, gain1, shift1, b_in, b_out, gain2, shift2, w_o, w_in, w_out)
+    )(a_own, a_got, x, gout, b_output, gain1, shift1, b_in, b_out, gain2, shift2, w_o, w_in, w_out)
 
 
 PIECES = ("A1", "A2", "A3", "B1", "B2", "B3", "WO", "C0", "C1", "C2", "C3")
@@ -894,23 +973,16 @@
     dp_size, inputs, grad_out, lengths, rand_blocks, w_query, b_query, w_key, w_value, b_value,
     w_output, b_output, gain_one, shift_one, w_in, b_in, w_out, b_out, gain_two, shift_two,
 ):
-    core = lax.axis_index("mp").astype(jnp.int32)
-    swap = lambda a: lax.ppermute(a, "mp", [(0, 1), (1, 0)])
-    vec = lambda a: a.reshape(1, -1)
     x = inputs[0]
-    half, width = x.shape
-    x_got = swap(x)
-    rand = jnp.concatenate([rand_blocks[0], swap(rand_blocks[0])], axis=0)
-    sc = jnp.stack([core, lengths[0]])
-    q, k, v, probs, a_own, a_send = attn_fwd(
-        sc, x, x_got, w_query, w_key, w_value, vec(b_query), vec(b_value), rand
+    x_got, a_own, a_oth, a_got, q, k, v, probs = front(
+        lengths, x, rand_blocks, b_query, b_value, w_query, w_key, w_value
     )
     out, gsum, ga0, ga_got, sa1, sa2, sa3, w_in_g, w_output_g, vec_g, bi_g = middle(
-        dp_size, a_own, a_send, x, grad_out[0], b_output, gain_one, shift_one, b_in, b_out,
+        dp_size, a_own, a_got, x, grad_out[0], b_output, gain_one, shift_one, b_in, b_out,
         gain_two, shift_two, w_output, w_in, w_out,
     )
     *mats, vals, bi = back(
-        dp_size, x, x_got, w_query, w_key, w_value, q, k, v, probs, a_own, a_send, ga0, ga_got,
+        dp_size, x, x_got, w_query, w_key, w_value, q, k, v, probs, a_own, a_oth, ga0, ga_got,
         gsum, vec_g, bi_g, (sa1, sa2, sa3), w_in_g, w_output_g,
     )
     (
@@ -1503,7 +1575,7 @@
         P("dp"),
     )
     sizes = dict(mesh.shape)
-    if sizes["mp"] == 2 and sizes["dp"] in (4, 8, 16, 32):
+    if sizes["mp"] == 2 and sizes["dp"] == 16:
         local_fn = functools.partial(local_pair, sizes["dp"])
     else:
         local_fn = local

time: 144 us -> 133 us (0.924)
  Pallas kernels: 136 us -> 130 us
  local copies, waits for them, and re-layouts: 4.77 us -> 1.35 us
    pallas_call x1, Pallas kernels: 26 us -> 23 us  [front(): pl.pallas_call(front_body, grid_spec=pltpu.PrefetchScalarGridSpec(num_sca...]
    reshape x2 -> x0, local copies, waits for them, and re-layouts: 2.53 us -> none  [local_pair(): vec = lambda a: a.reshape(1, -1)]
    pallas_call x1, Pallas kernels: 67.2 us -> 65.1 us  [back(): pl.pallas_call(functools.partial(back_body, dp_size), grid_spec=pltpu.Pre...]
  transfers between devices with their start and end apart: 2 -> 0, of which waited for: 0 -> 0; matrix products, arithmetic and copies ran while one was open for 3% -> 0% of each run, Pallas kernels for 0% -> 0%
where the time goes in v5:
time: 133 us
  Pallas kernels  130 us (98%)
  between operations  1.48 us (1%)
  local copies, waits for them, and re-layouts  1.35 us (1%)
    pallas_call x1, Pallas kernels, back(): pl.pallas_call(functools.partial(back_body, dp_size), grid_spec=pltpu.Pre...  65.1 us
    pallas_call x1, Pallas kernels, middle(): pl.pallas_call(functools.partial(middle_body, dp_size), in_specs=[vm] * 1...  38 us
    pallas_call x1, Pallas kernels, front(): pl.pallas_call(front_body, grid_spec=pltpu.PrefetchScalarGridSpec(num_sca...  23 us
    pallas_call x1, Pallas kernels, emit(): pl.pallas_call(functools.partial(emit_body, len(arrays)), in_specs=[vm] *...  3.7 us

profile of v5, /device:TPU:0, one launch (start us, length us, event | category | flops | bytes accessed | tf_op | source)
XLA Modules:
  0.0 132.6 jit_solution(9432463263437845731)
XLA Ops:
  1.3 1.3 %copy.36.rand = s32[1,8,3]{2,1,0:T(8,128)} copy(s32[1,8,3]{1,0,2:T(1,128)} %param.22) | data formatting | bytes 192 | tf_op args[3]
  2.6 23.0 %front.1 = (bf16[512,768]{1,0:T(8,128)(2,1)}, bf16[512,384]{1,0:T(8,128)(2,1)}, bf16[512,384]{1,0:T(8,128)(2,1)}, bf16[512,384]{1,0:T(8,128)(2,1)}, bf16[1024,38...) custom-call(s32[1]{0:T(128)S(6)} %copy.37.lengths, ...), custom_call_target="tpu_custom_call" | custom-call | flops 20000000000 | bytes 20000000 | tf_op jit(solution)/shard_map/front/pallas_call | solution.py:196
  25.6 38.0 %middle.1 = (bf16[512,768]{1,0:T(8,128)(2,1)}, f32[512,768]{1,0:T(8,128)}, bf16[512,384]{1,0:T(8,128)(2,1)}, bf16[512,384]{1,0:T(8,128)(2,1)}, bf16[2,2,2,48,512...) custom-call(bf16[512,384]{1,0:T(8,128)(2,1)} %get-tuple-element.62.a, ...), custom_call_target="tpu_custom_call" | custom-call | flops 16999999488 | bytes 20000000 | tf_op jit(solution)/shard_map/middle/pallas_call | solution.py:564
  63.6 65.1 %back.1 = (f32[512,768]{1,0:T(8,128)}, f32[48,384]{1,0:T(8,128)}, f32[48,384]{1,0:T(8,128)}, f32[48,384]{1,0:T(8,128)}, f32[48,384]{1,0:T(8,128)}, /*index=5*/f3...) custom-call(bf16[512,768]{1,0:T(8,128)(2,1)} %bitcast.10, ...), custom_call_target="tpu_custom_call" | custom-call | flops 40000000000 | bytes 20000000 | tf_op jit(solution)/shard_map/back/pallas_call | solution.py:897
  128.7 3.7 %emit.1 = (bf16[512,768]{1,0:T(8,128)(2,1)}, f32[512,768]{1,0:T(8,128)}, f32[48,384]{1,0:T(8,128)}, f32[48,384]{1,0:T(8,128)}, f32[48,384]{1,0:T(8,128)}, /*inde...) custom-call(bf16[512,768]{1,0:T(8,128)(2,1)} %get-tuple-element.64.r, ...), custom_call_target="tpu_custom_call" | custom-call | tf_op jit(solution)/shard_map/emit/pallas_call | solution.py:960

commit v6 on v5

--- a/solution.py
+++ b/solution.py
@@ -58,8 +58,8 @@
 
 def front_body(
     lengths, x, rand, bq, bv, wq, wk, wv,
-    x_got, a_own, a_oth, a_got, q_o, k_o, v_o, p_o,
-    xg_s, ag_s, w_s, b_s, rand_s, rand_r, bias, wsem, send, recv,
+    x_got, a_own, a_oth, a_got, q_o, k_o, v_o, p_h,
+    xg_s, ag_s, p_s, w_s, b_s, rand_s, rand_r, bias, wsem, psem, send, recv,
 ):
     me = lax.axis_index("mp")
     p = pl.program_id(0)
@@ -71,7 +71,27 @@
     tile = 256
     x_copy = partner_copy(x, xg_s, send.at[0], recv.at[0], me)
     rand_copy = partner_copy(rand_s, rand_r, send.at[1], recv.at[1], me)
-    own_cols = pl.ds(pl.multiple_of(me * hw, hw), hw)
+
+    def w_loads(j):
+        own = pl.ds(pl.multiple_of(me * hw + j * pw, pw), pw)
+        return [
+            pltpu.make_async_copy(
+                w.at[:, own], w_s.at[j, :, i * pw : (i + 1) * pw], wsem.at[3 * j + i]
+            )
+            for i, w in enumerate((wq, wk, wv))
+        ]
+
+    slot = p % 2
+
+    def p_store(slot_j, j, i):
+        r0, h = units[i]
+        return pltpu.make_async_copy(
+            p_s.at[slot_j, h, r0 : r0 + tile], p_h.at[2 * j + h, r0 : r0 + tile],
+            psem.at[slot_j, i],
+        )
+
+    order = [half + t * tile for t in range(half // tile)] + [t * tile for t in range(half // tile)]
+    units = [(r0, h) for r0 in order for h in range(2)]
 
     @pl.when(p == 0)
     def _():
@@ -79,30 +99,37 @@
         pl.semaphore_signal(
             barrier, inc=1, device_id={"mp": 1 - me}, device_id_type=pl.DeviceIdType.MESH
         )
-        loads = [
-            pltpu.make_async_copy(w.at[:, own_cols], w_s.at[i], wsem.at[i])
-            for i, w in enumerate((wq, wk, wv))
-        ]
-        for c in loads:
-            c.start()
+        for j in range(hw // pw):
+            for c in w_loads(j):
+                c.start()
         rand_s[...] = jnp.zeros_like(rand_s)
-        rand_s[:, : rand.shape[2]] = rand[0]
+        for j in range(rand.shape[0]):
+            rand_s[j : j + 1, : nb // 2] = rand[j]
         b_s[0:1, :] = bq[...].astype(F32)[None, :]
         b_s[1:2, :] = bv[...].astype(F32)[None, :]
         pl.semaphore_wait(barrier, 1)
         x_copy.start()
         rand_copy.start()
-        for c in loads:
-            c.wait()
 
     cols = pl.ds(pl.multiple_of(p * pw, pw), pw)
     bias_cols = pl.ds(pl.multiple_of(me * hw + p * pw, pw), pw)
 
+    for j in range(hw // pw):
+
+        @pl.when(p == j)
+        def _(j=j):
+            for c in w_loads(j):
+                c.wait()
+            if j == 2:
+                for i in range(len(units)):
+                    p_store(0, 0, i).wait()
+
     def project(i, xr):
         rs = slice(i * half, (i + 1) * half)
-        q_o[rs, :] = (mm(xr[...], w_s[0, :, cols]) + b_s[0:1, bias_cols]).astype(BF16)
-        k_o[rs, :] = mm(xr[...], w_s[1, :, cols]).astype(BF16)
-        v_o[rs, :] = (mm(xr[...], w_s[2, :, cols]) + b_s[1:2, bias_cols]).astype(BF16)
+        qkv = mm(xr[...], w_s[p])
+        q_o[rs, :] = (qkv[:, :pw] + b_s[0:1, bias_cols]).astype(BF16)
+        k_o[rs, :] = qkv[:, pw : 2 * pw].astype(BF16)
+        v_o[rs, :] = (qkv[:, 2 * pw :] + b_s[1:2, bias_cols]).astype(BF16)
 
     project(0, x)
 
@@ -117,8 +144,9 @@
         kpos = jnp.where(kp < half, kp + half * me, kp - half * me)
         kb = kpos // BLK
         ok = (jnp.abs(kb - qb) <= 1) | (kb == 0) | (kb == last)
-        both = jnp.concatenate([rand_s[...], rand_r[...]], axis=0)
-        for j in range(rand.shape[2]):
+        listed = [r[...].astype(F32).T[: nb // 2] for r in (rand_s, rand_r)]
+        both = jnp.concatenate(listed, axis=0).astype(jnp.int32)
+        for j in range(rand.shape[0]):
             ok = ok | (kb == both[:, j : j + 1])
         ok = ok | (qb == 0) | (qb == last)
         ok = ok & (kpos < ln)
@@ -131,8 +159,6 @@
     project(1, xg_s)
 
     low = lax.broadcasted_iota(jnp.int32, (tile, pw), 1) < HD
-    order = [half + t * tile for t in range(half // tile)] + [t * tile for t in range(half // tile)]
-    units = [(r0, h) for r0 in order for h in range(2)]
     scores, probs, outs = {}, {}, {}
 
     def score(i):
@@ -164,7 +190,8 @@
         s = scores.pop(i)
         e = jnp.exp(s - jnp.max(s, axis=-1, keepdims=True))
         pr = (e * (1.0 / jnp.sum(e, axis=-1, keepdims=True))).astype(BF16)
-        p_o[h, r0 : r0 + tile, :] = pr
+        p_s[slot, h, r0 : r0 + tile, :] = pr
+        p_store(slot, p, i).start()
         probs[i] = pr
         if i >= 1:
             attend(i - 1)
@@ -180,6 +207,9 @@
             c.wait_send()
             c.wait_recv()
         a_got[...] = ag_s[...]
+        for j in range(1, hw // pw):
+            for i in range(len(units)):
+                p_store(j % 2, j, i).wait()
 
 
 def front(lengths, x, rand, bq, bv, wq, wk, wv):
@@ -199,16 +229,18 @@
             num_scalar_prefetch=0,
             grid=(pairs,),
             in_specs=[pl.BlockSpec(memory_space=pltpu.SMEM)] + [vm] * 4 + [hbm] * 3,
-            out_specs=[vm] * 4 + [col] * 3 + [pl.BlockSpec((2, rows, rows), lambda p: (p, 0, 0))],
+            out_specs=[vm] * 4 + [col] * 3 + [hbm],
             scratch_shapes=[
                 V((half, width), BF16),
                 V((half, hw), BF16),
-                V((3, width, hw), BF16),
+                V((2, 2, rows, rows), BF16),
+                V((pairs, width, 3 * pw), BF16),
                 V((8, width), F32),
-                V((rand.shape[1], 128), jnp.int32),
-                V((rand.shape[1], 128), jnp.int32),
+                V((8, 128), jnp.int32),
+                V((8, 128), jnp.int32),
                 V((rows // BLK, 8, rows), F32),
-                sem((3,)),
+                sem((3 * pairs,)),
+                sem((2, 8)),
                 sem((2 + pairs,)),
                 sem((2 + pairs,)),
             ],
@@ -319,10 +351,11 @@
 def middle_body(
     dp_size, a_own, a_got, x, gout, b_output, gain1, shift1, b_in, b_out, gain2, shift2,
     w_o_h, w_in_h, w_out_h,
-    out_o, gsum_o, ga_o, gat_o, sa1, sa2, sa3, win_g, wo_g, vec_o, bi_o,
+    out_h, gsum_h, ga_o, gat_o, sa1, sa2, sa3, win_h, wo_g, vec_o, bi_o,
+    out_o, gsum_o, win_g,
     fl, feed_s, feed_g, gf, part_s, part_g, gat_s, gb, wo_s, wo_r, vec_s, vec_r, bi_s, bi_s2, bi_r, wout_g, got_a1, got_a2, got_a3,
     w_o, w_in, w_out, act, slope, gh, u_s, first_s, own_s, gtwo_s,
-    load_sem, send_sem, recv_sem, a_send_sem, a_recv_sem,
+    load_sem, store_sem, send_sem, recv_sem, a_send_sem, a_recv_sem,
 ):
     me = lax.axis_index("mp")
     half, width = x.shape
@@ -345,6 +378,10 @@
     barrier = pltpu.get_barrier_semaphore()
     for device in [{"mp": 1 - me}] + [{"dp": a.peer(0)} for a in outs_a]:
         pl.semaphore_signal(barrier, inc=1, device_id=device, device_id_type=pl.DeviceIdType.MESH)
+    stores = [
+        pltpu.make_async_copy(src, dst, store_sem.at[i])
+        for i, (src, dst) in enumerate(((out_o, out_h), (win_g, win_h), (gsum_o, gsum_h)))
+    ]
     loads = []
     for i, (src, dst) in enumerate(((w_o_h, w_o), (w_in_h, w_in), (w_out_h, w_out))):
         loads.append(pltpu.make_async_copy(src, dst, load_sem.at[i]))
@@ -440,6 +477,7 @@
         return carry
 
     lax.fori_loop(0, tiles, second_norm, 0)
+    stores[0].start()
     bi_s[...] = jnp.zeros_like(bi_s)
 
     def feed_back(i, t):
@@ -487,6 +525,7 @@
         lax.fori_loop(0, width // tile, step, 0)
 
     weights(win_g, fl, gh)
+    stores[1].start()
 
     def first_norm(t, carry):
         r = rows(t)
@@ -506,6 +545,7 @@
         return carry
 
     lax.fori_loop(0, tiles, first_norm, 0)
+    stores[2].start()
     vec_copy = copy(vec_s, vec_r, 11)
     vec_copy.start()
     bi_s2[0:1, :] = bi_s[0:1, :width]
@@ -544,6 +584,8 @@
         return carry
 
     lax.fori_loop(0, tiles, finish, 0)
+    for c in stores:
+        c.wait()
     for a in outs_a:
         a.copy(0).wait_send()
     vec_copy.wait_send()
@@ -564,7 +606,7 @@
     return pl.pallas_call(
         functools.partial(middle_body, dp_size),
         in_specs=[vm] * 11 + [hbm] * 3,
-        out_specs=[vm] * 11,
+        out_specs=[hbm] * 2 + [vm] * 5 + [hbm] + [vm] * 3,
         out_shape=[
             shape((half, width), BF16),
             shape((half, width), F32),
@@ -579,6 +621,9 @@
             shape((8, width), F32),
         ],
         scratch_shapes=[
+            V((half, width), BF16),
+            V((half, width), F32),
+            V((width, ff), BF16),
             V((2, half, width), BF16),
             V((half, width), BF16),
             V((half, width), BF16),
@@ -609,6 +654,7 @@
             V((half, width), F32),
             V((half, width), F32),
             pltpu.SemaphoreType.DMA((3,)),
+            pltpu.SemaphoreType.DMA((3,)),
             pltpu.SemaphoreType.DMA((14,)),
             pltpu.SemaphoreType.DMA((14,)),
             pltpu.SemaphoreType.DMA((3 * nb,)),
@@ -635,13 +681,13 @@
 
 
 def back_body(
-    dp_size, xo, xt, q_i, k_i, v_i, p_i, ao, at, go, gt, gsum, vec, bi,
-    wq, wk, wv, sa1, sa2, sa3, win, wo,
+    dp_size, q_i, k_i, v_i, ao, at, go, gt, vec, bi,
+    xo_h, xt_h, p_h, gsum_h, wq, wk, wv, sa1, sa2, sa3, win, wo,
     ig_o, wq_o, wk_o, wv_o, wo_o, win_o, wout_o, vals_o, bi_o,
-    g_s, gT, qT, dkT, dvT, dqkv, wcat, xT, acc, ig_s, ig_r, wsrc, gots, kepts,
+    xo, xt, p_s, gsum, g_s, gT, qT, dkT, dvT, dqkv, wcat, xT, acc, ig_s, ig_r, wsrc, gots, kepts,
     tb, tb_m, ts, trs, send, recv, lsem, vsend, vrecv, wsem,
 ):
-    half, width = xo.shape
+    half, width = ig_o.shape
     rows = 2 * half
     pw = 2 * HD
     tile = 256
@@ -664,6 +710,14 @@
         s0 = 1 if name[0] == "A" else 0
         P[name] = Piece(bits, sems, i * nb, src, gots[i], kepts[i], s0)
     from_hbm = PIECES[:7]
+    x_loads = [
+        pltpu.make_async_copy(s, d, wsem.at[5 + i])
+        for i, (s, d) in enumerate(((xo_h, xo), (xt_h, xt), (gsum_h, gsum)))
+    ]
+
+    def p_load(j):
+        return pltpu.make_async_copy(p_h.at[2 * j : 2 * j + 2], p_s.at[j % 2], wsem.at[3 + j % 2])
+
     ig_copy = partner_copy(ig_s, ig_r, vsend.at[0], vrecv.at[0], me)
     tb_copy = partner_copy(tb, tb_m, vsend.at[1], vrecv.at[1], me)
     t_copies = [
@@ -687,10 +741,26 @@
         pl.semaphore_wait(barrier, len(everyone))
         for name in from_hbm:
             P[name].copy(P[name].stage0).start()
+        for c in x_loads[:2]:
+            c.start()
+        p_load(0).start()
+        p_load(1).start()
+        x_loads[2].start()
+        for c in x_loads[:2]:
+            c.wait()
         xT[:, :half] = xo[...].T
         xT[:, half:] = xt[...].T
         tb[...] = jnp.zeros_like(tb)
 
+    for j in range(HEADS // 4):
+
+        @pl.when(p == j)
+        def _(j=j):
+            if j == 1:
+                p_load(2).start()
+            p_load(j).wait()
+
+    slot = p % 2
     c_off = pl.multiple_of(me * (width // 2) + p * pw, pw)
     w_copies = [
         pltpu.make_async_copy(
@@ -754,7 +824,7 @@
             hs = slice(h * HD, (h + 1) * HD)
             dp = mm(jnp.where(mine, g, BF16(0)), v_i[...], NT)
             delta = jnp.sum(jnp.where(mine, ga, 0.0), axis=-1, keepdims=True)
-            pr = p_i[h, rs, :]
+            pr = p_s[slot, h, rs, :]
             ds = (pr.astype(F32) * (dp - delta)).astype(BF16)
             outs.append(mm(ds, k_i[...]))
             dvT[hs, :] += mm(gT[hs, rs], pr)
@@ -823,6 +893,7 @@
         forward(1, "C0")
         forward(0, "C2", "C3")
         ig_copy.wait_recv()
+        x_loads[2].wait()
         ig_o[...] = gsum[...] + (acc[:half, :] + ig_r[...].astype(F32))
         next_table(1)
         forward(2, "B3")
@@ -899,14 +970,13 @@
         grid_spec=pltpu.PrefetchScalarGridSpec(
             num_scalar_prefetch=0,
             grid=(pairs,),
-            in_specs=[whole(xo), whole(xt)]
-            + [col(rows, pw)] * 3
-            + [pl.BlockSpec((2, rows, rows), lambda p: (p, 0, 0))]
-            + [col(half, pw)] * 4
-            + [whole(gsum), whole(vec), whole(bi)]
-            + [hbm] * 8,
+            in_specs=[col(rows, pw)] * 3 + [col(half, pw)] * 4 + [whole(vec), whole(bi)] + [hbm] * 12,
             out_specs=[vm] * 9,
             scratch_shapes=[
+                V((half, width), BF16),
+                V((half, width), BF16),
+                V((2, 2, rows, rows), BF16),
+                V((half, width), F32),
                 V((rows, pw), BF16),
                 V((pw, rows), BF16),
                 V((pw, rows), BF16),
@@ -930,7 +1000,7 @@
                 sem((len(plan),)),
                 sem((2 + nb,)),
                 sem((2 + nb,)),
-                sem((3,)),
+                sem((8,)),
             ],
         ),
         out_shape=[shape((half, width), F32)]
@@ -942,7 +1012,7 @@
         ),
         cost_estimate=cost(40e9, 20e6),
         name="back",
-    )(xo, xt, q, k, v, probs, ao, at, go, gt, gsum, vec, bi, wq, wk, wv, *sa, split(win), split(wo))
+    )(q, k, v, ao, at, go, gt, vec, bi, xo, xt, probs, gsum, wq, wk, wv, *sa, split(win), split(wo))
 
 
 def emit_body(big, *refs):
@@ -975,7 +1045,7 @@
 ):
     x = inputs[0]
     x_got, a_own, a_oth, a_got, q, k, v, probs = front(
-        lengths, x, rand_blocks, b_query, b_value, w_query, w_key, w_value
+        lengths, x, rand_blocks.transpose(2, 0, 1), b_query, b_value, w_query, w_key, w_value
     )
     out, gsum, ga0, ga_got, sa1, sa2, sa3, w_in_g, w_output_g, vec_g, bi_g = middle(
         dp_size, a_own, a_got, x, grad_out[0], b_output, gain_one, shift_one, b_in, b_out,

time: 133 us -> 125 us (0.940)
  Pallas kernels: 130 us -> 123 us
  local copies, waits for them, and re-layouts: 1.35 us -> 0 us
    pallas_call x1, Pallas kernels: 65.1 us -> 61.8 us  [back(): pl.pallas_call(functools.partial(back_body, dp_size), grid_spec=pltpu.Pre...]
    pallas_call x1, Pallas kernels: 23 us -> 21.3 us  [front(): pl.pallas_call(front_body, grid_spec=pltpu.PrefetchScalarGridSpec(num_sca...]
    pallas_call x1, Pallas kernels: 38 us -> 36.6 us  [middle(): pl.pallas_call(functools.partial(middle_body, dp_size), in_specs=[vm] * 1...]
    unnamed x1 -> x0, local copies, waits for them, and re-layouts: 1.35 us -> none
where the time goes in v6:
time: 125 us
  Pallas kernels  123 us (98%)
  between operations  1.48 us (1%)
    pallas_call x1, Pallas kernels, back(): pl.pallas_call(functools.partial(back_body, dp_size), grid_spec=pltpu.Pre...  61.8 us
    pallas_call x1, Pallas kernels, middle(): pl.pallas_call(functools.partial(middle_body, dp_size), in_specs=[vm] * 1...  36.6 us
    pallas_call x1, Pallas kernels, front(): pl.pallas_call(front_body, grid_spec=pltpu.PrefetchScalarGridSpec(num_sca...  21.3 us
    pallas_call x1, Pallas kernels, emit(): pl.pallas_call(functools.partial(emit_body, len(arrays)), in_specs=[vm] *...  3.7 us

profile of v6, /device:TPU:0, one launch (start us, length us, event | category | flops | bytes accessed | tf_op | source)
XLA Modules:
  0.0 124.8 jit_solution(1096319218281742712)
XLA Ops:
  1.3 21.3 %front.1 = (bf16[512,768]{1,0:T(8,128)(2,1)}, bf16[512,384]{1,0:T(8,128)(2,1)}, bf16[512,384]{1,0:T(8,128)(2,1)}, bf16[512,384]{1,0:T(8,128)(2,1)}, bf16[1024,38...) custom-call(s32[1]{0:T(128)S(6)} %copy.36.lengths, ...), custom_call_target="tpu_custom_call" | custom-call | flops 20000000000 | bytes 20000000 | tf_op jit(solution)/shard_map/front/pallas_call | solution.py:226
  22.6 36.6 %middle.1 = (bf16[512,768]{1,0:T(8,128)(2,1)}, f32[512,768]{1,0:T(8,128)}, bf16[512,384]{1,0:T(8,128)(2,1)}, bf16[512,384]{1,0:T(8,128)(2,1)}, bf16[2,2,2,48,512...) custom-call(bf16[512,384]{1,0:T(8,128)(2,1)} %get-tuple-element.62.a, ...), custom_call_target="tpu_custom_call" | custom-call | flops 16999999488 | bytes 20000000 | tf_op jit(solution)/shard_map/middle/pallas_call | solution.py:606
  59.2 61.8 %back.1 = (f32[512,768]{1,0:T(8,128)}, f32[48,384]{1,0:T(8,128)}, f32[48,384]{1,0:T(8,128)}, f32[48,384]{1,0:T(8,128)}, f32[48,384]{1,0:T(8,128)}, /*index=5*/f3...) custom-call(bf16[1024,384]{1,0:T(8,128)(2,1)} %get-tuple-element.65.q_i, ...), custom_call_target="tpu_custom_call" | custom-call | flops 40000000000 | bytes 20000000 | tf_op jit(solution)/shard_map/back/pallas_call | solution.py:968
  121.0 3.7 %emit.1 = (bf16[512,768]{1,0:T(8,128)(2,1)}, f32[512,768]{1,0:T(8,128)}, f32[48,384]{1,0:T(8,128)}, f32[48,384]{1,0:T(8,128)}, f32[48,384]{1,0:T(8,128)}, /*inde...) custom-call(bf16[512,768]{1,0:T(8,128)(2,1)} %get-tuple-element.64.r, ...), custom_call_target="tpu_custom_call" | custom-call | tf_op jit(solution)/shard_map/emit/pallas_call | solution.py:1030

commit v7 on v6

--- a/solution.py
+++ b/solution.py
@@ -796,15 +796,9 @@
 
             @pl.when(p == 1)
             def _():
+                forward(0, "B1", "B2", "B3")
                 forward(1, "A3")
-                forward(0, "B3")
                 forward(2, "A1", "A2")
-
-        if t == 1:
-
-            @pl.when(p == 1)
-            def _():
-                forward(0, "B1", "B2")
 
             @pl.when(p == 2)
             def _():

time: 125 us -> 124 us (level)
    pallas_call x1, Pallas kernels: 61.8 us -> 60.1 us  [back(): pl.pallas_call(functools.partial(back_body, dp_size), grid_spec=pltpu.Pre...]
where the time goes in v7:
time: 124 us; the launch traced here: 123 us
  Pallas kernels  122 us (98%)
  between operations  1.48 us (1%)
    pallas_call x1, Pallas kernels, back(): pl.pallas_call(functools.partial(back_body, dp_size), grid_spec=pltpu.Pre...  60.1 us
    pallas_call x1, Pallas kernels, middle(): pl.pallas_call(functools.partial(middle_body, dp_size), in_specs=[vm] * 1...  36.6 us
    pallas_call x1, Pallas kernels, front(): pl.pallas_call(front_body, grid_spec=pltpu.PrefetchScalarGridSpec(num_sca...  21.3 us
    pallas_call x1, Pallas kernels, emit(): pl.pallas_call(functools.partial(emit_body, len(arrays)), in_specs=[vm] *...  3.7 us

profile of v7, /device:TPU:0, one launch (start us, length us, event | category | flops | bytes accessed | tf_op | source)
XLA Modules:
  0.0 123.2 jit_solution(14730250846800180896)
XLA Ops:
  1.3 21.3 %front.1 = (bf16[512,768]{1,0:T(8,128)(2,1)}, bf16[512,384]{1,0:T(8,128)(2,1)}, bf16[512,384]{1,0:T(8,128)(2,1)}, bf16[512,384]{1,0:T(8,128)(2,1)}, bf16[1024,38...) custom-call(s32[1]{0:T(128)S(6)} %copy.36.lengths, ...), custom_call_target="tpu_custom_call" | custom-call | flops 20000000000 | bytes 20000000 | tf_op jit(solution)/shard_map/front/pallas_call | solution.py:226
  22.6 36.6 %middle.1 = (bf16[512,768]{1,0:T(8,128)(2,1)}, f32[512,768]{1,0:T(8,128)}, bf16[512,384]{1,0:T(8,128)(2,1)}, bf16[512,384]{1,0:T(8,128)(2,1)}, bf16[2,2,2,48,512...) custom-call(bf16[512,384]{1,0:T(8,128)(2,1)} %get-tuple-element.62.a, ...), custom_call_target="tpu_custom_call" | custom-call | flops 16999999488 | bytes 20000000 | tf_op jit(solution)/shard_map/middle/pallas_call | solution.py:606
  59.2 60.1 %back.1 = (f32[512,768]{1,0:T(8,128)}, f32[48,384]{1,0:T(8,128)}, f32[48,384]{1,0:T(8,128)}, f32[48,384]{1,0:T(8,128)}, f32[48,384]{1,0:T(8,128)}, /*index=5*/f3...) custom-call(bf16[1024,384]{1,0:T(8,128)(2,1)} %get-tuple-element.65.q_i, ...), custom_call_target="tpu_custom_call" | custom-call | flops 40000000000 | bytes 20000000 | tf_op jit(solution)/shard_map/back/pallas_call | solution.py:962
  119.3 3.7 %emit.1 = (bf16[512,768]{1,0:T(8,128)(2,1)}, f32[512,768]{1,0:T(8,128)}, f32[48,384]{1,0:T(8,128)}, f32[48,384]{1,0:T(8,128)}, f32[48,384]{1,0:T(8,128)}, /*inde...) custom-call(bf16[512,768]{1,0:T(8,128)(2,1)} %get-tuple-element.64.r, ...), custom_call_target="tpu_custom_call" | custom-call | tf_op jit(solution)/shard_map/emit/pallas_call | solution.py:1024

commit v8 on v7

--- a/solution.py
+++ b/solution.py
@@ -58,8 +58,8 @@
 
 def front_body(
     lengths, x, rand, bq, bv, wq, wk, wv,
-    x_got, a_own, a_oth, a_got, q_o, k_o, v_o, p_h,
-    xg_s, ag_s, p_s, w_s, b_s, rand_s, rand_r, bias, wsem, psem, send, recv,
+    x_got, a_own, a_oth, q_o, k_o, v_o, p_h,
+    later_loads, middle_part, xg_s, ag_s, p_s, w_s, b_s, rand_s, rand_r, bias, wsem, psem, send, recv,
 ):
     me = lax.axis_index("mp")
     p = pl.program_id(0)
@@ -96,18 +96,24 @@
     @pl.when(p == 0)
     def _():
         barrier = pltpu.get_barrier_semaphore()
-        pl.semaphore_signal(
-            barrier, inc=1, device_id={"mp": 1 - me}, device_id_type=pl.DeviceIdType.MESH
-        )
+        dev = lax.axis_index("dp")
+        everyone = [{"mp": 1 - me}]
+        everyone += [{"dp": dev + 2**b * (1 - 2 * ((dev // 2**b) % 2))} for b in range(3)]
+        for device in everyone:
+            pl.semaphore_signal(
+                barrier, inc=1, device_id=device, device_id_type=pl.DeviceIdType.MESH
+            )
         for j in range(hw // pw):
             for c in w_loads(j):
                 c.start()
+        for c in later_loads:
+            c.start()
         rand_s[...] = jnp.zeros_like(rand_s)
         for j in range(rand.shape[0]):
             rand_s[j : j + 1, : nb // 2] = rand[j]
         b_s[0:1, :] = bq[...].astype(F32)[None, :]
         b_s[1:2, :] = bv[...].astype(F32)[None, :]
-        pl.semaphore_wait(barrier, 1)
+        pl.semaphore_wait(barrier, len(everyone))
         x_copy.start()
         rand_copy.start()
 
@@ -206,55 +212,10 @@
             c = partner_copy(a_oth.at[:, cs], ag_s.at[:, cs], send.at[2 + j], recv.at[2 + j], me)
             c.wait_send()
             c.wait_recv()
-        a_got[...] = ag_s[...]
+        middle_part(ag_s)
         for j in range(1, hw // pw):
             for i in range(len(units)):
                 p_store(j % 2, j, i).wait()
-
-
-def front(lengths, x, rand, bq, bv, wq, wk, wv):
-    half, width = x.shape
-    rows = 2 * half
-    pairs = HEADS // 4
-    pw = 2 * HD
-    hw = width // 2
-    vm = pl.BlockSpec(memory_space=pltpu.VMEM)
-    hbm = pl.BlockSpec(memory_space=pl.ANY)
-    col = pl.BlockSpec((rows, pw), lambda p: (0, p))
-    V = pltpu.VMEM
-    sem = pltpu.SemaphoreType.DMA
-    return pl.pallas_call(
-        front_body,
-        grid_spec=pltpu.PrefetchScalarGridSpec(
-            num_scalar_prefetch=0,
-            grid=(pairs,),
-            in_specs=[pl.BlockSpec(memory_space=pltpu.SMEM)] + [vm] * 4 + [hbm] * 3,
-            out_specs=[vm] * 4 + [col] * 3 + [hbm],
-            scratch_shapes=[
-                V((half, width), BF16),
-                V((half, hw), BF16),
-                V((2, 2, rows, rows), BF16),
-                V((pairs, width, 3 * pw), BF16),
-                V((8, width), F32),
-                V((8, 128), jnp.int32),
-                V((8, 128), jnp.int32),
-                V((rows // BLK, 8, rows), F32),
-                sem((3 * pairs,)),
-                sem((2, 8)),
-                sem((2 + pairs,)),
-                sem((2 + pairs,)),
-            ],
-        ),
-        out_shape=[shape((half, width), BF16)]
-        + [shape((half, hw), BF16)] * 3
-        + [shape((rows, hw), BF16)] * 3
-        + [shape((2 * pairs, rows, rows), BF16)],
-        compiler_params=pltpu.CompilerParams(
-            vmem_limit_bytes=60 << 20, collective_id=3, has_side_effects=True
-        ),
-        cost_estimate=cost(20e9, 20e6, 6 * rows * rows),
-        name="front",
-    )(lengths, x, rand, bq, bv, wq, wk, wv)
 
 
 class Piece:
@@ -349,13 +310,12 @@
 
 
 def middle_body(
-    dp_size, a_own, a_got, x, gout, b_output, gain1, shift1, b_in, b_out, gain2, shift2,
-    w_o_h, w_in_h, w_out_h,
+    dp_size, loads, a_own, a_got, x, gout, b_output, gain1, shift1, b_in, b_out, gain2, shift2,
     out_h, gsum_h, ga_o, gat_o, sa1, sa2, sa3, win_h, wo_g, vec_o, bi_o,
-    out_o, gsum_o, win_g,
-    fl, feed_s, feed_g, gf, part_s, part_g, gat_s, gb, wo_s, wo_r, vec_s, vec_r, bi_s, bi_s2, bi_r, wout_g, got_a1, got_a2, got_a3,
-    w_o, w_in, w_out, act, slope, gh, u_s, first_s, own_s, gtwo_s,
-    load_sem, store_sem, send_sem, recv_sem, a_send_sem, a_recv_sem,
+    out_o, gsum_o, win_g, gat_r,
+    fl, feed_s, feed_g, gf, part_s, part_g, gat_s, wo_s, wo_r, vec_s, vec_r, bi_s, bi_s2, bi_r, wout_g, got_a1, got_a2, got_a3,
+    w_o, w_in, w_out, act, gh, u_s, first_s, own_s, gtwo_s,
+    store_sem, send_sem, recv_sem, a_send_sem, a_recv_sem,
 ):
     me = lax.axis_index("mp")
     half, width = x.shape
@@ -375,23 +335,15 @@
             zip(bit_orders(dp_size), (got_a1, got_a2, got_a3), (sa1, sa2, sa3))
         )
     ]
-    barrier = pltpu.get_barrier_semaphore()
-    for device in [{"mp": 1 - me}] + [{"dp": a.peer(0)} for a in outs_a]:
-        pl.semaphore_signal(barrier, inc=1, device_id=device, device_id_type=pl.DeviceIdType.MESH)
     stores = [
         pltpu.make_async_copy(src, dst, store_sem.at[i])
         for i, (src, dst) in enumerate(((out_o, out_h), (win_g, win_h), (gsum_o, gsum_h)))
     ]
-    loads = []
-    for i, (src, dst) in enumerate(((w_o_h, w_o), (w_in_h, w_in), (w_out_h, w_out))):
-        loads.append(pltpu.make_async_copy(src, dst, load_sem.at[i]))
-        loads[-1].start()
-    pl.semaphore_wait(barrier, 4)
-
     def copy(src, dst, i):
         return partner_copy(src, dst, send_sem.at[i], recv_sem.at[i], me)
 
-    loads[0].wait()
+    for c in loads:
+        c.wait()
 
     def rows(t):
         return pl.ds(pl.multiple_of(t * tile, tile), tile)
@@ -409,7 +361,7 @@
         return copy(part_s.at[rows(t)], part_g.at[rows(t)], 7 + t)
 
     def ga_copy(t):
-        return copy(gat_s.at[rows(t)], gat_o.at[rows(t)], 9 + t)
+        return copy(gat_s.at[rows(t)], gat_r.at[rows(t)], 9 + t)
 
     own_o = pl.ds(pl.multiple_of(me * hw, hw), hw)
     got_o = pl.ds(pl.multiple_of((1 - me) * hw, hw), hw)
@@ -428,8 +380,6 @@
         return carry
 
     lax.fori_loop(0, tiles, project, 0)
-    loads[1].wait()
-    loads[2].wait()
 
     def feed_forward(i, t):
         r = rows(t)
@@ -437,7 +387,7 @@
         a, s = gelu_and_slope(v)
         a = a.astype(BF16)
         act[i, r, :] = a
-        slope[i, r, :] = s.astype(BF16)
+        gh[i, r, :] = s.astype(BF16)
         return mm(a, w_out[...], NT)
 
     def forward_own(t, carry):
@@ -482,7 +432,7 @@
 
     def feed_back(i, t):
         r = rows(t)
-        g = (mm(gf[i, r, :], w_out[...]) * slope[i, r, :].astype(F32)).astype(BF16)
+        g = (mm(gf[i, r, :], w_out[...]) * gh[i, r, :].astype(F32)).astype(BF16)
         gh[i, r, :] = g
         bi_s[0:1, :] += jnp.sum(g.astype(F32), 0, keepdims=True)
         return mm(g, w_in[...], NT)
@@ -535,7 +485,7 @@
         d = norm_back(e, n, rs, gain1[...].astype(F32)[None, :])
         low = d.astype(BF16)
         gsum_o[r, :] = d
-        gb[r, :] = low
+        gout[r, :] = low
         gat_s[r, :] = mm(low, w_o[got_o, :], NT).astype(BF16)
         ga_copy(t).start()
         ga_o[r, :] = mm(low, w_o[own_o, :], NT).astype(BF16)
@@ -554,12 +504,12 @@
     bi_copy.start()
     cols_own = own_o
     cols_got = got_o
-    wo_s[own_o, :] = mm(a_own[...], gb[:, cols_got], TN).astype(BF16)
-    wo_s[got_o, :] = mm(a_got[...], gb[:, cols_got], TN).astype(BF16)
+    wo_s[own_o, :] = mm(a_own[...], gout[:, cols_got], TN).astype(BF16)
+    wo_s[got_o, :] = mm(a_got[...], gout[:, cols_got], TN).astype(BF16)
     wo_copy = copy(wo_s, wo_r, 13)
     wo_copy.start()
-    own_part = mm(a_own[...], gb[:, cols_own], TN)
-    got_part = mm(a_got[...], gb[:, cols_own], TN)
+    own_part = mm(a_own[...], gout[:, cols_own], TN)
+    got_part = mm(a_got[...], gout[:, cols_own], TN)
     wo_copy.wait_recv()
     wo_g[own_o, :] = (own_part + wo_r[own_o, :].astype(F32)).astype(BF16)
     wo_g[got_o, :] = (got_part + wo_r[got_o, :].astype(F32)).astype(BF16)
@@ -584,6 +534,7 @@
         return carry
 
     lax.fori_loop(0, tiles, finish, 0)
+    gat_o[...] = gat_r[...]
     for c in stores:
         c.wait()
     for a in outs_a:
@@ -593,8 +544,31 @@
     wo_copy.wait_send()
 
 
-def middle(dp_size, a_own, a_got, x, gout, b_output, gain1, shift1, b_in, b_out, gain2, shift2, w_o, w_in, w_out):
+def first_half_body(dp_size, *refs):
+    ins, refs = refs[:19], refs[19:]
+    outs, refs = refs[:18], refs[18:]
+    mine, (gout, load_sem), rest = refs[:12], refs[12:14], refs[14:]
+    lengths, x, rand, bq, bv, wq, wk, wv, gout_h = ins[:9]
+    vectors, weights_h = ins[9:16], ins[16:]
+    weights = [rest[i] for i in (22, 23, 24)]
+    loads = [
+        pltpu.make_async_copy(a, b, load_sem.at[i])
+        for i, (a, b) in enumerate(zip((gout_h,) + tuple(weights_h), [gout] + weights))
+    ]
+
+    def middle_part(a_got):
+        middle_body(
+            dp_size, loads, outs[1], a_got, x, gout, *vectors, *outs[7:], *rest
+        )
+
+    front_body(lengths, x, rand, bq, bv, wq, wk, wv, *outs[:7], loads, middle_part, *mine)
+
+
+def first_half(dp_size, lengths, x, rand, bq, bv, wq, wk, wv, gout, vectors, w_o, w_in, w_out):
     half, width = x.shape
+    rows = 2 * half
+    pairs = HEADS // 4
+    pw = 2 * HD
     hw = width // 2
     ff = w_in.shape[1]
     nb = dp_size.bit_length() - 1
@@ -602,12 +576,74 @@
     part = (2,) * (nb - 1) + (n, ff // 3)
     vm = pl.BlockSpec(memory_space=pltpu.VMEM)
     hbm = pl.BlockSpec(memory_space=pl.ANY)
+    col = pl.BlockSpec((rows, pw), lambda p: (0, p))
     V = pltpu.VMEM
+    sem = pltpu.SemaphoreType.DMA
     return pl.pallas_call(
-        functools.partial(middle_body, dp_size),
-        in_specs=[vm] * 11 + [hbm] * 3,
-        out_specs=[hbm] * 2 + [vm] * 5 + [hbm] + [vm] * 3,
-        out_shape=[
+        functools.partial(first_half_body, dp_size),
+        grid_spec=pltpu.PrefetchScalarGridSpec(
+            num_scalar_prefetch=0,
+            grid=(pairs,),
+            in_specs=[pl.BlockSpec(memory_space=pltpu.SMEM)] + [vm] * 4 + [hbm] * 4 + [vm] * 7 + [hbm] * 3,
+            out_specs=[vm] * 3 + [col] * 3 + [hbm] + [hbm] * 2 + [vm] * 5 + [hbm] + [vm] * 3,
+            scratch_shapes=[
+                V((half, width), BF16),
+                V((half, hw), BF16),
+                V((2, 2, rows, rows), BF16),
+                V((pairs, width, 3 * pw), BF16),
+                V((8, width), F32),
+                V((8, 128), jnp.int32),
+                V((8, 128), jnp.int32),
+                V((rows // BLK, 8, rows), F32),
+                sem((3 * pairs,)),
+                sem((2, 8)),
+                sem((2 + pairs,)),
+                sem((2 + pairs,)),
+                V((half, width), BF16),
+                sem((4,)),
+                V((half, width), BF16),
+                V((half, width), F32),
+                V((width, ff), BF16),
+                V((half, hw), BF16),
+                V((2, half, width), BF16),
+                V((half, width), BF16),
+                V((half, width), BF16),
+                V((2, half, width), BF16),
+                V((half, width), BF16),
+                V((half, width), BF16),
+                V((half, hw), BF16),
+                V((width, hw), BF16),
+                V((width, hw), BF16),
+                V((8, width), F32),
+                V((8, width), F32),
+                V((8, ff), F32),
+                V((8, width), F32),
+                V((8, width), F32),
+                V((2,) * nb + (n, ff), BF16),
+                V(part, BF16),
+                V(part, BF16),
+                V(part, BF16),
+                V((width, width), BF16),
+                V((width, ff), BF16),
+                V((width, ff), BF16),
+                V((2, half, ff), BF16),
+                V((2, half, ff), BF16),
+                V((half, width), F32),
+                V((half, width), F32),
+                V((half, width), F32),
+                V((half, width), F32),
+                pltpu.SemaphoreType.DMA((3,)),
+                pltpu.SemaphoreType.DMA((14,)),
+                pltpu.SemaphoreType.DMA((14,)),
+                pltpu.SemaphoreType.DMA((3 * nb,)),
+                pltpu.SemaphoreType.DMA((3 * nb,)),
+            ],
+        ),
+        out_shape=[shape((half, width), BF16)]
+        + [shape((half, hw), BF16)] * 2
+        + [shape((rows, hw), BF16)] * 3
+        + [shape((2 * pairs, rows, rows), BF16)]
+        + [
             shape((half, width), BF16),
             shape((half, width), F32),
             shape((half, hw), BF16),
@@ -620,52 +656,12 @@
             shape((8, width), F32),
             shape((8, width), F32),
         ],
-        scratch_shapes=[
-            V((half, width), BF16),
-            V((half, width), F32),
-            V((width, ff), BF16),
-            V((2, half, width), BF16),
-            V((half, width), BF16),
-            V((half, width), BF16),
-            V((2, half, width), BF16),
-            V((half, width), BF16),
-            V((half, width), BF16),
-            V((half, hw), BF16),
-            V((half, width), BF16),
-            V((width, hw), BF16),
-            V((width, hw), BF16),
-            V((8, width), F32),
-            V((8, width), F32),
-            V((8, ff), F32),
-            V((8, width), F32),
-            V((8, width), F32),
-            V((2,) * nb + (n, ff), BF16),
-            V(part, BF16),
-            V(part, BF16),
-            V(part, BF16),
-            V((width, width), BF16),
-            V((width, ff), BF16),
-            V((width, ff), BF16),
-            V((2, half, ff), BF16),
-            V((2, half, ff), BF16),
-            V((2, half, ff), BF16),
-            V((half, width), F32),
-            V((half, width), F32),
-            V((half, width), F32),
-            V((half, width), F32),
-            pltpu.SemaphoreType.DMA((3,)),
-            pltpu.SemaphoreType.DMA((3,)),
-            pltpu.SemaphoreType.DMA((14,)),
-            pltpu.SemaphoreType.DMA((14,)),
-            pltpu.SemaphoreType.DMA((3 * nb,)),
-            pltpu.SemaphoreType.DMA((3 * nb,)),
-        ],
         compiler_params=pltpu.CompilerParams(
-            vmem_limit_bytes=62 << 20, collective_id=1, has_side_effects=True
+            vmem_limit_bytes=63 << 20, collective_id=1, has_side_effects=True
         ),
-        cost_estimate=cost(17e9, 20e6),
-        name="middle",
-    )(a_own, a_got, x, gout, b_output, gain1, shift1, b_in, b_out, gain2, shift2, w_o, w_in, w_out)
+        cost_estimate=cost(37e9, 40e6, 6 * rows * rows),
+        name="first_half",
+    )(lengths, x, rand, bq, bv, wq, wk, wv, gout, *vectors, w_o, w_in, w_out)
 
 
 PIECES = ("A1", "A2", "A3", "B1", "B2", "B3", "WO", "C0", "C1", "C2", "C3")
@@ -788,6 +784,13 @@
             x.forward(k, loaded)
 
     def at_tile(t):
+        if t == 1:
+
+            @pl.when(p == 2)
+            def _():
+                forward(0, "WO")
+                forward(2, "A3")
+
         if t == 3:
 
             @pl.when(p == 0)
@@ -803,8 +806,7 @@
             @pl.when(p == 2)
             def _():
                 forward(1, "B1", "B2")
-                forward(2, "A3")
-                forward(0, "WO")
+                forward(0, "C0")
 
     for t in range(rows // tile):
         rs = slice(t * tile, (t + 1) * tile)
@@ -874,7 +876,6 @@
             if k + 1 < nb:
                 t_copies[k + 1].start()
 
-        forward(0, "C0")
         tb_copy.wait_recv()
         ts[0][0:8, :] = tb[...] + tb_m[...] + vec[...]
         ts[0][8:16, :] = bi[...]
@@ -1038,12 +1039,13 @@
     w_output, b_output, gain_one, shift_one, w_in, b_in, w_out, b_out, gain_two, shift_two,
 ):
     x = inputs[0]
-    x_got, a_own, a_oth, a_got, q, k, v, probs = front(
-        lengths, x, rand_blocks.transpose(2, 0, 1), b_query, b_value, w_query, w_key, w_value
-    )
-    out, gsum, ga0, ga_got, sa1, sa2, sa3, w_in_g, w_output_g, vec_g, bi_g = middle(
-        dp_size, a_own, a_got, x, grad_out[0], b_output, gain_one, shift_one, b_in, b_out,
-        gain_two, shift_two, w_output, w_in, w_out,
+    (
+        x_got, a_own, a_oth, q, k, v, probs, out, gsum, ga0, ga_got, sa1, sa2, sa3, w_in_g,
+        w_output_g, vec_g, bi_g,
+    ) = first_half(
+        dp_size, lengths, x, rand_blocks.transpose(2, 0, 1), b_query, b_value, w_query, w_key,
+        w_value, grad_out[0],
+        (b_output, gain_one, shift_one, b_in, b_out, gain_two, shift_two), w_output, w_in, w_out,
     )
     *mats, vals, bi = back(
         dp_size, x, x_got, w_query, w_key, w_value, q, k, v, probs, a_own, a_oth, ga0, ga_got,

time: 124 us -> 121 us (0.976)
  Pallas kernels: 122 us -> 120 us
    pallas_call x2 -> x1, Pallas kernels: 57.9 us -> 54.3 us  [first_half(): pl.pallas_call(functools.partial(first_half_body, dp_size), grid_spec=plt...]
    pallas_call x1, Pallas kernels: 60.1 us -> 61.7 us  [back(): pl.pallas_call(functools.partial(back_body, dp_size), grid_spec=pltpu.Pre...]
where the time goes in v8:
time: 121 us
  Pallas kernels  120 us (99%)
  between operations  1.48 us (1%)
    pallas_call x1, Pallas kernels, back(): pl.pallas_call(functools.partial(back_body, dp_size), grid_spec=pltpu.Pre...  61.7 us
    pallas_call x1, Pallas kernels, first_half(): pl.pallas_call(functools.partial(first_half_body, dp_size), grid_spec=plt...  54.3 us
    pallas_call x1, Pallas kernels, emit(): pl.pallas_call(functools.partial(emit_body, len(arrays)), in_specs=[vm] *...  3.7 us

profile of v8, /device:TPU:0, one launch (start us, length us, event | category | flops | bytes accessed | tf_op | source)
XLA Modules:
  0.0 121.2 jit_solution(4820467388933421885)
XLA Ops:
  1.3 54.3 %first_half.1 = (bf16[512,768]{1,0:T(8,128)(2,1)}, bf16[512,384]{1,0:T(8,128)(2,1)}, bf16[512,384]{1,0:T(8,128)(2,1)}, bf16[1024,384]{1,0:T(8,128)(2,1)}, bf16[1...) custom-call(s32[1]{0:T(128)S(6)} %copy.36.refs_0_, ...), custom_call_target="tpu_custom_call" | custom-call | flops 36999999488 | bytes 40000000 | tf_op jit(solution)/shard_map/first_half/pallas_call | solution.py:582
  55.7 61.7 %back.1 = (f32[512,768]{1,0:T(8,128)}, f32[48,384]{1,0:T(8,128)}, f32[48,384]{1,0:T(8,128)}, f32[48,384]{1,0:T(8,128)}, f32[48,384]{1,0:T(8,128)}, /*index=5*/f3...) custom-call(bf16[1024,384]{1,0:T(8,128)(2,1)} %get-tuple-element.62.q_i, ...), custom_call_target="tpu_custom_call" | custom-call | flops 40000000000 | bytes 20000000 | tf_op jit(solution)/shard_map/back/pallas_call | solution.py:963
  117.3 3.7 %emit.1 = (bf16[512,768]{1,0:T(8,128)(2,1)}, f32[512,768]{1,0:T(8,128)}, f32[48,384]{1,0:T(8,128)}, f32[48,384]{1,0:T(8,128)}, f32[48,384]{1,0:T(8,128)}, /*inde...) custom-call(bf16[512,768]{1,0:T(8,128)(2,1)} %get-tuple-element.61.r, ...), custom_call_target="tpu_custom_call" | custom-call | tf_op jit(solution)/shard_map/emit/pallas_call | solution.py:1025

commit v9 on v8

--- a/solution.py
+++ b/solution.py
@@ -900,8 +900,9 @@
         forward(2, "C1")
         for i in range(3):
             wout_o[:, i * third : (i + 1) * third] = P["A%d" % (i + 1)].result()
+        forward(2, "C2", "C3")
+        for i in range(3):
             win_o[:, i * third : (i + 1) * third] = P["B%d" % (i + 1)].result()
-        forward(2, "C2", "C3")
         wo_o[...] = P["WO"].result()
         next_table(nb - 1)
         table = ts[nb][...]

time: 121 us -> 121 us (level)
  no operation moved by 1% of the time
where the time goes in v9:
time: 121 us
  Pallas kernels  120 us (99%)
  between operations  1.48 us (1%)
    pallas_call x1, Pallas kernels, back(): pl.pallas_call(functools.partial(back_body, dp_size), grid_spec=pltpu.Pre...  61.7 us
    pallas_call x1, Pallas kernels, first_half(): pl.pallas_call(functools.partial(first_half_body, dp_size), grid_spec=plt...  54.3 us
    pallas_call x1, Pallas kernels, emit(): pl.pallas_call(functools.partial(emit_body, len(arrays)), in_specs=[vm] *...  3.7 us

profile of v9, /device:TPU:0, one launch (start us, length us, event | category | flops | bytes accessed | tf_op | source)
XLA Modules:
  0.0 121.2 jit_solution(11773170649058692707)
XLA Ops:
  1.3 54.3 %first_half.1 = (bf16[512,768]{1,0:T(8,128)(2,1)}, bf16[512,384]{1,0:T(8,128)(2,1)}, bf16[512,384]{1,0:T(8,128)(2,1)}, bf16[1024,384]{1,0:T(8,128)(2,1)}, bf16[1...) custom-call(s32[1]{0:T(128)S(6)} %copy.36.refs_0_, ...), custom_call_target="tpu_custom_call" | custom-call | flops 36999999488 | bytes 40000000 | tf_op jit(solution)/shard_map/first_half/pallas_call | solution.py:582
  55.7 61.7 %back.1 = (f32[512,768]{1,0:T(8,128)}, f32[48,384]{1,0:T(8,128)}, f32[48,384]{1,0:T(8,128)}, f32[48,384]{1,0:T(8,128)}, f32[48,384]{1,0:T(8,128)}, /*index=5*/f3...) custom-call(bf16[1024,384]{1,0:T(8,128)(2,1)} %get-tuple-element.62.q_i, ...), custom_call_target="tpu_custom_call" | custom-call | flops 40000000000 | bytes 20000000 | tf_op jit(solution)/shard_map/back/pallas_call | solution.py:964
  117.3 3.7 %emit.1 = (bf16[512,768]{1,0:T(8,128)(2,1)}, f32[512,768]{1,0:T(8,128)}, f32[48,384]{1,0:T(8,128)}, f32[48,384]{1,0:T(8,128)}, f32[48,384]{1,0:T(8,128)}, /*inde...) custom-call(bf16[512,768]{1,0:T(8,128)(2,1)} %get-tuple-element.61.r, ...), custom_call_target="tpu_custom_call" | custom-call | tf_op jit(solution)/shard_map/emit/pallas_call | solution.py:1026
